TPU v7x, 32 devices: a whole 2x2x4 slice. The times are simulated.
32 devices in a mesh: lon: 4 (over x, core), lat: 4 (over z), batch: 2 (over y).
Axes of the slice: x: 2, y: 2, z: 4, core: 2. Of those that a mesh axis runs over, the one named last changes fastest.
Arguments:
- features: bfloat16 [2, 96, 96, 128], P('batch', 'lon', 'lat'), may hold values from -160 to 160
- weight_one: bfloat16 [3, 3, 128, 128], replicated, may hold values from -0.1875 to 0.1875
- norm_gain: float32 [128], replicated, may hold values from 0.1 to 1.9
- norm_bias: float32 [128], replicated, may hold values from -0.6 to 0.6
- weight_two: bfloat16 [3, 3, 128, 128], replicated, may hold values from -0.1875 to 0.1875
- out_cotangent: bfloat16 [2, 96, 96, 128], P('batch', 'lon', 'lat'), may hold values from -0.109375 to 0.109375
Outputs:
- output_maps: bfloat16 [2, 96, 96, 128], P('batch', 'lon', 'lat')
- grad_one: float32 [3, 3, 128, 128], replicated
- grad_two: float32 [3, 3, 128, 128], replicated
- grad_gain: float32 [128], replicated
- grad_bias: float32 [128], replicated
All inputs are finite; a program needn't handle non-finite values.
Results may differ from a plain program's by a relative error of at most 0.005.
Values may be sent and summed in bfloat16 or wider, within the bound.
No kernel may reach another device: no remote copies, remote signals or barrier semaphores. Data moves between devices by JAX's collectives and lax.ppermute only.
A program may use at most 64 MiB of HBM per device.

v0:
```python
import jax
import jax.numpy as jnp
from jax import lax
from jax.sharding import PartitionSpec as P

RATE_ONE = 6
RATE_TWO = 12


def extended(value, sides, width, wrap):
    for axis, dim in sides:
        devices, length = (lax.axis_size(axis), value.shape[dim])
        up = [(i, (i + 1) % devices) for i in range(devices if wrap else devices - 1)]
        down = [(j, i) for i, j in up]
        last = lax.slice_in_dim(value, length - width, length, axis=dim)
        initial = lax.slice_in_dim(value, 0, width, axis=dim)
        before = lax.ppermute(last, axis, up)
        after = lax.ppermute(initial, axis, down)
        value = jnp.concatenate([before, value, after], axis=dim)
    return value


def extend(field, width):
    wide = extended(field, (("lon", 1),), width, True)
    return extended(wide, (("lat", 2),), width, False)


def conv_valid(padded, kernel, rate):
    return lax.conv_general_dilated(
        padded,
        kernel,
        (1, 1),
        "VALID",
        rhs_dilation=(rate, rate),
        dimension_numbers=("NHWC", "HWIO", "NHWC"),
        preferred_element_type=jnp.float32,
    )


def kernel_grad(padded, grad, rate):
    rows, cols = (grad.shape[1], grad.shape[2])
    result = []
    for first in range(3):
        line = []
        for second in range(3):
            window = padded[
                :, first * rate : first * rate + rows, second * rate : second * rate + cols
            ]
            line.append(
                jnp.einsum("spqc,spqo->co", window, grad, preferred_element_type=jnp.float32)
            )
        result.append(jnp.stack(line))
    return jnp.stack(result)


def local(features, weight_one, norm_gain, norm_bias, weight_two, out_cotangent):
    count = (
        features.shape[0]
        * features.shape[1]
        * features.shape[2]
        * lax.axis_size("lon")
        * lax.axis_size("lat")
    )
    feats_wide = extend(features, RATE_ONE)
    pre_one = conv_valid(feats_wide, weight_one, RATE_ONE)
    total = lax.psum(jnp.sum(pre_one, axis=(0, 1, 2)), ("lon", "lat"))
    mean = total / count
    spread = lax.psum(jnp.sum((pre_one - mean) ** 2, axis=(0, 1, 2)), ("lon", "lat"))
    var = spread / count
    rstd = lax.rsqrt(var + 1e-05)
    normed = (pre_one - mean) * rstd
    shifted = norm_gain * normed + norm_bias
    sig = jax.nn.sigmoid(shifted)
    hidden = (shifted * sig).astype(jnp.bfloat16)
    hidden_wide = extend(hidden, RATE_TWO)
    cotan_wide = extend(out_cotangent, RATE_TWO)
    output_maps = conv_valid(hidden_wide, weight_two, RATE_TWO).astype(jnp.bfloat16)
    flipped = jnp.flip(weight_two, (0, 1)).transpose(0, 1, 3, 2)
    grad_hidden = conv_valid(cotan_wide, flipped, RATE_TWO)
    grad_shift = grad_hidden * sig * (1.0 + shifted * (1.0 - sig))
    local_b = jnp.sum(grad_shift, axis=(0, 1, 2))
    local_ba = jnp.sum(grad_shift * normed, axis=(0, 1, 2))
    sum_b, sum_ba = lax.psum((local_b, local_ba), ("lon", "lat"))
    grad_pre = (
        (norm_gain * grad_shift - norm_gain * sum_b / count - normed * norm_gain * sum_ba / count)
        * rstd
    ).astype(jnp.bfloat16)
    part_two = kernel_grad(hidden_wide, out_cotangent, RATE_TWO)
    part_one = kernel_grad(feats_wide, grad_pre, RATE_ONE)
    grad_one, grad_two, grad_gain, grad_bias = lax.psum(
        (part_one, part_two, local_ba, local_b), ("lon", "lat", "batch")
    )
    return (output_maps, grad_one, grad_two, grad_gain, grad_bias)


def solution(mesh):
    placed = (P("batch", "lon", "lat", None), P(), P(), P(), P(), P("batch", "lon", "lat", None))
    return jax.shard_map(
        local,
        mesh=mesh,
        in_specs=placed,
        out_specs=(P("batch", "lon", "lat", None), P(), P(), P(), P()),
        check_vma=False,
    )
```

profile of v0, /device:TPU:0, one launch (start us, length us, event | category | flops | bytes accessed | tf_op | source)
XLA Modules:
  0.0 293.1 jit_solution(8037319284931728598)
XLA Ops:
  7.2 0.8 fusion.103
  8.1 0.5 collective-permute-start
  8.7 2.0 collective-permute-start.1
  10.7 0.9 fusion.101
  11.7 0.1 copy.84
  11.8 0.7 collective-permute-start.8
  12.5 0.1 copy.85
  12.6 1.1 collective-permute-start.9
  13.8 0.1 constant_dynamic-update-slice_fusion.2
  13.8 0.2 constant_dynamic-update-slice_fusion.1
  14.1 0.1 constant_dynamic-update-slice_fusion
  14.2 0.2 fusion.99
  14.4 4.3 %collective-permute-start.2 = (bf16[1,36,6,128]{3,0,2,1:T(2,128)(2,1)S(1)}, bf16[1,36,6,128]{3,0,2,1:T(2,128)(2,1)S(1)}, u32[]{:S(2)}, u32[]{:S(2)}) collective-permute-start(bf16[1,36,6,128]{3,0,2,1:T(2,128)(2,1)S(1)} %get-tuple-element.40), channel_id=1, source_target_pairs={{0,2},{2,4},{4,6},{1,3},{3,5},{5,7},{8,10},{10,12},{12,14},{9,11},... | collective-permute-start | bytes 165896 | tf_op jit(solution)/shard_map/ppermute | solution.py:17
  18.7 1.3 collective-permute-start.3
  20.0 0.6 copy.40
  20.6 0.6 copy.42
  21.3 0.2 constant_dynamic-update-slice_fusion.5
  21.4 0.2 constant_dynamic-update-slice_fusion.4
  21.7 0.2 constant_dynamic-update-slice_fusion.3
  21.9 1.4 fusion.98
  23.3 5.3 %collective-permute-start.10 = (bf16[1,48,12,128]{3,0,2,1:T(2,128)(2,1)}, bf16[1,48,12,128]{3,0,2,1:T(2,128)(2,1)}, u32[]{:S(2)}, u32[]{:S(2)}) collective-permute-start(bf16[1,48,12,128]{3,0,2,1:T(2,128)(2,1)} %get-tuple-element.29), channel_id=1, source_target_pairs={{0,2},{2,4},{4,6},{1,3},{3,5},{5,7},{8,10},{10,12},{12,14},{9,11},... | collective-permute-start | bytes 442376 | tf_op jit(solution)/shard_map/ppermute | solution.py:17
  28.5 1.3 collective-permute-start.11
  29.9 2.2 fusion.104
  32.0 33.0 %psum.56 = f32[128]{0:T(128)S(1)} all-reduce(f32[128]{0:T(128)S(1)} %get-tuple-element.51), channel_id=1, replica_groups=mesh['lon'=4,'lat'=4,'batch'=2] {'lon','lat'}, use_global_device_ids=true, to_apply=%region_1.0 | all-reduce | flops 128 | bytes 1024 | tf_op jit(solution)/shard_map/psum | solution.py:66
  65.1 0.1 multiply_reduce_fusion.1
  65.1 29.7 %psum.57 = f32[128]{0:T(128)S(1)} all-reduce(f32[128]{0:T(128)S(1)} %multiply_reduce_fusion.1), channel_id=1, replica_groups=mesh['lon'=4,'lat'=4,'batch'=2] {'lon','lat'}, use_global_device_ids=true, to_apply=%region_3.0 | all-reduce | flops 128 | bytes 1024 | tf_op jit(solution)/shard_map/psum | solution.py:68
  94.8 3.9 %fusion.10 = (bf16[1,24,24,128]{3,0,2,1:T(2,128)(2,1)}, bf16[1,24,24,128]{3,0,2,1:T(2,128)(2,1)S(1)}, bf16[1,24,24,128]{3,0,2,1:T(2,128)(2,1)S(1)}, bf16[1,24,24...) fusion(bf16[1,36,24,128]{3,0,2,1:T(2,128)(2,1)S(1)} %constant_dynamic-update-, ...), kind=kLoop, calls=%fused_computation.39 | loop fusion | flops 442368 | bytes 1216512 | tf_op jit(solution)/shard_map/concatenate | solution.py:19
  98.8 3.4 %fusion.2 = f32[1,24,24,128]{3,0,2,1:T(1,128)S(1)} fusion(bf16[3,3,128,128]{3,2,1,0:T(8,128)(2,1)S(1)} %copy-done, bf16[1,48,12,128]{3,0,2,1:T(2,128)(2,1)} %collective-permute-done.11, bf16[1,48,24,128]{3,0,2,1:T(2,128)(2,1)S(1)} %constant_dynamic-update-slice_fusion.3, bf16[1,48,12,128]{3,0,2,1:T(2,128)(2,1)} %collective-permute-done.10), kind=kOutput, calls=%fused_computation.3 | convolution fusion | flops 171638784 | bytes 1179648 | tf_op jit(solution)/shard_map/conv_general_dilated | solution.py:29
  102.2 0.2 fusion.97
  102.4 0.2 convolution_bitcast_fusion.4
  102.6 31.9 %all-reduce.2 = (f32[128]{0:T(128)S(1)}, f32[128]{0:T(128)S(1)}) all-reduce(f32[128]{0:T(128)S(1)} %get-tuple-element.21, f32[128]{0:T(128)S(1)} %get-tuple-element.20), channel_id=1, replica_groups=mesh['lon'=4,'lat'=4,'batch'=2] {'lon','lat'}, use_global_device_ids=true, to_apply=%region_7.8 | all-reduce | flops 256 | bytes 2048 | tf_op jit(solution)/shard_map/psum | solution.py:83
  134.6 0.1 multiply_convert_fusion
  134.7 0.3 convolution_bitcast_fusion.13
  135.0 0.2 convolution_bitcast_fusion.16
  135.2 0.2 copy-done.7
  135.5 0.2 convolution_bitcast_fusion.10
  135.8 1.7 collective-permute-start.5
  137.5 0.2 convolution_bitcast_fusion.17
  137.7 0.2 convolution_bitcast_fusion.11
  138.0 0.2 convolution_bitcast_fusion.14
  138.2 0.2 convolution_bitcast_fusion.12
  138.5 0.2 convolution_bitcast_fusion.9
  138.7 0.2 convolution_bitcast_fusion.15
  139.0 0.9 pad_maximum_fusion.5
  140.0 1.9 collective-permute-start.6
  142.0 1.5 collective-permute-start.7
  143.4 0.2 convolution_bitcast_fusion.7
  143.7 0.2 convolution_bitcast_fusion.1
  143.9 3.0 %collective-permute-done.6 = bf16[1,48,12,128]{3,2,1,0:T(8,128)(2,1)S(1)} collective-permute-done((bf16[1,48,12,128]{3,2,1,0:T(8,128)(2,1)S(1)}, bf16[1,48,12,128]{3,2,1,0:T(8,128)(2,1)S(1)}, u32[]{:S(2)}, u32[]{:S(2)}) %collective-permute-start.6) | collective-permute-done | bytes 147488 | tf_op jit(solution)/shard_map/ppermute | solution.py:17
  147.0 0.2 convolution_bitcast_fusion.2
  147.2 4.4 %collective-permute-done.7 = bf16[1,48,12,128]{3,2,1,0:T(8,128)(2,1)S(1)} collective-permute-done((bf16[1,48,12,128]{3,2,1,0:T(8,128)(2,1)S(1)}, bf16[1,48,12,128]{3,2,1,0:T(8,128)(2,1)S(1)}, u32[]{:S(2)}, u32[]{:S(2)}) %collective-permute-start.7) | collective-permute-done | bytes 147488 | tf_op jit(solution)/shard_map/ppermute | solution.py:18
  151.6 0.2 convolution_bitcast_fusion
  151.9 0.2 convolution_bitcast_fusion.5
  152.1 0.2 convolution_bitcast_fusion.8
  152.4 0.2 convolution_bitcast_fusion.3
  152.6 0.2 convolution_bitcast_fusion.6
  152.9 0.9 pad_maximum_fusion.6
  153.8 38.1 %all-reduce = (f32[128]{0:T(128)}, f32[128]{0:T(128)}) all-reduce(f32[128]{0:T(128)S(1)} %get-tuple-element.21, f32[128]{0:T(128)S(1)} %get-tuple-element.20), channel_id=1, replica_groups=mesh['lon'=4,'lat'=4,'batch'=2] {'lon','lat','batch'}, use_global_device_ids=true, to_apply=%region_10.11 | all-reduce | flops 256 | bytes 2048 | tf_op jit(solution)/shard_map/psum | solution.py:90
  191.9 0.2 pad_maximum_fusion.4
  192.1 2.0 fusion.3
  194.1 0.7 copy.43
  194.8 88.6 %all-reduce.5.cloned.1.call-done = (f32[3,3,128,128]{3,2,1,0:T(8,128)}, f32[3,3,128,128]{3,2,1,0:T(8,128)}) async-done(((f32[3,3,128,128]{3,2,1,0:T(8,128)}, f32[3,3,128,128]{3,2,1,0:T(8,128)}), (f32[3,3,128,128]{3,2,1,0:T(8,128)}, f32[3,3,128,128]{3,2,1,0:T(8,128)})) %all-reduce.5.cloned.1.call-update) | async-done | bytes 1179664 | tf_op jit(solution)/shard_map/psum | solution.py:90
  283.4 2.0 copy.92
  285.4 0.8 copy.93
  (46 shorter events, 0.5 us)
Async XLA Ops:
  7.2 91.6 %copy-start = (bf16[3,3,128,128]{3,2,1,0:T(8,128)(2,1)S(1)}, bf16[3,3,128,128]{3,2,1,0:T(8,128)(2,1)}, u32[]{:S(2)}) copy-start(bf16[3,3,128,128]{3,2,1,0:T(8,128)(2,1)} %param.10) | copy-start | bytes 884740
  7.2 276.2 %all-reduce.5.cloned.1.call-start = ((), (), s32[]{:S(2)}) async-start(), calls=%async_computation | async-start | bytes 2359296 | tf_op jit(solution)/shard_map/psum | solution.py:90
  8.1 5.8 %copy-start.1 = (bf16[1,24,24,128]{3,2,1,0:T(8,128)(2,1)S(1)}, bf16[1,24,24,128]{3,2,1,0:T(8,128)(2,1)}, u32[]{:S(2)}) copy-start(bf16[1,24,24,128]{3,2,1,0:T(8,128)(2,1)} %param.6) | copy-start | bytes 442372
  8.1 5.6 %collective-permute-start = (bf16[1,6,24,128]{3,0,2,1:T(2,128)(2,1)S(1)}, bf16[1,6,24,128]{3,0,2,1:T(2,128)(2,1)S(1)}, u32[]{:S(2)}, u32[]{:S(2)}) collective-permute-start(bf16[1,6,24,128]{3,0,2,1:T(2,128)(2,1)S(1)} %copy.82), channel_id=1, source_target_pairs={{0,8},{8,16},{16,24},{24,0},{1,9},{9,17},{17,25},{25,1},{2,10},{10... | collective-permute-start | bytes 110600 | tf_op jit(solution)/shard_map/ppermute | solution.py:17
  8.7 5.4 %collective-permute-start.1 = (bf16[1,6,24,128]{3,0,2,1:T(2,128)(2,1)S(1)}, bf16[1,6,24,128]{3,0,2,1:T(2,128)(2,1)S(1)}, u32[]{:S(2)}, u32[]{:S(2)}) collective-permute-start(bf16[1,6,24,128]{3,0,2,1:T(2,128)(2,1)S(1)} %copy.83), channel_id=1, source_target_pairs={{8,0},{16,8},{24,16},{0,24},{9,1},{17,9},{25,17},{1,25},{10,2},{18... | collective-permute-start | bytes 110600 | tf_op jit(solution)/shard_map/ppermute | solution.py:18
  11.8 9.5 %collective-permute-start.8 = (bf16[1,12,24,128]{3,0,2,1:T(2,128)(2,1)S(1)}, bf16[1,12,24,128]{3,0,2,1:T(2,128)(2,1)S(1)}, u32[]{:S(2)}, u32[]{:S(2)}) collective-permute-start(bf16[1,12,24,128]{3,0,2,1:T(2,128)(2,1)S(1)} %copy.84), channel_id=1, source_target_pairs={{0,8},{8,16},{16,24},{24,0},{1,9},{9,17},{17,25},{25,1},{2,10},{10... | collective-permute-start | bytes 221192 | tf_op jit(solution)/shard_map/ppermute | solution.py:17
  12.6 9.1 %collective-permute-start.9 = (bf16[1,12,24,128]{3,0,2,1:T(2,128)(2,1)S(1)}, bf16[1,12,24,128]{3,0,2,1:T(2,128)(2,1)S(1)}, u32[]{:S(2)}, u32[]{:S(2)}) collective-permute-start(bf16[1,12,24,128]{3,0,2,1:T(2,128)(2,1)S(1)} %copy.85), channel_id=1, source_target_pairs={{8,0},{16,8},{24,16},{0,24},{9,1},{17,9},{25,17},{1,25},{10,2},{18... | collective-permute-start | bytes 221192 | tf_op jit(solution)/shard_map/ppermute | solution.py:18
  14.1 7.3 %copy-start.2 = (bf16[1,24,24,128]{3,2,1,0:T(8,128)(2,1)S(1)}, bf16[1,24,24,128]{3,2,1,0:T(8,128)(2,1)}, u32[]{:S(2)}) copy-start(bf16[1,24,24,128]{3,2,1,0:T(8,128)(2,1)} %param.11) | copy-start | bytes 442372
  14.4 15.4 %collective-permute-start.2 = (bf16[1,36,6,128]{3,0,2,1:T(2,128)(2,1)S(1)}, bf16[1,36,6,128]{3,0,2,1:T(2,128)(2,1)S(1)}, u32[]{:S(2)}, u32[]{:S(2)}) collective-permute-start(bf16[1,36,6,128]{3,0,2,1:T(2,128)(2,1)S(1)} %get-tuple-element.40), channel_id=1, source_target_pairs={{0,2},{2,4},{4,6},{1,3},{3,5},{5,7},{8,10},{10,12},{12,14},{9,11},... | collective-permute-start | bytes 165896 | tf_op jit(solution)/shard_map/ppermute | solution.py:17
  18.7 11.1 %collective-permute-start.3 = (bf16[1,36,6,128]{3,0,2,1:T(2,128)(2,1)S(1)}, bf16[1,36,6,128]{3,0,2,1:T(2,128)(2,1)S(1)}, u32[]{:S(2)}, u32[]{:S(2)}) collective-permute-start(bf16[1,36,6,128]{3,0,2,1:T(2,128)(2,1)S(1)} %get-tuple-element.41), channel_id=1, source_target_pairs={{2,0},{4,2},{6,4},{3,1},{5,3},{7,5},{10,8},{12,10},{14,12},{11,9},... | collective-permute-start | bytes 165896 | tf_op jit(solution)/shard_map/ppermute | solution.py:18
  21.9 8.0 %copy-start.10 = (bf16[3,3,128,128]{3,2,1,0:T(8,128)(2,1)S(1)}, bf16[3,3,128,128]{3,2,1,0:T(8,128)(2,1)}, u32[]{:S(2)}) copy-start(bf16[3,3,128,128]{3,2,1,0:T(8,128)(2,1)} %param.7) | copy-start | bytes 884740
  23.3 75.4 %collective-permute-start.10 = (bf16[1,48,12,128]{3,0,2,1:T(2,128)(2,1)}, bf16[1,48,12,128]{3,0,2,1:T(2,128)(2,1)}, u32[]{:S(2)}, u32[]{:S(2)}) collective-permute-start(bf16[1,48,12,128]{3,0,2,1:T(2,128)(2,1)} %get-tuple-element.29), channel_id=1, source_target_pairs={{0,2},{2,4},{4,6},{1,3},{3,5},{5,7},{8,10},{10,12},{12,14},{9,11},... | collective-permute-start | bytes 442376 | tf_op jit(solution)/shard_map/ppermute | solution.py:17
  28.5 70.2 %collective-permute-start.11 = (bf16[1,48,12,128]{3,0,2,1:T(2,128)(2,1)}, bf16[1,48,12,128]{3,0,2,1:T(2,128)(2,1)}, u32[]{:S(2)}, u32[]{:S(2)}) collective-permute-start(bf16[1,48,12,128]{3,0,2,1:T(2,128)(2,1)} %get-tuple-element.30), channel_id=1, source_target_pairs={{2,0},{4,2},{6,4},{3,1},{5,3},{7,5},{10,8},{12,10},{14,12},{11,9},... | collective-permute-start | bytes 442376 | tf_op jit(solution)/shard_map/ppermute | solution.py:18
  29.9 2.2 copy-start.5
  98.7 3.4 %copy-start.8 = (f32[128]{0:T(128)S(1)}, f32[128]{0:T(128)}, u32[]{:S(2)}) copy-start(f32[128]{0:T(128)} %param.8) | copy-start | bytes 1540
  98.7 3.4 %copy-start.9 = (f32[128]{0:T(128)S(1)}, f32[128]{0:T(128)}, u32[]{:S(2)}) copy-start(f32[128]{0:T(128)} %param.9) | copy-start | bytes 1540
  102.6 32.3 %copy-start.6 = (bf16[1,6,24,128]{3,2,1,0:T(8,128)(2,1)S(1)}, bf16[1,6,24,128]{3,2,1,0:T(8,128)(2,1)}, u32[]{:S(2)}) copy-start(bf16[1,6,24,128]{3,2,1,0:T(8,128)(2,1)} %copy.40) | copy-start | bytes 110596
  134.7 0.8 copy-start.7
  135.0 2.5 copy-start.4
  135.7 4.2 %collective-permute-start.4 = (bf16[1,12,24,128]{3,2,1,0:T(8,128)(2,1)S(1)}, bf16[1,12,24,128]{3,2,1,0:T(8,128)(2,1)S(1)}, u32[]{:S(2)}, u32[]{:S(2)}) collective-permute-start(bf16[1,12,24,128]{3,2,1,0:T(8,128)(2,1)S(1)} %get-tuple-element.47), channel_id=1, source_target_pairs={{0,8},{8,16},{16,24},{24,0},{1,9},{9,17},{17,25},{25,1},{2,10},{10... | collective-permute-start | bytes 221192 | tf_op jit(solution)/shard_map/ppermute | solution.py:17
  135.8 4.1 %collective-permute-start.5 = (bf16[1,12,24,128]{3,2,1,0:T(8,128)(2,1)S(1)}, bf16[1,12,24,128]{3,2,1,0:T(8,128)(2,1)S(1)}, u32[]{:S(2)}, u32[]{:S(2)}) collective-permute-start(bf16[1,12,24,128]{3,2,1,0:T(8,128)(2,1)S(1)} %get-tuple-element.48), channel_id=1, source_target_pairs={{8,0},{16,8},{24,16},{0,24},{9,1},{17,9},{25,17},{1,25},{10,2},{18... | collective-permute-start | bytes 221192 | tf_op jit(solution)/shard_map/ppermute | solution.py:18
  140.0 6.9 %collective-permute-start.6 = (bf16[1,48,12,128]{3,2,1,0:T(8,128)(2,1)S(1)}, bf16[1,48,12,128]{3,2,1,0:T(8,128)(2,1)S(1)}, u32[]{:S(2)}, u32[]{:S(2)}) collective-permute-start(bf16[1,48,12,128]{3,2,1,0:T(8,128)(2,1)S(1)} %get-tuple-element.43), channel_id=1, source_target_pairs={{0,2},{2,4},{4,6},{1,3},{3,5},{5,7},{8,10},{10,12},{12,14},{9,11},... | collective-permute-start | bytes 442376 | tf_op jit(solution)/shard_map/ppermute | solution.py:17
  142.0 9.7 %collective-permute-start.7 = (bf16[1,48,12,128]{3,2,1,0:T(8,128)(2,1)S(1)}, bf16[1,48,12,128]{3,2,1,0:T(8,128)(2,1)S(1)}, u32[]{:S(2)}, u32[]{:S(2)}) collective-permute-start(bf16[1,48,12,128]{3,2,1,0:T(8,128)(2,1)S(1)} %get-tuple-element.44), channel_id=1, source_target_pairs={{2,0},{4,2},{6,4},{3,1},{5,3},{7,5},{10,8},{12,10},{14,12},{11,9},... | collective-permute-start | bytes 442376 | tf_op jit(solution)/shard_map/ppermute | solution.py:18
  283.4 2.0 copy-start.3
Sparse Core Ops, SparseCore 0:
  153.9 129.4 all-reduce.4
where the time goes:
time: 294 us; the launch traced here: 293 us
  blocking collectives  133 us (45%)
  waiting for transfers between devices  96.1 us (33%)
  starting transfers between devices  21.7 us (7%)
  between operations  14.5 us (5%)
  matrix products  11.8 us (4%)
  local copies, waits for them, and re-layouts  9.81 us (3%)
  other arithmetic  6.36 us (2%)
    psum x1, waiting for transfers between devices, local(): lax.psum((part_one, part_two, local_ba, local_b), ('lon', 'lat', 'batch'))  88.6 us
    psum x1, blocking collectives, local(): lax.psum((part_one, part_two, local_ba, local_b), ('lon', 'lat', 'batch'))  38.1 us
    psum x1, blocking collectives, local(): total = lax.psum(jnp.sum(pre_one, axis=(0, 1, 2)), ('lon', 'lat'))  33 us
    psum x1, blocking collectives, local(): sum_b, sum_ba = lax.psum((local_b, local_ba), ('lon', 'lat'))  31.9 us
    psum x1, blocking collectives, local(): lax.psum(jnp.sum((pre_one - mean) ** 2, axis=(0, 1, 2)), ('lon', 'lat'))  29.7 us
    ppermute x6, starting transfers between devices, extended(): before = lax.ppermute(last, axis, up)  12.8 us
    ppermute x6, starting transfers between devices, extended(): after = lax.ppermute(initial, axis, down)  8.88 us
    conv_general_dilated x3, matrix products, conv_valid(): lax.conv_general_dilated(padded, kernel, (1, 1), 'VALID', rhs_dilation=(r...  7.5 us
  transfers between devices with their start and end apart: 13, of which 3 were waited for; matrix products, arithmetic and copies ran while one was open for 6% of the time, Pallas kernels for 0%

commit v1 on v0

v1 whole, which is shorter than its diff:
```python
import jax
import jax.numpy as jnp
from jax import lax
from jax.sharding import PartitionSpec as P

RATE_ONE = 6
RATE_TWO = 12
TILE = ("lon", "lat")
EVERY = ("lon", "lat", "batch")


def extended(value, sides, width, wrap):
    for axis, dim in sides:
        devices, length = (lax.axis_size(axis), value.shape[dim])
        up = [(i, (i + 1) % devices) for i in range(devices if wrap else devices - 1)]
        down = [(j, i) for i, j in up]
        last = lax.slice_in_dim(value, length - width, length, axis=dim)
        initial = lax.slice_in_dim(value, 0, width, axis=dim)
        before = lax.ppermute(last, axis, up)
        after = lax.ppermute(initial, axis, down)
        value = jnp.concatenate([before, value, after], axis=dim)
    return value


def extend(field, width):
    wide = extended(field, (("lon", 1),), width, True)
    return extended(wide, (("lat", 2),), width, False)


def conv_valid(padded, kernel, rate):
    return lax.conv_general_dilated(
        padded,
        kernel,
        (1, 1),
        "VALID",
        rhs_dilation=(rate, rate),
        dimension_numbers=("NHWC", "HWIO", "NHWC"),
        preferred_element_type=jnp.float32,
    )


def windows(padded, rate, rows, cols):
    return [
        padded[:, a * rate : a * rate + rows, b * rate : b * rate + cols].reshape(-1, padded.shape[3])
        for a in range(3)
        for b in range(3)
    ]


def outer(left, right):
    return lax.dot_general(left, right, (((0,), (0,)), ((), ())), preferred_element_type=jnp.float32)


def gathered(value, axes):
    members = lax.axis_size(axes)
    copies = jnp.broadcast_to(value[None], (members,) + value.shape)
    return lax.all_to_all(copies, axes, 0, 0)


def summed(parts):
    lon, lat, batch = (lax.axis_size(a) for a in EVERY)
    pairs = [(i, i ^ 1) for i in range(lon)]
    core = lax.axis_index("lon") % 2
    groups = [
        [((x * 2 + c) * lat + z) * batch + y for x in range(lon // 2) for z in range(lat) for y in range(batch)]
        for c in range(2)
    ]
    members = lon // 2 * lat * batch
    sent = lax.dynamic_index_in_dim(parts, 1 - core, 0, keepdims=False).astype(jnp.bfloat16)
    kept = lax.dynamic_index_in_dim(parts, core, 0, keepdims=False)
    half = kept + lax.ppermute(sent, "lon", pairs).astype(jnp.float32)
    rows = half.shape[0]
    chunk = -(-rows // (members * 8)) * 8
    half = jnp.pad(half.astype(jnp.bfloat16), ((0, chunk * members - rows), (0, 0)))
    chunks = lax.all_to_all(half.reshape(members, chunk, -1), EVERY, 0, 0, axis_index_groups=groups)
    own = jnp.sum(chunks.astype(jnp.float32), axis=0).astype(jnp.bfloat16)
    copies = jnp.broadcast_to(own[None], (members,) + own.shape)
    whole = lax.all_to_all(copies, EVERY, 0, 0, axis_index_groups=groups)
    mine = whole.reshape(members * chunk, -1)[:rows]
    other = lax.ppermute(mine, "lon", pairs)
    first = jnp.where(core == 0, mine, other).astype(jnp.float32)
    second = jnp.where(core == 0, other, mine).astype(jnp.float32)
    return first, second


def local(features, weight_one, norm_gain, norm_bias, weight_two, out_cotangent):
    cells = features.shape[0] * features.shape[1] * features.shape[2]
    count = cells * lax.axis_size(TILE)
    rows, cols = features.shape[1:3]
    feats_wide = extend(features, RATE_ONE)
    pre_one = conv_valid(feats_wide, weight_one, RATE_ONE)
    near = jnp.sum(pre_one, axis=(0, 1, 2)) / cells
    around = jnp.sum((pre_one - near) ** 2, axis=(0, 1, 2))
    stats = gathered(jnp.stack([near, around]), TILE)
    mean = jnp.mean(stats[:, 0], axis=0)
    var = (jnp.sum(stats[:, 1], axis=0) + cells * jnp.sum((stats[:, 0] - mean) ** 2, axis=0)) / count
    rstd = lax.rsqrt(var + 1e-05)
    normed = (pre_one - mean) * rstd
    shifted = norm_gain * normed + norm_bias
    sig = jax.nn.sigmoid(shifted)
    hidden = (shifted * sig).astype(jnp.bfloat16)
    cotan_wide = extend(out_cotangent, RATE_TWO)
    flipped = jnp.flip(weight_two, (0, 1)).transpose(0, 1, 3, 2)
    grad_hidden = conv_valid(cotan_wide, flipped, RATE_TWO)
    grad_shift = grad_hidden * sig * (1.0 + shifted * (1.0 - sig))
    local_b = jnp.sum(grad_shift, axis=(0, 1, 2))
    local_ba = jnp.sum(grad_shift * normed, axis=(0, 1, 2))
    every = gathered(jnp.stack([local_b, local_ba]), EVERY)
    every = every.reshape(-1, lax.axis_size("batch"), 2, every.shape[-1])
    group = jnp.sum(every, axis=0)
    sum_b, sum_ba = lax.dynamic_index_in_dim(group, lax.axis_index("batch"), 0, keepdims=False)
    grad_bias, grad_gain = jnp.sum(group, axis=0)
    grad_pre = (
        (norm_gain * grad_shift - norm_gain * sum_b / count - normed * norm_gain * sum_ba / count)
        * rstd
    ).astype(jnp.bfloat16)
    hidden_wide = extend(hidden, RATE_TWO)
    output_maps = conv_valid(hidden_wide, weight_two, RATE_TWO).astype(jnp.bfloat16)
    hidden_rows = hidden.reshape(cells, -1)
    grad_rows = grad_pre.reshape(cells, -1)
    part_two = jnp.concatenate([outer(hidden_rows, w) for w in reversed(windows(cotan_wide, RATE_TWO, rows, cols))])
    part_one = jnp.concatenate([outer(w, grad_rows) for w in windows(feats_wide, RATE_ONE, rows, cols)])
    grad_one, grad_two = summed(jnp.stack([part_one, part_two]))
    shape = weight_one.shape
    return (output_maps, grad_one.reshape(shape), grad_two.reshape(shape), grad_gain, grad_bias)


def solution(mesh):
    placed = (P("batch", "lon", "lat", None), P(), P(), P(), P(), P("batch", "lon", "lat", None))
    return jax.shard_map(
        local,
        mesh=mesh,
        in_specs=placed,
        out_specs=(P("batch", "lon", "lat", None), P(), P(), P(), P()),
        check_vma=False,
    )
```

time: 294 us -> 102 us (0.35)
  blocking collectives: 133 us -> 0 us
  waiting for transfers between devices: 96.1 us -> 19.5 us
  starting transfers between devices: 21.7 us -> 44.2 us
  between operations: 14.5 us -> 1.16 us
  other arithmetic: 6.36 us -> 12.2 us
    psum x4 -> x0, blocking collectives: 133 us -> none  [the longest x1 38.1 us: local(): lax.psum((part_one, part_two, local_ba, local_b), ('lon', 'lat', 'batch'))]
    psum x1 -> x0, waiting for transfers between devices: 88.6 us -> none  [local(): lax.psum((part_one, part_two, local_ba, local_b), ('lon', 'lat', 'batch'))]
    all_to_all x0 -> x4, starting transfers between devices: none -> 20.7 us  [the longest x2 10.6 us: gathered(): return lax.all_to_all(copies, axes, 0, 0)]
    all_to_all x0 -> x4, waiting for transfers between devices: none -> 16.3 us  [the longest x1 9.11 us: summed(): lax.all_to_all(half.reshape(members, chunk, -1), EVERY, 0, 0, axis_index_...]
    concatenate x3 -> x4, other arithmetic: 4.13 us -> 8.35 us  [extended(): value = jnp.concatenate([before, value, after], axis=dim)]
    ppermute x6, waiting for transfers between devices: 3.04 us -> 0.02 us  [extended(): before = lax.ppermute(last, axis, up)]
  transfers between devices with their start and end apart: 13 -> 18, of which waited for: 3 -> 6; matrix products, arithmetic and copies ran while one was open for 6% -> 24% of each run, Pallas kernels for 0% -> 0%
where the time goes in v1:
time: 102 us; the launch traced here: 101 us
  starting transfers between devices  44.2 us (43%)
  waiting for transfers between devices  19.5 us (19%)
  matrix products  12.9 us (13%)
  other arithmetic  12.2 us (12%)
  local copies, waits for them, and re-layouts  11.1 us (11%)
  between operations  1.16 us (1%)
    ppermute x6, starting transfers between devices, extended(): before = lax.ppermute(last, axis, up)  14.6 us
    all_to_all x2, starting transfers between devices, gathered(): return lax.all_to_all(copies, axes, 0, 0)  10.6 us
    all_to_all x1, waiting for transfers between devices, summed(): lax.all_to_all(half.reshape(members, chunk, -1), EVERY, 0, 0, axis_index_...  9.11 us
    ppermute x6, starting transfers between devices, extended(): after = lax.ppermute(initial, axis, down)  8.7 us
    concatenate x4, other arithmetic, extended(): value = jnp.concatenate([before, value, after], axis=dim)  8.35 us
    conv_general_dilated x3, matrix products, conv_valid(): lax.conv_general_dilated(padded, kernel, (1, 1), 'VALID', rhs_dilation=(r...  7.5 us
    all_to_all x1, starting transfers between devices, summed(): lax.all_to_all(half.reshape(members, chunk, -1), EVERY, 0, 0, axis_index_...  6.57 us
    dot_general x18, matrix products, outer(): lax.dot_general(left, right, (((0,), (0,)), ((), ())), preferred_element_...  5.36 us
  transfers between devices with their start and end apart: 18, of which 6 were waited for; matrix products, arithmetic and copies ran while one was open for 24% of the time, Pallas kernels for 0%

profile of v1, /device:TPU:0, one launch (start us, length us, event | category | flops | bytes accessed | tf_op | source)
XLA Modules:
  0.0 101.0 jit_solution(2379355992498206491)
XLA Ops:
  0.6 0.8 fusion.111
  1.6 0.5 collective-permute-start
  2.2 2.0 %collective-permute-start.1 = (bf16[1,6,24,128]{3,0,2,1:T(2,128)(2,1)S(1)}, bf16[1,6,24,128]{3,0,2,1:T(2,128)(2,1)S(1)}, u32[]{:S(2)}, u32[]{:S(2)}) collective-permute-start(bf16[1,6,24,128]{3,0,2,1:T(2,128)(2,1)S(1)} %copy.152), channel_id=1, source_target_pairs={{8,0},{16,8},{24,16},{0,24},{9,1},{17,9},{25,17},{1,25},{10,2},{18... | collective-permute-start | bytes 110600 | tf_op jit(solution)/shard_map/ppermute | solution.py:20
  4.1 0.9 fusion.109
  5.2 0.7 collective-permute-start.8
  6.1 1.1 %collective-permute-start.9 = (bf16[1,12,24,128]{3,0,2,1:T(2,128)(2,1)S(1)}, bf16[1,12,24,128]{3,0,2,1:T(2,128)(2,1)S(1)}, u32[]{:S(2)}, u32[]{:S(2)}) collective-permute-start(bf16[1,12,24,128]{3,0,2,1:T(2,128)(2,1)S(1)} %copy.154), channel_id=1, source_target_pairs={{8,0},{16,8},{24,16},{0,24},{9,1},{17,9},{25,17},{1,25},{10,2},{18... | collective-permute-start | bytes 221192 | tf_op jit(solution)/shard_map/ppermute | solution.py:20
  7.3 0.2 constant_dynamic-update-slice_fusion.1
  7.9 4.3 %collective-permute-start.2 = (bf16[1,36,6,128]{3,0,2,1:T(2,128)(2,1)S(1)}, bf16[1,36,6,128]{3,0,2,1:T(2,128)(2,1)S(1)}, u32[]{:S(2)}, u32[]{:S(2)}) collective-permute-start(bf16[1,36,6,128]{3,0,2,1:T(2,128)(2,1)S(1)} %get-tuple-element.55), channel_id=1, source_target_pairs={{0,2},{2,4},{4,6},{1,3},{3,5},{5,7},{8,10},{10,12},{12,14},{9,11},... | collective-permute-start | bytes 165896 | tf_op jit(solution)/shard_map/ppermute | solution.py:19
  12.2 1.3 %collective-permute-start.3 = (bf16[1,36,6,128]{3,0,2,1:T(2,128)(2,1)S(1)}, bf16[1,36,6,128]{3,0,2,1:T(2,128)(2,1)S(1)}, u32[]{:S(2)}, u32[]{:S(2)}) collective-permute-start(bf16[1,36,6,128]{3,0,2,1:T(2,128)(2,1)S(1)} %get-tuple-element.56), channel_id=1, source_target_pairs={{2,0},{4,2},{6,4},{3,1},{5,3},{7,5},{10,8},{12,10},{14,12},{11,9},... | collective-permute-start | bytes 165896 | tf_op jit(solution)/shard_map/ppermute | solution.py:20
  13.5 0.6 copy.72
  14.1 0.6 copy.73
  14.9 0.2 constant_dynamic-update-slice_fusion.4
  15.3 1.4 %fusion.106 = (bf16[1,48,12,128]{3,0,2,1:T(2,128)(2,1)}, bf16[1,48,12,128]{3,0,2,1:T(2,128)(2,1)}) fusion(bf16[1,48,24,128]{3,0,2,1:T(2,128)(2,1)S(1)} %constant_dynamic-update-slice_fusion.3), kind=kLoop, calls=%fused_computation.176 | loop fusion | bytes 589824 | tf_op jit(solution)/shard_map/slice | solution.py:17
  16.7 5.3 %collective-permute-start.10 = (bf16[1,48,12,128]{3,0,2,1:T(2,128)(2,1)}, bf16[1,48,12,128]{3,0,2,1:T(2,128)(2,1)}, u32[]{:S(2)}, u32[]{:S(2)}) collective-permute-start(bf16[1,48,12,128]{3,0,2,1:T(2,128)(2,1)} %get-tuple-element.44), channel_id=1, source_target_pairs={{0,2},{2,4},{4,6},{1,3},{3,5},{5,7},{8,10},{10,12},{12,14},{9,11},... | collective-permute-start | bytes 442376 | tf_op jit(solution)/shard_map/ppermute | solution.py:19
  22.0 1.3 %collective-permute-start.11 = (bf16[1,48,12,128]{3,0,2,1:T(2,128)(2,1)}, bf16[1,48,12,128]{3,0,2,1:T(2,128)(2,1)}, u32[]{:S(2)}, u32[]{:S(2)}) collective-permute-start(bf16[1,48,12,128]{3,0,2,1:T(2,128)(2,1)} %get-tuple-element.45), channel_id=1, source_target_pairs={{2,0},{4,2},{6,4},{3,1},{5,3},{7,5},{10,8},{12,10},{14,12},{11,9},... | collective-permute-start | bytes 442376 | tf_op jit(solution)/shard_map/ppermute | solution.py:20
  23.3 0.6 copy.75
  24.0 2.2 %fusion.113 = (f32[128]{0:T(128)S(1)}, f32[1,24,24,128]{3,0,2,1:T(1,128)S(1)}) fusion(bf16[3,3,128,128]{3,2,1,0:T(8,128)(2,1)S(1)} %copy-done.12, bf16[1,36,6,128]{3,0,2,1:T(2,128)(2,1)S(1)} %collective-permute-done.3, bf16[1,36,24,128]{3,0,2,1:T(2,128)(2,1)S(1)} %constant_dynamic-update-slice_fusion, bf16[1,36,6,128]{3,0,2,1:T(2,128)(2,1)S(1)} %collective-permute-done.2), kind=kOutput, calls=%fused_computation.183 | convolution fusion | flops 170938240 | bytes 922112 | tf_op jit(solution)/shard_map/conv_general_dilated | solution.py:31
  26.2 0.6 multiply_reduce_fusion.1
  26.8 0.6 broadcast_in_dim.6
  27.4 7.0 %all-to-all-start = ((f32[16,2,128]{2,1,0:T(2,128)}), f32[16,2,128]{2,1,0:T(2,128)S(1)}, u32[]{:S(2)}, u32[]{:S(2)}) async-start(f32[16,2,128]{2,1,0:T(2,128)} %broadcast_in_dim.6), calls=%async_computation | async-start | bytes 32768 | tf_op jit(solution)/shard_map/all_to_all | solution.py:57
  34.4 3.9 %pad_maximum_fusion.7 = (bf16[1,24,24,128]{3,0,2,1:T(2,128)(2,1)S(1)}, bf16[1,24,24,128]{3,0,2,1:T(2,128)(2,1)S(1)}, bf16[1,24,24,128]{3,0,2,1:T(2,128)(2,1)S(1)...) fusion(bf16[1,36,6,128]{3,0,2,1:T(2,128)(2,1)} %copy-done.6, ...), kind=kLoop, calls=%fused_computation.81 | loop fusion | flops 442368 | bytes 1216512 | tf_op jit(solution)/shard_map/concatenate | solution.py:21
  38.3 2.5 %all-to-all-done = f32[16,2,128]{2,1,0:T(2,128)S(1)} async-done(((f32[16,2,128]{2,1,0:T(2,128)}), f32[16,2,128]{2,1,0:T(2,128)S(1)}, u32[]{:S(2)}, u32[]{:S(2)}) %all-to-all-start) | async-done | bytes 16416 | tf_op jit(solution)/shard_map/all_to_all | solution.py:57
  41.0 3.4 %fusion.2 = f32[1,24,24,128]{3,0,2,1:T(1,128)S(1)} fusion(bf16[3,3,128,128]{3,2,1,0:T(8,128)(2,1)S(1)} %copy-done, bf16[1,48,12,128]{3,0,2,1:T(2,128)(2,1)} %collective-permute-done.11, bf16[1,48,24,128]{3,0,2,1:T(2,128)(2,1)S(1)} %constant_dynamic-update-slice_fusion.3, bf16[1,48,12,128]{3,0,2,1:T(2,128)(2,1)} %collective-permute-done.10), kind=kOutput, calls=%fused_computation.7 | convolution fusion | flops 171638784 | bytes 1179648 | tf_op jit(solution)/shard_map/conv_general_dilated | solution.py:31
  44.6 0.6 broadcast_in_dim.7
  45.2 3.6 %all-to-all-start.1 = ((f32[32,2,128]{2,1,0:T(2,128)}), f32[32,2,128]{2,1,0:T(2,128)S(1)}, u32[]{:S(2)}, u32[]{:S(2)}) async-start(f32[32,2,128]{2,1,0:T(2,128)} %broadcast_in_dim.7), calls=%async_computation.1 | async-start | bytes 65536 | tf_op jit(solution)/shard_map/all_to_all | solution.py:57
  48.9 4.2 %pad_maximum_fusion.5 = (bf16[1,24,24,128]{3,0,2,1:T(2,128)(2,1)S(1)}, bf16[1,24,24,128]{3,0,2,1:T(2,128)(2,1)S(1)}, bf16[1,24,24,128]{3,0,2,1:T(2,128)(2,1)S(1)...) fusion(bf16[1,48,24,128]{3,0,2,1:T(2,128)(2,1)S(1)} %constant_d, ...), kind=kLoop, calls=%fused_computation.79 | loop fusion | flops 442368 | bytes 1474560 | tf_op jit(solution)/shard_map/concatenate | solution.py:21
  53.0 0.2 fusion.14
  53.3 0.2 fusion.13
  53.5 0.2 fusion.12
  53.8 0.2 fusion.11
  54.0 0.2 fusion.10
  54.3 0.2 fusion.9
  54.5 0.2 fusion.8
  54.8 0.4 copy-done.7
  55.1 0.2 fusion.7
  55.4 0.2 fusion.6
  55.6 0.3 all-to-all-done.1
  56.1 0.4 copy-done.3
  56.5 1.2 %fusion.23 = f32[1152,128]{1,0:T(8,128)S(1)} fusion(bf16[1,24,24,128]{3,0,2,1:T(2,128)(2,1)} %get-tuple-element.53, bf16[1,24,24,128]{3,2,1,0:T(8,128)(2,1)S(1)} %multiply_convert_fusion), kind=kOutput, calls=%fused_computation.44 | convolution fusion | flops 18874368 | bytes 360448 | tf_op jit(solution)/shard_map/dot_general | solution.py:51
  57.7 0.2 fusion.22
  58.0 0.2 fusion.21
  58.2 0.2 fusion.20
  58.5 0.3 fusion.19
  58.7 0.2 fusion.18
  59.0 0.3 fusion.17
  59.2 0.3 copy-done.8
  59.5 0.2 fusion.16
  59.7 0.2 fusion.15
  60.3 1.5 %collective-permute-done.12 = bf16[1152,128]{1,0:T(8,128)(2,1)S(1)} collective-permute-done((bf16[1152,128]{1,0:T(8,128)(2,1)S(1)}, bf16[1152,128]{1,0:T(8,128)(2,1)S(1)}, u32[]{:S(2)}, u32[]{:S(2)}) %collective-permute-start.12) | collective-permute-done | bytes 294944 | tf_op jit(solution)/shard_map/ppermute | solution.py:71
  61.8 0.8 fusion.30
  62.6 6.6 %all-to-all-start.2 = ((bf16[16,72,128]{2,1,0:T(8,128)(2,1)}), bf16[16,72,128]{2,1,0:T(8,128)(2,1)S(1)}, u32[]{:S(2)}, u32[]{:S(2)}) async-start(bf16[16,72,128]{2,1,0:T(8,128)(2,1)} %bitcast.43), calls=%async_computation.2 | async-start | bytes 589824 | tf_op jit(solution)/shard_map/all_to_all | solution.py:75
  69.3 1.7 %collective-permute-start.5 = (bf16[1,12,24,128]{3,2,1,0:T(8,128)(2,1)S(1)}, bf16[1,12,24,128]{3,2,1,0:T(8,128)(2,1)S(1)}, u32[]{:S(2)}, u32[]{:S(2)}) collective-permute-start(bf16[1,12,24,128]{3,2,1,0:T(8,128)(2,1)S(1)} %get-tuple-element.63), channel_id=1, source_target_pairs={{8,0},{16,8},{24,16},{0,24},{9,1},{17,9},{25,17},{1,25},{10,2},{18... | collective-permute-start | bytes 221192 | tf_op jit(solution)/shard_map/ppermute | solution.py:20
  71.0 9.1 %all-to-all-done.2 = bf16[16,72,128]{2,1,0:T(8,128)(2,1)S(1)} async-done(((bf16[16,72,128]{2,1,0:T(8,128)(2,1)}), bf16[16,72,128]{2,1,0:T(8,128)(2,1)S(1)}, u32[]{:S(2)}, u32[]{:S(2)}) %all-to-all-start.2) | async-done | bytes 294944 | tf_op jit(solution)/shard_map/all_to_all | solution.py:75
  80.2 0.8 broadcast_in_dim.8
  81.0 3.5 %all-to-all-start.3 = ((bf16[16,72,128]{2,1,0:T(8,128)(2,1)}), bf16[16,72,128]{2,1,0:T(8,128)(2,1)S(1)}, u32[]{:S(2)}, u32[]{:S(2)}) async-start(bf16[16,72,128]{2,1,0:T(8,128)(2,1)} %broadcast_in_dim.8), calls=%async_computation.3 | async-start | bytes 589824 | tf_op jit(solution)/shard_map/all_to_all | solution.py:78
  84.7 3.7 %collective-permute-start.6 = (bf16[1,48,12,128]{3,2,1,0:T(8,128)(2,1)S(1)}, bf16[1,48,12,128]{3,2,1,0:T(8,128)(2,1)S(1)}, u32[]{:S(2)}, u32[]{:S(2)}) collective-permute-start(bf16[1,48,12,128]{3,2,1,0:T(8,128)(2,1)S(1)} %get-tuple-element.58), channel_id=1, source_target_pairs={{0,2},{2,4},{4,6},{1,3},{3,5},{5,7},{8,10},{10,12},{12,14},{9,11},... | collective-permute-start | bytes 442376 | tf_op jit(solution)/shard_map/ppermute | solution.py:19
  88.4 1.3 %collective-permute-start.7 = (bf16[1,48,12,128]{3,2,1,0:T(8,128)(2,1)S(1)}, bf16[1,48,12,128]{3,2,1,0:T(8,128)(2,1)S(1)}, u32[]{:S(2)}, u32[]{:S(2)}) collective-permute-start(bf16[1,48,12,128]{3,2,1,0:T(8,128)(2,1)S(1)} %get-tuple-element.59), channel_id=1, source_target_pairs={{2,0},{4,2},{6,4},{3,1},{5,3},{7,5},{10,8},{12,10},{14,12},{11,9},... | collective-permute-start | bytes 442376 | tf_op jit(solution)/shard_map/ppermute | solution.py:20
  89.7 0.5 slice_bitcast_fusion
  90.2 4.4 %all-to-all-done.3 = bf16[16,72,128]{2,1,0:T(8,128)(2,1)S(1)} async-done(((bf16[16,72,128]{2,1,0:T(8,128)(2,1)}), bf16[16,72,128]{2,1,0:T(8,128)(2,1)S(1)}, u32[]{:S(2)}, u32[]{:S(2)}) %all-to-all-start.3) | async-done | bytes 294944 | tf_op jit(solution)/shard_map/all_to_all | solution.py:78
  94.6 1.7 %collective-permute-done.7 = bf16[1,48,12,128]{3,2,1,0:T(8,128)(2,1)S(1)} collective-permute-done((bf16[1,48,12,128]{3,2,1,0:T(8,128)(2,1)S(1)}, bf16[1,48,12,128]{3,2,1,0:T(8,128)(2,1)S(1)}, u32[]{:S(2)}, u32[]{:S(2)}) %collective-permute-start.7) | collective-permute-done | bytes 147488 | tf_op jit(solution)/shard_map/ppermute | solution.py:20
  96.6 2.0 %fusion.3 = bf16[1,24,24,128]{3,0,2,1:T(2,128)(2,1)S(1)} fusion(bf16[3,3,128,128]{3,2,1,0:T(8,128)(2,1)S(1)} %copy-done, bf16[1,48,48,128]{3,2,1,0:T(8,128)(2,1)S(1)} %pad_maximum_fusion.4), kind=kOutput, calls=%fused_computation.8 | convolution fusion | flops 169943040 | bytes 1032192 | tf_op jit(solution)/shard_map/conv_general_dilated | solution.py:31
  98.6 0.7 copy.77
  99.3 0.9 convert.3
  100.2 0.9 convert.4
  (71 shorter events, 2.5 us)
Async XLA Ops:
  0.6 40.3 %copy-start = (bf16[3,3,128,128]{3,2,1,0:T(8,128)(2,1)S(1)}, bf16[3,3,128,128]{3,2,1,0:T(8,128)(2,1)}, u32[]{:S(2)}) copy-start(bf16[3,3,128,128]{3,2,1,0:T(8,128)(2,1)} %param.10) | copy-start | bytes 884740
  1.5 5.8 %copy-start.1 = (bf16[1,24,24,128]{3,2,1,0:T(8,128)(2,1)S(1)}, bf16[1,24,24,128]{3,2,1,0:T(8,128)(2,1)}, u32[]{:S(2)}) copy-start(bf16[1,24,24,128]{3,2,1,0:T(8,128)(2,1)} %param.6) | copy-start | bytes 442372
  1.6 5.6 %collective-permute-start = (bf16[1,6,24,128]{3,0,2,1:T(2,128)(2,1)S(1)}, bf16[1,6,24,128]{3,0,2,1:T(2,128)(2,1)S(1)}, u32[]{:S(2)}, u32[]{:S(2)}) collective-permute-start(bf16[1,6,24,128]{3,0,2,1:T(2,128)(2,1)S(1)} %copy.151), channel_id=1, source_target_pairs={{0,8},{8,16},{16,24},{24,0},{1,9},{9,17},{17,25},{25,1},{2,10},{10... | collective-permute-start | bytes 110600 | tf_op jit(solution)/shard_map/ppermute | solution.py:19
  2.2 5.4 %collective-permute-start.1 = (bf16[1,6,24,128]{3,0,2,1:T(2,128)(2,1)S(1)}, bf16[1,6,24,128]{3,0,2,1:T(2,128)(2,1)S(1)}, u32[]{:S(2)}, u32[]{:S(2)}) collective-permute-start(bf16[1,6,24,128]{3,0,2,1:T(2,128)(2,1)S(1)} %copy.152), channel_id=1, source_target_pairs={{8,0},{16,8},{24,16},{0,24},{9,1},{17,9},{25,17},{1,25},{10,2},{18... | collective-permute-start | bytes 110600 | tf_op jit(solution)/shard_map/ppermute | solution.py:20
  5.2 9.5 %collective-permute-start.8 = (bf16[1,12,24,128]{3,0,2,1:T(2,128)(2,1)S(1)}, bf16[1,12,24,128]{3,0,2,1:T(2,128)(2,1)S(1)}, u32[]{:S(2)}, u32[]{:S(2)}) collective-permute-start(bf16[1,12,24,128]{3,0,2,1:T(2,128)(2,1)S(1)} %copy.153), channel_id=1, source_target_pairs={{0,8},{8,16},{16,24},{24,0},{1,9},{9,17},{17,25},{25,1},{2,10},{10... | collective-permute-start | bytes 221192 | tf_op jit(solution)/shard_map/ppermute | solution.py:19
  6.1 9.1 %collective-permute-start.9 = (bf16[1,12,24,128]{3,0,2,1:T(2,128)(2,1)S(1)}, bf16[1,12,24,128]{3,0,2,1:T(2,128)(2,1)S(1)}, u32[]{:S(2)}, u32[]{:S(2)}) collective-permute-start(bf16[1,12,24,128]{3,0,2,1:T(2,128)(2,1)S(1)} %copy.154), channel_id=1, source_target_pairs={{8,0},{16,8},{24,16},{0,24},{9,1},{17,9},{25,17},{1,25},{10,2},{18... | collective-permute-start | bytes 221192 | tf_op jit(solution)/shard_map/ppermute | solution.py:20
  7.5 7.3 %copy-start.2 = (bf16[1,24,24,128]{3,2,1,0:T(8,128)(2,1)S(1)}, bf16[1,24,24,128]{3,2,1,0:T(8,128)(2,1)}, u32[]{:S(2)}) copy-start(bf16[1,24,24,128]{3,2,1,0:T(8,128)(2,1)} %param.11) | copy-start | bytes 442372
  7.9 16.0 %collective-permute-start.2 = (bf16[1,36,6,128]{3,0,2,1:T(2,128)(2,1)S(1)}, bf16[1,36,6,128]{3,0,2,1:T(2,128)(2,1)S(1)}, u32[]{:S(2)}, u32[]{:S(2)}) collective-permute-start(bf16[1,36,6,128]{3,0,2,1:T(2,128)(2,1)S(1)} %get-tuple-element.55), channel_id=1, source_target_pairs={{0,2},{2,4},{4,6},{1,3},{3,5},{5,7},{8,10},{10,12},{12,14},{9,11},... | collective-permute-start | bytes 165896 | tf_op jit(solution)/shard_map/ppermute | solution.py:19
  12.2 11.8 %collective-permute-start.3 = (bf16[1,36,6,128]{3,0,2,1:T(2,128)(2,1)S(1)}, bf16[1,36,6,128]{3,0,2,1:T(2,128)(2,1)S(1)}, u32[]{:S(2)}, u32[]{:S(2)}) collective-permute-start(bf16[1,36,6,128]{3,0,2,1:T(2,128)(2,1)S(1)} %get-tuple-element.56), channel_id=1, source_target_pairs={{2,0},{4,2},{6,4},{3,1},{5,3},{7,5},{10,8},{12,10},{14,12},{11,9},... | collective-permute-start | bytes 165896 | tf_op jit(solution)/shard_map/ppermute | solution.py:20
  15.3 8.7 %copy-start.12 = (bf16[3,3,128,128]{3,2,1,0:T(8,128)(2,1)S(1)}, bf16[3,3,128,128]{3,2,1,0:T(8,128)(2,1)}, u32[]{:S(2)}) copy-start(bf16[3,3,128,128]{3,2,1,0:T(8,128)(2,1)} %param.7) | copy-start | bytes 884740
  16.7 24.2 %collective-permute-start.10 = (bf16[1,48,12,128]{3,0,2,1:T(2,128)(2,1)}, bf16[1,48,12,128]{3,0,2,1:T(2,128)(2,1)}, u32[]{:S(2)}, u32[]{:S(2)}) collective-permute-start(bf16[1,48,12,128]{3,0,2,1:T(2,128)(2,1)} %get-tuple-element.44), channel_id=1, source_target_pairs={{0,2},{2,4},{4,6},{1,3},{3,5},{5,7},{8,10},{10,12},{12,14},{9,11},... | collective-permute-start | bytes 442376 | tf_op jit(solution)/shard_map/ppermute | solution.py:19
  22.0 19.0 %collective-permute-start.11 = (bf16[1,48,12,128]{3,0,2,1:T(2,128)(2,1)}, bf16[1,48,12,128]{3,0,2,1:T(2,128)(2,1)}, u32[]{:S(2)}, u32[]{:S(2)}) collective-permute-start(bf16[1,48,12,128]{3,0,2,1:T(2,128)(2,1)} %get-tuple-element.45), channel_id=1, source_target_pairs={{2,0},{4,2},{6,4},{3,1},{5,3},{7,5},{10,8},{12,10},{14,12},{11,9},... | collective-permute-start | bytes 442376 | tf_op jit(solution)/shard_map/ppermute | solution.py:20
  23.9 2.2 %copy-start.5 = (bf16[1,36,6,128]{3,0,2,1:T(2,128)(2,1)}, bf16[1,36,6,128]{3,0,2,1:T(2,128)(2,1)S(1)}, u32[]{:S(2)}) copy-start(bf16[1,36,6,128]{3,0,2,1:T(2,128)(2,1)S(1)} %collective-permute-done.2) | copy-start | bytes 165892
  24.0 2.2 %copy-start.6 = (bf16[1,36,6,128]{3,0,2,1:T(2,128)(2,1)}, bf16[1,36,6,128]{3,0,2,1:T(2,128)(2,1)S(1)}, u32[]{:S(2)}) copy-start(bf16[1,36,6,128]{3,0,2,1:T(2,128)(2,1)S(1)} %collective-permute-done.3) | copy-start | bytes 165892
  27.4 13.4 %all-to-all-start = ((f32[16,2,128]{2,1,0:T(2,128)}), f32[16,2,128]{2,1,0:T(2,128)S(1)}, u32[]{:S(2)}, u32[]{:S(2)}) async-start(f32[16,2,128]{2,1,0:T(2,128)} %broadcast_in_dim.6), calls=%async_computation | async-start | bytes 32768 | tf_op jit(solution)/shard_map/all_to_all | solution.py:57
  40.9 3.4 %copy-start.10 = (f32[128]{0:T(128)S(1)}, f32[128]{0:T(128)}, u32[]{:S(2)}) copy-start(f32[128]{0:T(128)} %param.8) | copy-start | bytes 1540
  40.9 3.4 %copy-start.11 = (f32[128]{0:T(128)S(1)}, f32[128]{0:T(128)}, u32[]{:S(2)}) copy-start(f32[128]{0:T(128)} %param.9) | copy-start | bytes 1540
  45.2 10.7 %all-to-all-start.1 = ((f32[32,2,128]{2,1,0:T(2,128)}), f32[32,2,128]{2,1,0:T(2,128)S(1)}, u32[]{:S(2)}, u32[]{:S(2)}) async-start(f32[32,2,128]{2,1,0:T(2,128)} %broadcast_in_dim.7), calls=%async_computation.1 | async-start | bytes 65536 | tf_op jit(solution)/shard_map/all_to_all | solution.py:57
  54.3 0.9 copy-start.7
  55.9 0.6 copy-start.3
  56.0 1.8 %copy-start.9 = (bf16[1,6,24,128]{3,2,1,0:T(8,128)(2,1)S(1)}, bf16[1,6,24,128]{3,2,1,0:T(8,128)(2,1)}, u32[]{:S(2)}) copy-start(bf16[1,6,24,128]{3,2,1,0:T(8,128)(2,1)} %copy.72) | copy-start | bytes 110596
  58.7 0.8 copy-start.8
  60.1 1.6 %collective-permute-start.12 = (bf16[1152,128]{1,0:T(8,128)(2,1)S(1)}, bf16[1152,128]{1,0:T(8,128)(2,1)S(1)}, u32[]{:S(2)}, u32[]{:S(2)}) collective-permute-start(bf16[1152,128]{1,0:T(8,128)(2,1)S(1)} %fusion.39), channel_id=1, source_target_pairs={{0,8},{8,0},{16,24},{24,16},{1,9},{9,1},{17,25},{25,17},{2,10},{10... | collective-permute-start | bytes 884744 | tf_op jit(solution)/shard_map/ppermute | solution.py:71
  62.6 8.4 %copy-start.4 = (f32[32,2,128]{2,1,0:T(2,128)S(1)}, f32[32,2,128]{2,1,0:T(2,128)}, u32[]{:S(2)}) copy-start(f32[32,2,128]{2,1,0:T(2,128)} %copy-done.3) | copy-start | bytes 98308
  62.6 17.6 %all-to-all-start.2 = ((bf16[16,72,128]{2,1,0:T(8,128)(2,1)}), bf16[16,72,128]{2,1,0:T(8,128)(2,1)S(1)}, u32[]{:S(2)}, u32[]{:S(2)}) async-start(bf16[16,72,128]{2,1,0:T(8,128)(2,1)} %bitcast.43), calls=%async_computation.2 | async-start | bytes 589824 | tf_op jit(solution)/shard_map/all_to_all | solution.py:75
  69.2 15.3 %collective-permute-start.4 = (bf16[1,12,24,128]{3,2,1,0:T(8,128)(2,1)S(1)}, bf16[1,12,24,128]{3,2,1,0:T(8,128)(2,1)S(1)}, u32[]{:S(2)}, u32[]{:S(2)}) collective-permute-start(bf16[1,12,24,128]{3,2,1,0:T(8,128)(2,1)S(1)} %get-tuple-element.62), channel_id=1, source_target_pairs={{0,8},{8,16},{16,24},{24,0},{1,9},{9,17},{17,25},{25,1},{2,10},{10... | collective-permute-start | bytes 221192 | tf_op jit(solution)/shard_map/ppermute | solution.py:19
  69.3 15.3 %collective-permute-start.5 = (bf16[1,12,24,128]{3,2,1,0:T(8,128)(2,1)S(1)}, bf16[1,12,24,128]{3,2,1,0:T(8,128)(2,1)S(1)}, u32[]{:S(2)}, u32[]{:S(2)}) collective-permute-start(bf16[1,12,24,128]{3,2,1,0:T(8,128)(2,1)S(1)} %get-tuple-element.63), channel_id=1, source_target_pairs={{8,0},{16,8},{24,16},{0,24},{9,1},{17,9},{25,17},{1,25},{10,2},{18... | collective-permute-start | bytes 221192 | tf_op jit(solution)/shard_map/ppermute | solution.py:20
  81.0 13.7 %all-to-all-start.3 = ((bf16[16,72,128]{2,1,0:T(8,128)(2,1)}), bf16[16,72,128]{2,1,0:T(8,128)(2,1)S(1)}, u32[]{:S(2)}, u32[]{:S(2)}) async-start(bf16[16,72,128]{2,1,0:T(8,128)(2,1)} %broadcast_in_dim.8), calls=%async_computation.3 | async-start | bytes 589824 | tf_op jit(solution)/shard_map/all_to_all | solution.py:78
  84.7 10.0 %collective-permute-start.6 = (bf16[1,48,12,128]{3,2,1,0:T(8,128)(2,1)S(1)}, bf16[1,48,12,128]{3,2,1,0:T(8,128)(2,1)S(1)}, u32[]{:S(2)}, u32[]{:S(2)}) collective-permute-start(bf16[1,48,12,128]{3,2,1,0:T(8,128)(2,1)S(1)} %get-tuple-element.58), channel_id=1, source_target_pairs={{0,2},{2,4},{4,6},{1,3},{3,5},{5,7},{8,10},{10,12},{12,14},{9,11},... | collective-permute-start | bytes 442376 | tf_op jit(solution)/shard_map/ppermute | solution.py:19
  88.4 8.0 %collective-permute-start.7 = (bf16[1,48,12,128]{3,2,1,0:T(8,128)(2,1)S(1)}, bf16[1,48,12,128]{3,2,1,0:T(8,128)(2,1)S(1)}, u32[]{:S(2)}, u32[]{:S(2)}) collective-permute-start(bf16[1,48,12,128]{3,2,1,0:T(8,128)(2,1)S(1)} %get-tuple-element.59), channel_id=1, source_target_pairs={{2,0},{4,2},{6,4},{3,1},{5,3},{7,5},{10,8},{12,10},{14,12},{11,9},... | collective-permute-start | bytes 442376 | tf_op jit(solution)/shard_map/ppermute | solution.py:20
  94.6 4.6 %collective-permute-start.13 = (bf16[1152,128]{1,0:T(8,128)(2,1)S(1)}, bf16[1152,128]{1,0:T(8,128)(2,1)S(1)}, u32[]{:S(2)}, u32[]{:S(2)}) collective-permute-start(bf16[1152,128]{1,0:T(8,128)(2,1)S(1)} %bitcast.216), channel_id=1, source_target_pairs={{0,8},{8,0},{16,24},{24,16},{1,9},{9,1},{17,25},{25,17},{2,10},{10... | collective-permute-start | bytes 884744 | tf_op jit(solution)/shard_map/ppermute | solution.py:80

commit v2 on v0

v2 whole, which is shorter than its diff:
```python
import jax
import jax.numpy as jnp
from jax import lax
from jax.experimental import pallas as pl
from jax.experimental.pallas import tpu as pltpu
from jax.sharding import PartitionSpec as P

RATE_ONE = 6
RATE_TWO = 12
TILE = ("lon", "lat")
EVERY = ("lon", "lat", "batch")
TAPS = [(a, b) for a in range(3) for b in range(3)]
LIMIT = 32 * 1024 * 1024


def swapped(first, last, axis, wrap):
    devices = lax.axis_size(axis)
    odd = lax.axis_index(axis) % 2 == 1
    near = [(i, i ^ 1) for i in range(devices)]
    far = [(i, (i + 1 if i % 2 else i - 1) % devices) for i in range(devices)]
    if not wrap:
        far = [(i, j) for i, j in far if abs(i - j) == 1]
    one = lax.ppermute(jnp.where(odd, first, last), axis, near)
    two = lax.ppermute(jnp.where(odd, last, first), axis, far)
    return jnp.where(odd, one, two), jnp.where(odd, two, one)


def along_lon(tile, width):
    before, after = swapped(tile[:width], tile[-width:], "lon", True)
    return jnp.concatenate([before, tile, after])


def along_lat(tall, width):
    cols = tall.shape[1]
    before, after = swapped(tall[:, :width], tall[:, -width:], "lat", False)
    down = jnp.concatenate([before, tall[:, : cols - width]], axis=1)
    up = jnp.concatenate([tall[:, width:], after], axis=1)
    return [s.reshape(-1, s.shape[2]) for s in (down, tall, up)]


def call(body, outs, flops, *args):
    moved = sum(a.size * a.dtype.itemsize for a in args) + sum(o.size * o.dtype.itemsize for o in outs)
    return pl.pallas_call(
        body,
        out_shape=outs,
        compiler_params=pltpu.CompilerParams(vmem_limit_bytes=LIMIT),
        cost_estimate=pl.CostEstimate(flops=flops, bytes_accessed=moved, transcendentals=0),
    )(*args)


def shaped(rows, channels, kind=jnp.float32):
    return jax.ShapeDtypeStruct((rows, channels), kind)


def dot(left, right, over):
    return lax.dot_general(left, right, ((over[:1], over[1:]), ((), ())), preferred_element_type=jnp.float32)


def convolved(shifts, weight, step, cells, flip):
    total = None
    for a, b in TAPS:
        kernel = weight[2 - a, 2 - b] if flip else weight[a, b]
        term = dot(shifts[b][a * step : a * step + cells, :], kernel, (1, 1) if flip else (1, 0))
        total = term if total is None else total + term
    return total


def local(features, weight_one, norm_gain, norm_bias, weight_two, out_cotangent):
    _, rows, cols, channels = features.shape
    cells = rows * cols
    count = cells * lax.axis_size(TILE)
    step_one, step_two = RATE_ONE * cols, RATE_TWO * cols
    work = 2 * 9 * cells * channels * channels
    gain, bias = norm_gain[None], norm_bias[None]

    feats_tall = along_lon(features[0], RATE_ONE)
    cotan_tall = along_lon(out_cotangent[0], RATE_TWO)
    feats = along_lat(feats_tall, RATE_ONE)

    def first_conv(s0, s1, s2, weight, pre_ref, stat_ref):
        pre = convolved((s0, s1, s2), weight, step_one, cells, False)
        near = jnp.sum(pre, axis=0, keepdims=True) * (1.0 / cells)
        around = jnp.sum((pre - near) ** 2, axis=0, keepdims=True)
        pre_ref[...] = pre
        stat_ref[...] = jnp.concatenate([near, around])

    pre_one, stat = call(first_conv, [shaped(cells, channels), shaped(2, channels)], work, *feats, weight_one)
    members = lax.axis_size(TILE)
    stats = lax.all_to_all(jnp.broadcast_to(stat[None], (members, 2, channels)), TILE, 0, 0)

    cotan = along_lat(cotan_tall, RATE_TWO)

    def cotangent_conv(c0, c1, c2, weight, out_ref):
        out_ref[...] = convolved((c0, c1, c2), weight, step_two, cells, True)

    (grad_hidden,) = call(cotangent_conv, [shaped(cells, channels)], work, *cotan, weight_two)

    def activate(stats, pre, grad, gain, bias, hidden_ref, shift_ref, normed_ref, rstd_ref, sums_ref):
        means = stats[:, 0, :]
        mean = jnp.sum(means, axis=0, keepdims=True) * (1.0 / members)
        apart = jnp.sum((means - mean) ** 2, axis=0, keepdims=True)
        var = (jnp.sum(stats[:, 1, :], axis=0, keepdims=True) + cells * apart) * (1.0 / count)
        rstd = lax.rsqrt(var + 1e-05)
        normed = (pre[...] - mean) * rstd
        shifted = gain[...] * normed + bias[...]
        sig = 1.0 / (1.0 + jnp.exp(-shifted))
        hidden_ref[...] = (shifted * sig).astype(jnp.bfloat16)
        shift = grad[...] * sig * (1.0 + shifted * (1.0 - sig))
        shift_ref[...] = shift
        normed_ref[...] = normed
        rstd_ref[...] = rstd
        sum_b = jnp.sum(shift, axis=0, keepdims=True)
        sum_ba = jnp.sum(shift * normed, axis=0, keepdims=True)
        sums_ref[...] = jnp.concatenate([sum_b, sum_ba])

    hidden, grad_shift, normed, rstd, sums = call(
        activate,
        [
            shaped(cells, channels, jnp.bfloat16),
            shaped(cells, channels),
            shaped(cells, channels),
            shaped(1, channels),
            shaped(2, channels),
        ],
        cells * channels * 20,
        stats, pre_one, grad_hidden, gain, bias,
    )
    devices = lax.axis_size(EVERY)
    batches = lax.axis_size("batch")
    every = lax.all_to_all(jnp.broadcast_to(sums[None], (devices, 2, channels)), EVERY, 0, 0)
    group = jnp.sum(every.reshape(-1, batches, 2, channels), axis=0)
    grad_bias, grad_gain = jnp.sum(group, axis=0)
    own = lax.dynamic_index_in_dim(group, lax.axis_index("batch"), 0, keepdims=False)

    hidden_tall = along_lon(hidden.reshape(rows, cols, channels), RATE_TWO)
    hiddens = along_lat(hidden_tall, RATE_TWO)

    def second_conv(h0, h1, h2, weight, out_ref):
        out_ref[...] = convolved((h0, h1, h2), weight, step_two, cells, False).astype(jnp.bfloat16)

    def second_grad(hidden, c0, c1, c2, out_ref):
        for n, (a, b) in enumerate(TAPS):
            window = (c0, c1, c2)[2 - b][(2 - a) * step_two : (2 - a) * step_two + cells, :]
            out_ref[n * channels : (n + 1) * channels, :] = dot(hidden[...], window, (0, 0)).astype(jnp.bfloat16)

    part_shape = shaped(9 * channels, channels, jnp.bfloat16)
    (part_two,) = call(second_grad, [part_shape], work, hidden, *cotan)

    def first_grad(own, shift, normed, gain, rstd, s0, s1, s2, out_ref):
        scale = gain[...] * rstd[...]
        base = own[0:1, :] * (1.0 / count)
        slope = own[1:2, :] * (1.0 / count)
        grad = ((shift[...] - base - normed[...] * slope) * scale).astype(jnp.bfloat16)
        for n, (a, b) in enumerate(TAPS):
            window = (s0, s1, s2)[b][a * step_one : a * step_one + cells, :]
            out_ref[n * channels : (n + 1) * channels, :] = dot(window, grad, (0, 0)).astype(jnp.bfloat16)

    (part_one,) = call(first_grad, [part_shape], work, own, grad_shift, normed, gain, rstd, *feats)

    lon, lat, batch = (lax.axis_size(a) for a in EVERY)
    pairs = [(i, i ^ 1) for i in range(lon)]
    core = lax.axis_index("lon") % 2 == 1
    groups = [
        [((x * 2 + c) * lat + z) * batch + y for x in range(lon // 2) for z in range(lat) for y in range(batch)]
        for c in range(2)
    ]
    size = devices // 2
    total = 9 * channels
    chunk = -(-total // (size * 8)) * 8
    sent = jnp.where(core, part_one, part_two)
    kept = jnp.where(core, part_two, part_one)
    half = (kept.astype(jnp.float32) + lax.ppermute(sent, "lon", pairs).astype(jnp.float32)).astype(jnp.bfloat16)
    half = jnp.pad(half, ((0, chunk * size - total), (0, 0)))
    chunks = lax.all_to_all(half.reshape(size, chunk, channels), EVERY, 0, 0, axis_index_groups=groups)
    piece = jnp.sum(chunks.astype(jnp.float32), axis=0).astype(jnp.bfloat16)
    whole = lax.all_to_all(
        jnp.broadcast_to(piece[None], (size, chunk, channels)), EVERY, 0, 0, axis_index_groups=groups
    )
    (maps,) = call(second_conv, [shaped(cells, channels, jnp.bfloat16)], work, *hiddens, weight_two)
    mine = whole.reshape(size * chunk, channels)[:total]
    other = lax.ppermute(mine, "lon", pairs)
    shape = weight_one.shape
    grad_one = jnp.where(core, other, mine).astype(jnp.float32).reshape(shape)
    grad_two = jnp.where(core, mine, other).astype(jnp.float32).reshape(shape)
    return (maps.reshape(features.shape), grad_one, grad_two, grad_gain, grad_bias)


def solution(mesh):
    placed = (P("batch", "lon", "lat", None), P(), P(), P(), P(), P("batch", "lon", "lat", None))
    return jax.shard_map(
        local,
        mesh=mesh,
        in_specs=placed,
        out_specs=(P("batch", "lon", "lat", None), P(), P(), P(), P()),
        check_vma=False,
    )
```

time: 294 us -> 77.6 us (0.26)
  blocking collectives: 133 us -> 0 us
  waiting for transfers between devices: 96.1 us -> 32.8 us
  between operations: 14.5 us -> 0.96 us
  matrix products: 11.8 us -> 0 us
  starting transfers between devices: 21.7 us -> 29.5 us
  local copies, waits for them, and re-layouts: 9.81 us -> 4.85 us
  Pallas kernels: 0 us -> 3.68 us
    psum x4 -> x0, blocking collectives: 133 us -> none  [the longest x1 38.1 us: local(): lax.psum((part_one, part_two, local_ba, local_b), ('lon', 'lat', 'batch'))]
    psum x1 -> x0, waiting for transfers between devices: 88.6 us -> none  [local(): lax.psum((part_one, part_two, local_ba, local_b), ('lon', 'lat', 'batch'))]
    all_to_all x0 -> x4, waiting for transfers between devices: none -> 25.4 us  [the longest x1 7.89 us: local(): lax.all_to_all(jnp.broadcast_to(piece[None], (size, chunk, channels)), EV...]
    all_to_all x0 -> x4, starting transfers between devices: none -> 15.6 us  [the longest x1 5.95 us: local(): lax.all_to_all(jnp.broadcast_to(stat[None], (members, 2, channels)), TILE...]
    ppermute x12 -> x14, starting transfers between devices: 21.7 us -> 13.9 us  [the longest x6 7.7 us: swapped(): one = lax.ppermute(jnp.where(odd, first, last), axis, near)]
    conv_general_dilated x3 -> x0, matrix products: 7.5 us -> none  [conv_valid(): lax.conv_general_dilated(padded, kernel, (1, 1), 'VALID', rhs_dilation=(r...]
    dot_general x18 -> x0, matrix products: 4.3 us -> none  [kernel_grad(): jnp.einsum('spqc,spqo->co', window, grad, preferred_element_type=jnp.floa...]
    pallas_call x0 -> x6, Pallas kernels: none -> 3.68 us  [call(): pl.pallas_call(body, out_shape=outs, compiler_params=pltpu.CompilerParams...]
  transfers between devices with their start and end apart: 13 -> 18, of which waited for: 3 -> 9; matrix products, arithmetic and copies ran while one was open for 6% -> 4% of each run, Pallas kernels for 0% -> 4%
where the time goes in v2:
time: 77.6 us; the launch traced here: 77 us
  waiting for transfers between devices  32.8 us (42%)
  starting transfers between devices  29.5 us (38%)
  other arithmetic  5.25 us (7%)
  local copies, waits for them, and re-layouts  4.85 us (6%)
  Pallas kernels  3.68 us (5%)
  between operations  0.96 us (1%)
    all_to_all x1, waiting for transfers between devices, local(): lax.all_to_all(jnp.broadcast_to(piece[None], (size, chunk, channels)), EV...  7.89 us
    ppermute x6, starting transfers between devices, swapped(): one = lax.ppermute(jnp.where(odd, first, last), axis, near)  7.7 us
    all_to_all x1, waiting for transfers between devices, local(): lax.all_to_all(jnp.broadcast_to(sums[None], (devices, 2, channels)), EVER...  6.59 us
    all_to_all x1, waiting for transfers between devices, local(): lax.all_to_all(half.reshape(size, chunk, channels), EVERY, 0, 0, axis_ind...  5.99 us
    ppermute x6, starting transfers between devices, swapped(): two = lax.ppermute(jnp.where(odd, last, first), axis, far)  5.98 us
    all_to_all x1, starting transfers between devices, local(): lax.all_to_all(jnp.broadcast_to(stat[None], (members, 2, channels)), TILE...  5.95 us
    all_to_all x1, waiting for transfers between devices, local(): lax.all_to_all(jnp.broadcast_to(stat[None], (members, 2, channels)), TILE...  4.9 us
    ppermute x6, waiting for transfers between devices, swapped(): two = lax.ppermute(jnp.where(odd, last, first), axis, far)  4.77 us
  transfers between devices with their start and end apart: 18, of which 9 were waited for; matrix products, arithmetic and copies ran while one was open for 4% of the time, Pallas kernels for 4%

profile of v2, /device:TPU:0, one launch (start us, length us, event | category | flops | bytes accessed | tf_op | source)
XLA Modules:
  0.0 77.0 jit_solution(3490243924488585860)
XLA Ops:
  0.7 0.8 %select_bitcast_fusion.3 = (bf16[6,24,128]{2,1,0:T(8,128)(2,1)S(1)}, bf16[6,24,128]{2,1,0:T(8,128)(2,1)S(1)}) fusion(pred[]{:T(512)S(6)} %eq.20, bf16[1,24,24,128]{3,2,1,0:T(8,128)(2,1)} %param.6), kind=kLoop, calls=%fused_computation.34 | loop fusion | flops 36864 | bytes 147457 | tf_op jit(solution)/shard_map/jit(_where)/select_n | solution.py:23
  1.5 0.6 collective-permute-start
  2.0 2.6 %collective-permute-start.1 = (bf16[6,24,128]{2,1,0:T(8,128)(2,1)S(1)}, bf16[6,24,128]{2,1,0:T(8,128)(2,1)S(1)}, u32[]{:S(2)}, u32[]{:S(2)}) collective-permute-start(bf16[6,24,128]{2,1,0:T(8,128)(2,1)S(1)} %get-tuple-element.48), channel_id=1, source_target_pairs={{0,24},{8,16},{16,8},{24,0},{1,25},{9,17},{17,9},{25,1},{2,26},{10... | collective-permute-start | bytes 110600 | tf_op jit(solution)/shard_map/ppermute | solution.py:24
  4.7 0.0 copy-start.5
  4.7 0.1 collective-permute-start.4
  4.8 0.0 collective-permute-start.5
  4.8 0.0 collective-permute-done
  4.8 1.7 %collective-permute-done.1 = bf16[6,24,128]{2,1,0:T(8,128)(2,1)S(1)} collective-permute-done((bf16[6,24,128]{2,1,0:T(8,128)(2,1)S(1)}, bf16[6,24,128]{2,1,0:T(8,128)(2,1)S(1)}, u32[]{:S(2)}, u32[]{:S(2)}) %collective-permute-start.1) | collective-permute-done | bytes 36896 | tf_op jit(solution)/shard_map/ppermute | solution.py:24
  6.6 0.1 fusion.2
  6.7 0.7 collective-permute-start.3
  7.4 4.4 %collective-permute-start.2 = (bf16[36,6,128]{2,1,0:T(8,128)(2,1)S(1)}, bf16[36,6,128]{2,1,0:T(8,128)(2,1)S(1)}, u32[]{:S(2)}, u32[]{:S(2)}) collective-permute-start(bf16[36,6,128]{2,1,0:T(8,128)(2,1)S(1)} %get-tuple-element.36), channel_id=1, source_target_pairs={{0,2},{2,0},{4,6},{6,4},{1,3},{3,1},{5,7},{7,5},{8,10},{10,8},{12,... | collective-permute-start | bytes 165896 | tf_op jit(solution)/shard_map/ppermute | solution.py:23
  11.8 0.0 collective-permute-done.4
  11.8 0.0 collective-permute-done.5
  11.9 0.7 fusion.1
  12.6 0.0 collective-permute-start.6
  12.7 0.7 collective-permute-start.7
  13.3 0.0 collective-permute-done.3
  13.4 1.1 %collective-permute-done.2 = bf16[36,6,128]{2,1,0:T(8,128)(2,1)S(1)} collective-permute-done((bf16[36,6,128]{2,1,0:T(8,128)(2,1)S(1)}, bf16[36,6,128]{2,1,0:T(8,128)(2,1)S(1)}, u32[]{:S(2)}, u32[]{:S(2)}) %collective-permute-start.2) | collective-permute-done | bytes 55328 | tf_op jit(solution)/shard_map/ppermute | solution.py:23
  14.4 0.0 copy-start.1
  14.4 0.2 pad_maximum_fusion.7
  14.6 0.8 %copy-done.1 = bf16[3,3,128,128]{3,2,1,0:T(8,128)(2,1)S(1)} copy-done((bf16[3,3,128,128]{3,2,1,0:T(8,128)(2,1)S(1)}, bf16[3,3,128,128]{3,2,1,0:T(8,128)(2,1)}, u32[]{:S(2)}) %copy-start.1) | copy-done | bytes 294936
  15.4 0.6 shard_map.101
  16.0 0.6 broadcast_in_dim.10
  16.6 6.0 %all-to-all-start = ((f32[16,2,128]{2,1,0:T(2,128)}), f32[16,2,128]{2,1,0:T(2,128)S(1)}, u32[]{:S(2)}, u32[]{:S(2)}) async-start(f32[16,2,128]{2,1,0:T(2,128)} %broadcast_in_dim.10), calls=%async_computation | async-start | bytes 32768 | tf_op jit(solution)/shard_map/all_to_all | solution.py:89
  22.6 0.0 collective-permute-done.6
  22.6 0.0 collective-permute-done.7
  22.6 0.0 copy-start
  22.6 0.2 pad_maximum_fusion.1
  22.9 0.7 copy-done
  23.6 0.5 shard_map.102.grad
  24.1 4.9 %all-to-all-done.stats = f32[16,2,128]{2,1,0:T(2,128)S(1)} async-done(((f32[16,2,128]{2,1,0:T(2,128)}), f32[16,2,128]{2,1,0:T(2,128)S(1)}, u32[]{:S(2)}, u32[]{:S(2)}) %all-to-all-start) | async-done | bytes 16416 | tf_op jit(solution)/shard_map/all_to_all | solution.py:89
  29.0 0.7 copy-done.2
  29.7 0.0 copy-done.3
  29.7 0.2 shard_map.103
  29.9 0.6 broadcast_in_dim.13
  30.5 2.6 %all-to-all-start.1 = ((f32[32,2,128]{2,1,0:T(2,128)}), f32[32,2,128]{2,1,0:T(2,128)S(1)}, u32[]{:S(2)}, u32[]{:S(2)}) async-start(f32[32,2,128]{2,1,0:T(2,128)} %broadcast_in_dim.13), calls=%async_computation.1 | async-start | bytes 65536 | tf_op jit(solution)/shard_map/all_to_all | solution.py:130
  33.1 0.6 shard_map.105
  33.7 6.6 %all-to-all-done.1 = f32[32,2,128]{2,1,0:T(2,128)S(1)} async-done(((f32[32,2,128]{2,1,0:T(2,128)}), f32[32,2,128]{2,1,0:T(2,128)S(1)}, u32[]{:S(2)}, u32[]{:S(2)}) %all-to-all-start.1) | async-done | bytes 32800 | tf_op jit(solution)/shard_map/all_to_all | solution.py:130
  40.3 0.6 shard_map.106
  41.0 0.2 collective-permute-start.12
  41.2 1.5 %collective-permute-done.12 = bf16[1152,128]{1,0:T(8,128)(2,1)S(1)} collective-permute-done((bf16[1152,128]{1,0:T(8,128)(2,1)S(1)}, bf16[1152,128]{1,0:T(8,128)(2,1)S(1)}, u32[]{:S(2)}, u32[]{:S(2)}) %collective-permute-start.12) | collective-permute-done | bytes 294944 | tf_op jit(solution)/shard_map/ppermute | solution.py:172
  42.6 0.8 %add_convert_fusion = bf16[1152,128]{1,0:T(8,128)(2,1)} fusion(bf16[1152,128]{1,0:T(8,128)(2,1)S(1)} %collective-permute-done.12, bf16[1152,128]{1,0:T(8,128)(2,1)S(1)} %shard_map.105, bf16[1152,128]{1,0:T(8,128)(2,1)S(1)} %shard_map.106, pred[]{:T(512)S(6)} %eq.20), kind=kLoop, calls=%fused_computation | loop fusion | flops 737280 | bytes 1179649 | tf_op jit(solution)/shard_map/convert_element_type | solution.py:172
  43.5 3.5 %all-to-all-start.2 = ((bf16[16,72,128]{2,1,0:T(8,128)(2,1)}), bf16[16,72,128]{2,1,0:T(8,128)(2,1)S(1)}, u32[]{:S(2)}, u32[]{:S(2)}) async-start(bf16[16,72,128]{2,1,0:T(8,128)(2,1)} %bitcast.23), calls=%async_computation.2 | async-start | bytes 589824 | tf_op jit(solution)/shard_map/all_to_all | solution.py:174
  47.0 1.4 %collective-permute-start.9 = (bf16[12,24,128]{2,1,0:T(8,128)(2,1)S(1)}, bf16[12,24,128]{2,1,0:T(8,128)(2,1)S(1)}, u32[]{:S(2)}, u32[]{:S(2)}) collective-permute-start(bf16[12,24,128]{2,1,0:T(8,128)(2,1)S(1)} %bitcast.67), channel_id=1, source_target_pairs={{0,24},{8,16},{16,8},{24,0},{1,25},{9,17},{17,9},{25,1},{2,26},{10... | collective-permute-start | bytes 221192 | tf_op jit(solution)/shard_map/ppermute | solution.py:24
  48.4 0.7 collective-permute-start.8
  49.1 3.1 %collective-permute-done.9 = bf16[12,24,128]{2,1,0:T(8,128)(2,1)S(1)} collective-permute-done((bf16[12,24,128]{2,1,0:T(8,128)(2,1)S(1)}, bf16[12,24,128]{2,1,0:T(8,128)(2,1)S(1)}, u32[]{:S(2)}, u32[]{:S(2)}) %collective-permute-start.9) | collective-permute-done | bytes 73760 | tf_op jit(solution)/shard_map/ppermute | solution.py:24
  52.2 0.0 collective-permute-done.8
  52.2 6.0 %all-to-all-done.2 = bf16[16,72,128]{2,1,0:T(8,128)(2,1)S(1)} async-done(((bf16[16,72,128]{2,1,0:T(8,128)(2,1)}), bf16[16,72,128]{2,1,0:T(8,128)(2,1)S(1)}, u32[]{:S(2)}, u32[]{:S(2)}) %all-to-all-start.2) | async-done | bytes 294944 | tf_op jit(solution)/shard_map/all_to_all | solution.py:174
  58.3 0.8 broadcast_in_dim.28
  59.0 3.5 %all-to-all-start.3 = ((bf16[16,72,128]{2,1,0:T(8,128)(2,1)}), bf16[16,72,128]{2,1,0:T(8,128)(2,1)S(1)}, u32[]{:S(2)}, u32[]{:S(2)}) async-start(bf16[16,72,128]{2,1,0:T(8,128)(2,1)} %broadcast_in_dim.28), calls=%async_computation.3 | async-start | bytes 589824 | tf_op jit(solution)/shard_map/all_to_all | solution.py:176
  62.6 0.1 fusion
  62.7 1.9 %collective-permute-start.10 = (bf16[48,12,128]{2,1,0:T(8,128)(2,1)S(1)}, bf16[48,12,128]{2,1,0:T(8,128)(2,1)S(1)}, u32[]{:S(2)}, u32[]{:S(2)}) collective-permute-start(bf16[48,12,128]{2,1,0:T(8,128)(2,1)S(1)} %get-tuple-element.26), channel_id=1, source_target_pairs={{0,2},{2,0},{4,6},{6,4},{1,3},{3,1},{5,7},{7,5},{8,10},{10,8},{12,... | collective-permute-start | bytes 442376 | tf_op jit(solution)/shard_map/ppermute | solution.py:23
  64.6 0.7 collective-permute-start.11
  65.2 0.5 slice_bitcast_fusion
  65.8 7.9 %all-to-all-done.3 = bf16[16,72,128]{2,1,0:T(8,128)(2,1)S(1)} async-done(((bf16[16,72,128]{2,1,0:T(8,128)(2,1)}), bf16[16,72,128]{2,1,0:T(8,128)(2,1)S(1)}, u32[]{:S(2)}, u32[]{:S(2)}) %all-to-all-start.3) | async-done | bytes 294944 | tf_op jit(solution)/shard_map/all_to_all | solution.py:176
  73.7 0.0 collective-permute-start.13
  73.7 0.0 collective-permute-done.11
  73.7 0.1 pad_maximum_fusion.5
  73.8 0.1 pad_maximum_fusion.4
  73.9 1.2 %shard_map.104 = bf16[576,128]{1,0:T(8,128)(2,1)} custom-call(bf16[1152,128]{1,0:T(8,128)(2,1)S(1)} %bitcast.55, bf16[1152,128]{1,0:T(8,128)(2,1)S(1)} %bitcast.44, bf16[1152,128]{1,0:T(8,128)(2,1)S(1)} %bitcast.54, bf16[3,3,128,128]{3,2,1,0:T(8,128)(2,1)S(1)} %copy-done), custom_call_target="tpu_custom_call" | custom-call | flops 169869312 | bytes 1327104 | tf_op jit(solution)/shard_map/pallas_call | solution.py:43
  75.1 0.1 collective-permute-done.13
  75.2 0.1 broadcast_select_fusion
  75.3 0.9 %convert.3 = f32[3,3,128,128]{3,2,1,0:T(8,128)} convert(bf16[3,3,128,128]{3,2,1,0:T(8,128)(2,1)S(1)} %bitcast.60) | non-fusion elementwise | flops 147456 | bytes 884736 | tf_op jit(solution)/shard_map/reshape | solution.py:183
  76.2 0.9 %convert.4 = f32[3,3,128,128]{3,2,1,0:T(8,128)} convert(bf16[3,3,128,128]{3,2,1,0:T(8,128)(2,1)S(1)} %bitcast.59) | non-fusion elementwise | flops 147456 | bytes 884736 | tf_op jit(solution)/shard_map/reshape | solution.py:184
  (23 shorter events, 0.5 us)
Async XLA Ops:
  0.6 4.0 %copy-start.4 = (bf16[1,24,24,128]{3,2,1,0:T(8,128)(2,1)S(1)}, bf16[1,24,24,128]{3,2,1,0:T(8,128)(2,1)}, u32[]{:S(2)}) copy-start(bf16[1,24,24,128]{3,2,1,0:T(8,128)(2,1)} %param.11) | copy-start | bytes 442372
  1.5 3.4 %collective-permute-start = (bf16[6,24,128]{2,1,0:T(8,128)(2,1)S(1)}, bf16[6,24,128]{2,1,0:T(8,128)(2,1)S(1)}, u32[]{:S(2)}, u32[]{:S(2)}) collective-permute-start(bf16[6,24,128]{2,1,0:T(8,128)(2,1)S(1)} %get-tuple-element.47), channel_id=1, source_target_pairs={{0,8},{8,0},{16,24},{24,16},{1,9},{9,1},{17,25},{25,17},{2,10},{10... | collective-permute-start | bytes 110600 | tf_op jit(solution)/shard_map/ppermute | solution.py:23
  2.0 4.5 %collective-permute-start.1 = (bf16[6,24,128]{2,1,0:T(8,128)(2,1)S(1)}, bf16[6,24,128]{2,1,0:T(8,128)(2,1)S(1)}, u32[]{:S(2)}, u32[]{:S(2)}) collective-permute-start(bf16[6,24,128]{2,1,0:T(8,128)(2,1)S(1)} %get-tuple-element.48), channel_id=1, source_target_pairs={{0,24},{8,16},{16,8},{24,0},{1,25},{9,17},{17,9},{25,1},{2,26},{10... | collective-permute-start | bytes 110600 | tf_op jit(solution)/shard_map/ppermute | solution.py:24
  4.7 1.9 %copy-start.5 = (bf16[1,24,24,128]{3,2,1,0:T(8,128)(2,1)S(1)}, bf16[1,24,24,128]{3,2,1,0:T(8,128)(2,1)}, u32[]{:S(2)}) copy-start(bf16[1,24,24,128]{3,2,1,0:T(8,128)(2,1)} %param.6) | copy-start | bytes 442372
  4.7 7.2 %collective-permute-start.4 = (bf16[12,24,128]{2,1,0:T(8,128)(2,1)S(1)}, bf16[12,24,128]{2,1,0:T(8,128)(2,1)S(1)}, u32[]{:S(2)}, u32[]{:S(2)}) collective-permute-start(bf16[12,24,128]{2,1,0:T(8,128)(2,1)S(1)} %get-tuple-element.43), channel_id=1, source_target_pairs={{0,8},{8,0},{16,24},{24,16},{1,9},{9,1},{17,25},{25,17},{2,10},{10... | collective-permute-start | bytes 221192 | tf_op jit(solution)/shard_map/ppermute | solution.py:23
  4.8 7.0 %collective-permute-start.5 = (bf16[12,24,128]{2,1,0:T(8,128)(2,1)S(1)}, bf16[12,24,128]{2,1,0:T(8,128)(2,1)S(1)}, u32[]{:S(2)}, u32[]{:S(2)}) collective-permute-start(bf16[12,24,128]{2,1,0:T(8,128)(2,1)S(1)} %get-tuple-element.44), channel_id=1, source_target_pairs={{0,24},{8,16},{16,8},{24,0},{1,25},{9,17},{17,9},{25,1},{2,26},{10... | collective-permute-start | bytes 221192 | tf_op jit(solution)/shard_map/ppermute | solution.py:24
  6.7 6.6 %collective-permute-start.3 = (bf16[36,6,128]{2,1,0:T(8,128)(2,1)S(1)}, bf16[36,6,128]{2,1,0:T(8,128)(2,1)S(1)}, u32[]{:S(2)}, u32[]{:S(2)}) collective-permute-start(bf16[36,6,128]{2,1,0:T(8,128)(2,1)S(1)} %get-tuple-element.35), channel_id=1, source_target_pairs={{2,4},{4,2},{3,5},{5,3},{10,12},{12,10},{11,13},{13,11},{18,20},{2... | collective-permute-start | bytes 165896 | tf_op jit(solution)/shard_map/ppermute | solution.py:24
  7.4 7.0 %collective-permute-start.2 = (bf16[36,6,128]{2,1,0:T(8,128)(2,1)S(1)}, bf16[36,6,128]{2,1,0:T(8,128)(2,1)S(1)}, u32[]{:S(2)}, u32[]{:S(2)}) collective-permute-start(bf16[36,6,128]{2,1,0:T(8,128)(2,1)S(1)} %get-tuple-element.36), channel_id=1, source_target_pairs={{0,2},{2,0},{4,6},{6,4},{1,3},{3,1},{5,7},{7,5},{8,10},{10,8},{12,... | collective-permute-start | bytes 165896 | tf_op jit(solution)/shard_map/ppermute | solution.py:23
  12.6 9.9 %collective-permute-start.6 = (bf16[48,12,128]{2,1,0:T(8,128)(2,1)}, bf16[48,12,128]{2,1,0:T(8,128)(2,1)S(1)}, u32[]{:S(2)}, u32[]{:S(2)}) collective-permute-start(bf16[48,12,128]{2,1,0:T(8,128)(2,1)} %get-tuple-element.30), channel_id=1, source_target_pairs={{0,2},{2,0},{4,6},{6,4},{1,3},{3,1},{5,7},{7,5},{8,10},{10,8},{12,... | collective-permute-start | bytes 442376 | tf_op jit(solution)/shard_map/ppermute | solution.py:23
  12.7 9.9 %collective-permute-start.7 = (bf16[48,12,128]{2,1,0:T(8,128)(2,1)S(1)}, bf16[48,12,128]{2,1,0:T(8,128)(2,1)S(1)}, u32[]{:S(2)}, u32[]{:S(2)}) collective-permute-start(bf16[48,12,128]{2,1,0:T(8,128)(2,1)S(1)} %get-tuple-element.31), channel_id=1, source_target_pairs={{2,4},{4,2},{3,5},{5,3},{10,12},{12,10},{11,13},{13,11},{18,20},{2... | collective-permute-start | bytes 442376 | tf_op jit(solution)/shard_map/ppermute | solution.py:24
  14.4 1.0 %copy-start.1 = (bf16[3,3,128,128]{3,2,1,0:T(8,128)(2,1)S(1)}, bf16[3,3,128,128]{3,2,1,0:T(8,128)(2,1)}, u32[]{:S(2)}) copy-start(bf16[3,3,128,128]{3,2,1,0:T(8,128)(2,1)} %weight.3) | copy-start | bytes 884740
  16.6 12.4 %all-to-all-start = ((f32[16,2,128]{2,1,0:T(2,128)}), f32[16,2,128]{2,1,0:T(2,128)S(1)}, u32[]{:S(2)}, u32[]{:S(2)}) async-start(f32[16,2,128]{2,1,0:T(2,128)} %broadcast_in_dim.10), calls=%async_computation | async-start | bytes 32768 | tf_op jit(solution)/shard_map/all_to_all | solution.py:89
  22.6 1.0 %copy-start = (bf16[3,3,128,128]{3,2,1,0:T(8,128)(2,1)S(1)}, bf16[3,3,128,128]{3,2,1,0:T(8,128)(2,1)}, u32[]{:S(2)}) copy-start(bf16[3,3,128,128]{3,2,1,0:T(8,128)(2,1)} %weight.5) | copy-start | bytes 884740
  29.0 0.7 copy-start.2
  29.0 0.7 copy-start.3
  30.5 9.8 %all-to-all-start.1 = ((f32[32,2,128]{2,1,0:T(2,128)}), f32[32,2,128]{2,1,0:T(2,128)S(1)}, u32[]{:S(2)}, u32[]{:S(2)}) async-start(f32[32,2,128]{2,1,0:T(2,128)} %broadcast_in_dim.13), calls=%async_computation.1 | async-start | bytes 65536 | tf_op jit(solution)/shard_map/all_to_all | solution.py:130
  41.0 1.6 %collective-permute-start.12 = (bf16[1152,128]{1,0:T(8,128)(2,1)S(1)}, bf16[1152,128]{1,0:T(8,128)(2,1)S(1)}, u32[]{:S(2)}, u32[]{:S(2)}) collective-permute-start(bf16[1152,128]{1,0:T(8,128)(2,1)S(1)} %broadcast_select_fusion.2), channel_id=1, source_target_pairs={{0,8},{8,0},{16,24},{24,16},{1,9},{9,1},{17,25},{25,17},{2,10},{10... | collective-permute-start | bytes 884744 | tf_op jit(solution)/shard_map/ppermute | solution.py:172
  43.5 14.8 %all-to-all-start.2 = ((bf16[16,72,128]{2,1,0:T(8,128)(2,1)}), bf16[16,72,128]{2,1,0:T(8,128)(2,1)S(1)}, u32[]{:S(2)}, u32[]{:S(2)}) async-start(bf16[16,72,128]{2,1,0:T(8,128)(2,1)} %bitcast.23), calls=%async_computation.2 | async-start | bytes 589824 | tf_op jit(solution)/shard_map/all_to_all | solution.py:174
  47.0 5.2 %collective-permute-start.9 = (bf16[12,24,128]{2,1,0:T(8,128)(2,1)S(1)}, bf16[12,24,128]{2,1,0:T(8,128)(2,1)S(1)}, u32[]{:S(2)}, u32[]{:S(2)}) collective-permute-start(bf16[12,24,128]{2,1,0:T(8,128)(2,1)S(1)} %bitcast.67), channel_id=1, source_target_pairs={{0,24},{8,16},{16,8},{24,0},{1,25},{9,17},{17,9},{25,1},{2,26},{10... | collective-permute-start | bytes 221192 | tf_op jit(solution)/shard_map/ppermute | solution.py:24
  48.4 3.8 %collective-permute-start.8 = (bf16[12,24,128]{2,1,0:T(8,128)(2,1)S(1)}, bf16[12,24,128]{2,1,0:T(8,128)(2,1)S(1)}, u32[]{:S(2)}, u32[]{:S(2)}) collective-permute-start(bf16[12,24,128]{2,1,0:T(8,128)(2,1)S(1)} %bitcast.66), channel_id=1, source_target_pairs={{0,8},{8,0},{16,24},{24,16},{1,9},{9,1},{17,25},{25,17},{2,10},{10... | collective-permute-start | bytes 221192 | tf_op jit(solution)/shard_map/ppermute | solution.py:23
  59.0 14.6 %all-to-all-start.3 = ((bf16[16,72,128]{2,1,0:T(8,128)(2,1)}), bf16[16,72,128]{2,1,0:T(8,128)(2,1)S(1)}, u32[]{:S(2)}, u32[]{:S(2)}) async-start(bf16[16,72,128]{2,1,0:T(8,128)(2,1)} %broadcast_in_dim.28), calls=%async_computation.3 | async-start | bytes 589824 | tf_op jit(solution)/shard_map/all_to_all | solution.py:176
  62.7 11.0 %collective-permute-start.10 = (bf16[48,12,128]{2,1,0:T(8,128)(2,1)S(1)}, bf16[48,12,128]{2,1,0:T(8,128)(2,1)S(1)}, u32[]{:S(2)}, u32[]{:S(2)}) collective-permute-start(bf16[48,12,128]{2,1,0:T(8,128)(2,1)S(1)} %get-tuple-element.26), channel_id=1, source_target_pairs={{0,2},{2,0},{4,6},{6,4},{1,3},{3,1},{5,7},{7,5},{8,10},{10,8},{12,... | collective-permute-start | bytes 442376 | tf_op jit(solution)/shard_map/ppermute | solution.py:23
  64.6 9.1 %collective-permute-start.11 = (bf16[48,12,128]{2,1,0:T(8,128)(2,1)S(1)}, bf16[48,12,128]{2,1,0:T(8,128)(2,1)S(1)}, u32[]{:S(2)}, u32[]{:S(2)}) collective-permute-start(bf16[48,12,128]{2,1,0:T(8,128)(2,1)S(1)} %get-tuple-element.27), channel_id=1, source_target_pairs={{2,4},{4,2},{3,5},{5,3},{10,12},{12,10},{11,13},{13,11},{18,20},{2... | collective-permute-start | bytes 442376 | tf_op jit(solution)/shard_map/ppermute | solution.py:24
  73.7 1.6 %collective-permute-start.13 = (bf16[1152,128]{1,0:T(8,128)(2,1)S(1)}, bf16[1152,128]{1,0:T(8,128)(2,1)S(1)}, u32[]{:S(2)}, u32[]{:S(2)}) collective-permute-start(bf16[1152,128]{1,0:T(8,128)(2,1)S(1)} %bitcast.61), channel_id=1, source_target_pairs={{0,8},{8,0},{16,24},{24,16},{1,9},{9,1},{17,25},{25,17},{2,10},{10... | collective-permute-start | bytes 884744 | tf_op jit(solution)/shard_map/ppermute | solution.py:181

commit v3 on v2

--- a/solution.py
+++ b/solution.py
@@ -4,6 +4,7 @@
 from jax.experimental import pallas as pl
 from jax.experimental.pallas import tpu as pltpu
 from jax.sharding import PartitionSpec as P
+
 
 RATE_ONE = 6
 RATE_TWO = 12
@@ -25,17 +26,24 @@
     return jnp.where(odd, one, two), jnp.where(odd, two, one)
 
 
-def along_lon(tile, width):
-    before, after = swapped(tile[:width], tile[-width:], "lon", True)
-    return jnp.concatenate([before, tile, after])
-
-
-def along_lat(tall, width):
-    cols = tall.shape[1]
-    before, after = swapped(tall[:, :width], tall[:, -width:], "lat", False)
-    down = jnp.concatenate([before, tall[:, : cols - width]], axis=1)
-    up = jnp.concatenate([tall[:, width:], after], axis=1)
-    return [s.reshape(-1, s.shape[2]) for s in (down, tall, up)]
+def widened(tile, width, axis):
+    dim = ("lon", "lat").index(axis)
+    length = tile.shape[dim]
+    first = lax.slice_in_dim(tile, 0, width, axis=dim)
+    last = lax.slice_in_dim(tile, length - width, length, axis=dim)
+    before, after = swapped(first, last, axis, axis == "lon")
+    return jnp.concatenate([before, tile, after], axis=dim)
+
+
+def shifts(wide, width):
+    cols = wide.shape[1] - 2 * width
+    return [wide[:, b * width : b * width + cols].reshape(-1, wide.shape[2]) for b in range(3)]
+
+
+def shifted_copies(tile, width, order):
+    for axis in order:
+        tile = widened(tile, width, axis)
+    return shifts(tile, width)
 
 
 def call(body, outs, flops, *args):
@@ -71,24 +79,33 @@
     count = cells * lax.axis_size(TILE)
     step_one, step_two = RATE_ONE * cols, RATE_TWO * cols
     work = 2 * 9 * cells * channels * channels
-    gain, bias = norm_gain[None], norm_bias[None]
-
-    feats_tall = along_lon(features[0], RATE_ONE)
-    cotan_tall = along_lon(out_cotangent[0], RATE_TWO)
-    feats = along_lat(feats_tall, RATE_ONE)
+
+    def stage(w1, w2, gain, bias, w1_ref, w2_ref, gain_ref, bias_ref):
+        w1_ref[...] = w1[...]
+        w2_ref[...] = w2[...]
+        gain_ref[...] = gain[...]
+        bias_ref[...] = bias[...]
+
+    row = shaped(1, channels)
+    held = jax.ShapeDtypeStruct(weight_one.shape, weight_one.dtype)
+    weight_one, weight_two, gain, bias = call(
+        stage, [held, held, row, row], 0, weight_one, weight_two, norm_gain[None], norm_bias[None]
+    )
+    feats = shifted_copies(features[0], RATE_ONE, ("lon", "lat"))
 
     def first_conv(s0, s1, s2, weight, pre_ref, stat_ref):
         pre = convolved((s0, s1, s2), weight, step_one, cells, False)
         near = jnp.sum(pre, axis=0, keepdims=True) * (1.0 / cells)
         around = jnp.sum((pre - near) ** 2, axis=0, keepdims=True)
         pre_ref[...] = pre
-        stat_ref[...] = jnp.concatenate([near, around])
-
-    pre_one, stat = call(first_conv, [shaped(cells, channels), shaped(2, channels)], work, *feats, weight_one)
+        stat_ref[...] = jnp.broadcast_to(jnp.concatenate([near, around])[None], stat_ref.shape)
+
     members = lax.axis_size(TILE)
-    stats = lax.all_to_all(jnp.broadcast_to(stat[None], (members, 2, channels)), TILE, 0, 0)
-
-    cotan = along_lat(cotan_tall, RATE_TWO)
+    copies = jax.ShapeDtypeStruct((members, 2, channels), jnp.float32)
+    pre_one, stat = call(first_conv, [shaped(cells, channels), copies], work, *feats, weight_one)
+    stats = lax.all_to_all(stat, TILE, 0, 0)
+
+    cotan = shifted_copies(out_cotangent[0], RATE_TWO, ("lon", "lat"))
 
     def cotangent_conv(c0, c1, c2, weight, out_ref):
         out_ref[...] = convolved((c0, c1, c2), weight, step_two, cells, True)
@@ -111,7 +128,7 @@
         rstd_ref[...] = rstd
         sum_b = jnp.sum(shift, axis=0, keepdims=True)
         sum_ba = jnp.sum(shift * normed, axis=0, keepdims=True)
-        sums_ref[...] = jnp.concatenate([sum_b, sum_ba])
+        sums_ref[...] = jnp.broadcast_to(jnp.concatenate([sum_b, sum_ba])[None], sums_ref.shape)
 
     hidden, grad_shift, normed, rstd, sums = call(
         activate,
@@ -119,21 +136,15 @@
             shaped(cells, channels, jnp.bfloat16),
             shaped(cells, channels),
             shaped(cells, channels),
-            shaped(1, channels),
-            shaped(2, channels),
+            row,
+            copies,
         ],
         cells * channels * 20,
         stats, pre_one, grad_hidden, gain, bias,
     )
-    devices = lax.axis_size(EVERY)
-    batches = lax.axis_size("batch")
-    every = lax.all_to_all(jnp.broadcast_to(sums[None], (devices, 2, channels)), EVERY, 0, 0)
-    group = jnp.sum(every.reshape(-1, batches, 2, channels), axis=0)
-    grad_bias, grad_gain = jnp.sum(group, axis=0)
-    own = lax.dynamic_index_in_dim(group, lax.axis_index("batch"), 0, keepdims=False)
-
-    hidden_tall = along_lon(hidden.reshape(rows, cols, channels), RATE_TWO)
-    hiddens = along_lat(hidden_tall, RATE_TWO)
+    every = lax.all_to_all(sums, TILE, 0, 0)
+
+    hiddens = shifted_copies(hidden.reshape(rows, cols, channels), RATE_TWO, ("lat", "lon"))
 
     def second_conv(h0, h1, h2, weight, out_ref):
         out_ref[...] = convolved((h0, h1, h2), weight, step_two, cells, False).astype(jnp.bfloat16)
@@ -146,8 +157,10 @@
     part_shape = shaped(9 * channels, channels, jnp.bfloat16)
     (part_two,) = call(second_grad, [part_shape], work, hidden, *cotan)
 
-    def first_grad(own, shift, normed, gain, rstd, s0, s1, s2, out_ref):
+    def first_grad(every, shift, normed, gain, rstd, s0, s1, s2, out_ref, own_ref):
         scale = gain[...] * rstd[...]
+        own = jnp.sum(every[...], axis=0)
+        own_ref[...] = own
         base = own[0:1, :] * (1.0 / count)
         slope = own[1:2, :] * (1.0 / count)
         grad = ((shift[...] - base - normed[...] * slope) * scale).astype(jnp.bfloat16)
@@ -155,21 +168,26 @@
             window = (s0, s1, s2)[b][a * step_one : a * step_one + cells, :]
             out_ref[n * channels : (n + 1) * channels, :] = dot(window, grad, (0, 0)).astype(jnp.bfloat16)
 
-    (part_one,) = call(first_grad, [part_shape], work, own, grad_shift, normed, gain, rstd, *feats)
+    part_one, own = call(first_grad, [part_shape, shaped(2, channels)], work, every, grad_shift, normed, gain, rstd, *feats)
 
     lon, lat, batch = (lax.axis_size(a) for a in EVERY)
+    both = own
+    for shift in range(1, batch):
+        both = both + lax.ppermute(own, "batch", [(i, (i + shift) % batch) for i in range(batch)])
+    grad_bias, grad_gain = both
     pairs = [(i, i ^ 1) for i in range(lon)]
     core = lax.axis_index("lon") % 2 == 1
     groups = [
         [((x * 2 + c) * lat + z) * batch + y for x in range(lon // 2) for z in range(lat) for y in range(batch)]
         for c in range(2)
     ]
-    size = devices // 2
+    size = lon * lat * batch // 2
     total = 9 * channels
     chunk = -(-total // (size * 8)) * 8
     sent = jnp.where(core, part_one, part_two)
     kept = jnp.where(core, part_two, part_one)
-    half = (kept.astype(jnp.float32) + lax.ppermute(sent, "lon", pairs).astype(jnp.float32)).astype(jnp.bfloat16)
+    arrived = lax.ppermute(sent, "lon", pairs)
+    half = (kept.astype(jnp.float32) + arrived.astype(jnp.float32)).astype(jnp.bfloat16)
     half = jnp.pad(half, ((0, chunk * size - total), (0, 0)))
     chunks = lax.all_to_all(half.reshape(size, chunk, channels), EVERY, 0, 0, axis_index_groups=groups)
     piece = jnp.sum(chunks.astype(jnp.float32), axis=0).astype(jnp.bfloat16)
@@ -179,14 +197,30 @@
     (maps,) = call(second_conv, [shaped(cells, channels, jnp.bfloat16)], work, *hiddens, weight_two)
     mine = whole.reshape(size * chunk, channels)[:total]
     other = lax.ppermute(mine, "lon", pairs)
+    odd = core.astype(jnp.int32).reshape(1, 1)
+
+    def emit(odd, mine, other, one_ref, two_ref):
+        swap = jnp.broadcast_to(odd[...], (8, channels)) == 1
+
+        def body(i, _):
+            at = pl.ds(pl.multiple_of(i * channels, channels), channels)
+            a, b = mine[at, :].astype(jnp.float32), other[at, :].astype(jnp.float32)
+            pick = jnp.broadcast_to(swap[:1], (channels, channels))
+            one_ref[at, :] = jnp.where(pick, b, a)
+            two_ref[at, :] = jnp.where(pick, a, b)
+            return 0
+
+        lax.fori_loop(0, 9, body, 0)
+
+    grad_one, grad_two = call(emit, [shaped(total, channels)] * 2, 0, odd, mine, other)
     shape = weight_one.shape
-    grad_one = jnp.where(core, other, mine).astype(jnp.float32).reshape(shape)
-    grad_two = jnp.where(core, mine, other).astype(jnp.float32).reshape(shape)
+    grad_one, grad_two = grad_one.reshape(shape), grad_two.reshape(shape)
     return (maps.reshape(features.shape), grad_one, grad_two, grad_gain, grad_bias)
 
 
 def solution(mesh):
     placed = (P("batch", "lon", "lat", None), P(), P(), P(), P(), P("batch", "lon", "lat", None))
+
     return jax.shard_map(
         local,
         mesh=mesh,

time: 77.6 us -> 77.8 us (level)
  starting transfers between devices: 29.5 us -> 34.5 us
  waiting for transfers between devices: 32.8 us -> 28.1 us
  Pallas kernels: 3.68 us -> 6.25 us
  other arithmetic: 5.25 us -> 3.65 us
  local copies, waits for them, and re-layouts: 4.85 us -> 3.72 us
    all_to_all x1, waiting for transfers between devices: 7.89 us -> 2.96 us  [local(): lax.all_to_all(jnp.broadcast_to(piece[None], (size, chunk, channels)), EV...]
    all_to_all x1, waiting for transfers between devices: 5.99 us -> 2.09 us  [local(): lax.all_to_all(half.reshape(size, chunk, channels), EVERY, 0, 0, axis_ind...]
    pallas_call x6 -> x8, Pallas kernels: 3.68 us -> 6.25 us  [call(): pl.pallas_call(body, out_shape=outs, compiler_params=pltpu.CompilerParams...]
    ppermute x1 -> x2, waiting for transfers between devices: 1.47 us -> 3.57 us  [the longest x1 2.1 us: local(): lax.ppermute(own, 'batch', [(i, (i + shift) % batch) for i in range(batch)])]
    ppermute x6, waiting for transfers between devices: 1.07 us -> 2.86 us  [swapped(): one = lax.ppermute(jnp.where(odd, first, last), axis, near)]
    reshape x2 -> x0, other arithmetic: 1.72 us -> none  [the longest x1 0.86 us: local(): grad_one = jnp.where(core, other, mine).astype(jnp.float32).reshape(shape)]
    ppermute x6, starting transfers between devices: 7.7 us -> 9.28 us  [swapped(): one = lax.ppermute(jnp.where(odd, first, last), axis, near)]
    ppermute x1 -> x2, starting transfers between devices: 0.18 us -> 1.71 us  [the longest x1 1.53 us: local(): lax.ppermute(own, 'batch', [(i, (i + shift) % batch) for i in range(batch)])]
  transfers between devices with their start and end apart: 18 -> 19, of which waited for: 9 -> 9; matrix products, arithmetic and copies ran while one was open for 4% -> 3% of each run, Pallas kernels for 4% -> 5%
where the time goes in v3:
time: 77.8 us; the launch traced here: 77.2 us
  starting transfers between devices  34.5 us (44%)
  waiting for transfers between devices  28.1 us (36%)
  Pallas kernels  6.25 us (8%)
  local copies, waits for them, and re-layouts  3.72 us (5%)
  other arithmetic  3.65 us (5%)
  between operations  1 us (1%)
    ppermute x6, starting transfers between devices, swapped(): one = lax.ppermute(jnp.where(odd, first, last), axis, near)  9.28 us
    ppermute x6, starting transfers between devices, swapped(): two = lax.ppermute(jnp.where(odd, last, first), axis, far)  6.6 us
    pallas_call x8, Pallas kernels, call(): pl.pallas_call(body, out_shape=outs, compiler_params=pltpu.CompilerParams...  6.25 us
    all_to_all x1, waiting for transfers between devices, local(): every = lax.all_to_all(sums, TILE, 0, 0)  5.77 us
    all_to_all x1, waiting for transfers between devices, local(): stats = lax.all_to_all(stat, TILE, 0, 0)  5.64 us
    all_to_all x1, starting transfers between devices, local(): stats = lax.all_to_all(stat, TILE, 0, 0)  5.14 us
    ppermute x6, waiting for transfers between devices, swapped(): two = lax.ppermute(jnp.where(odd, last, first), axis, far)  5.11 us
    all_to_all x1, starting transfers between devices, local(): lax.all_to_all(jnp.broadcast_to(piece[None], (size, chunk, channels)), EV...  4.72 us
  transfers between devices with their start and end apart: 19, of which 9 were waited for; matrix products, arithmetic and copies ran while one was open for 3% of the time, Pallas kernels for 5%

profile of v3, /device:TPU:0, one launch (start us, length us, event | category | flops | bytes accessed | tf_op | source)
XLA Modules:
  0.0 77.2 jit_solution(12944911660502819084)
XLA Ops:
  0.6 0.0 copy-start
  0.7 0.8 %select_bitcast_fusion.3 = (bf16[6,24,128]{2,1,0:T(8,128)(2,1)S(1)}, bf16[6,24,128]{2,1,0:T(8,128)(2,1)S(1)}) fusion(pred[]{:T(512)S(6)} %eq.19, bf16[1,24,24,128]{3,2,1,0:T(8,128)(2,1)} %param.6), kind=kLoop, calls=%fused_computation.39 | loop fusion | flops 36864 | bytes 147457 | tf_op jit(solution)/shard_map/jit(_where)/select_n | solution.py:24
  1.5 0.6 collective-permute-start
  2.1 2.6 %collective-permute-start.1 = (bf16[6,24,128]{2,1,0:T(8,128)(2,1)S(1)}, bf16[6,24,128]{2,1,0:T(8,128)(2,1)S(1)}, u32[]{:S(2)}, u32[]{:S(2)}) collective-permute-start(bf16[6,24,128]{2,1,0:T(8,128)(2,1)S(1)} %get-tuple-element.63), channel_id=1, source_target_pairs={{0,24},{8,16},{16,8},{24,0},{1,25},{9,17},{17,9},{25,1},{2,26},{10... | collective-permute-start | bytes 110600 | tf_op jit(solution)/shard_map/ppermute | solution.py:25
  4.7 0.9 %select_bitcast_fusion.1 = (bf16[12,24,128]{2,1,0:T(8,128)(2,1)S(1)}, bf16[12,24,128]{2,1,0:T(8,128)(2,1)S(1)}) fusion(pred[]{:T(512)S(6)} %eq.19, bf16[1,24,24,128]{3,2,1,0:T(8,128)(2,1)} %param.11), kind=kLoop, calls=%fused_computation.31 | loop fusion | flops 73728 | bytes 294913 | tf_op jit(solution)/shard_map/jit(_where)/select_n | solution.py:24
  5.6 0.1 collective-permute-start.4
  5.7 0.0 collective-permute-start.5
  5.8 0.0 copy-done
  5.8 0.0 copy-start.1
  5.8 1.0 %copy-done.1 = bf16[3,3,128,128]{3,2,1,0:T(8,128)(2,1)S(1)} copy-done((bf16[3,3,128,128]{3,2,1,0:T(8,128)(2,1)S(1)}, bf16[3,3,128,128]{3,2,1,0:T(8,128)(2,1)}, u32[]{:S(2)}) %copy-start.1) | copy-done | bytes 294936
  6.7 0.7 copy-done.2
  7.4 0.7 copy-done.3
  8.1 0.0 copy-start.4
  8.1 0.0 collective-permute-done
  8.1 0.0 collective-permute-done.1
  8.2 2.2 %collective-permute-start.2 = (bf16[36,6,128]{2,1,0:T(8,128)(2,1)S(1)}, bf16[36,6,128]{2,1,0:T(8,128)(2,1)S(1)}, u32[]{:S(2)}, u32[]{:S(2)}) collective-permute-start(bf16[36,6,128]{2,1,0:T(8,128)(2,1)S(1)} %get-tuple-element.51), channel_id=1, source_target_pairs={{0,2},{2,0},{4,6},{6,4},{1,3},{3,1},{5,7},{7,5},{8,10},{10,8},{12,... | collective-permute-start | bytes 165896 | tf_op jit(solution)/shard_map/ppermute | solution.py:24
  10.4 0.7 collective-permute-start.3
  11.1 0.0 collective-permute-done.4
  11.1 0.0 collective-permute-done.5
  11.1 0.0 copy-done.4
  11.2 0.1 broadcast_select_fusion.3
  11.2 4.5 %collective-permute-start.6 = (bf16[48,12,128]{2,1,0:T(8,128)(2,1)S(1)}, bf16[48,12,128]{2,1,0:T(8,128)(2,1)S(1)}, u32[]{:S(2)}, u32[]{:S(2)}) collective-permute-start(bf16[48,12,128]{2,1,0:T(8,128)(2,1)S(1)} %get-tuple-element.47), channel_id=1, source_target_pairs={{0,2},{2,0},{4,6},{6,4},{1,3},{3,1},{5,7},{7,5},{8,10},{10,8},{12,... | collective-permute-start | bytes 442376 | tf_op jit(solution)/shard_map/ppermute | solution.py:24
  15.7 0.7 collective-permute-start.7
  16.4 0.0 collective-permute-done.2
  16.4 0.0 collective-permute-done.3
  16.4 0.2 pad_maximum_fusion.9
  16.6 1.2 %shard_map.102 = (f32[576,128]{1,0:T(8,128)S(1)}, f32[16,2,128]{2,1,0:T(2,128)}) custom-call(bf16[864,128]{1,0:T(8,128)(2,1)S(1)} %bitcast.45, bf16[864,128]{1,0:T(8,128)(2,1)S(1)} %bitcast.34, bf16[864,128]{1,0:T(8,128)(2,1)S(1)} %bitcast.43, bf16[3,3,128,128]{3,2,1,0:T(8,128)(2,1)S(1)} %get-tuple-element.20.weight), custom_call_target="tpu_custom_call" | custom-call | flops 169869312 | bytes 1269760 | tf_op jit(solution)/shard_map/pallas_call | solution.py:51
  17.8 5.1 %all-to-all-start = ((f32[16,2,128]{2,1,0:T(2,128)}), f32[16,2,128]{2,1,0:T(2,128)S(1)}, u32[]{:S(2)}, u32[]{:S(2)}) async-start(f32[16,2,128]{2,1,0:T(2,128)} %get-tuple-element.21), calls=%async_computation | async-start | bytes 32768 | tf_op jit(solution)/shard_map/all_to_all | solution.py:106
  23.0 0.0 collective-permute-done.6
  23.0 0.0 collective-permute-done.7
  23.0 0.2 pad_maximum_fusion.1
  23.3 0.5 shard_map.103.grad
  23.8 5.6 %all-to-all-done.stats = f32[16,2,128]{2,1,0:T(2,128)S(1)} async-done(((f32[16,2,128]{2,1,0:T(2,128)}), f32[16,2,128]{2,1,0:T(2,128)S(1)}, u32[]{:S(2)}, u32[]{:S(2)}) %all-to-all-start) | async-done | bytes 16416 | tf_op jit(solution)/shard_map/all_to_all | solution.py:106
  29.4 0.9 %shard_map.104 = (bf16[576,128]{1,0:T(8,128)(2,1)S(1)}, f32[576,128]{1,0:T(8,128)S(1)}, f32[576,128]{1,0:T(8,128)S(1)}, f32[1,128]{1,0:T(1,128)S(1)}, f32[16,2,128]{2,1,0:T(2,128)}) custom-call(f32[16,2,128]{2,1,0:T(2,128)S(1)} %all-to-all-done.stats, f32[576,128]{1,0:T(8,128)S(1)} %get-tuple-element.22.pre, f32[576,128]{1,0:T(8,128)S(1)} %shard_map.103.grad, ...), custom_call_target="tpu_custom_call" | custom-call | flops 1474560 | bytes 1361408 | tf_op jit(solution)/shard_map/pallas_call | solution.py:51
  30.3 3.5 %all-to-all-start.1 = ((f32[16,2,128]{2,1,0:T(2,128)}), f32[16,2,128]{2,1,0:T(2,128)S(1)}, u32[]{:S(2)}, u32[]{:S(2)}) async-start(f32[16,2,128]{2,1,0:T(2,128)} %get-tuple-element.27), calls=%async_computation.1 | async-start | bytes 32768 | tf_op jit(solution)/shard_map/all_to_all | solution.py:145
  33.8 0.6 shard_map.106
  34.4 5.8 %all-to-all-done.1.every = f32[16,2,128]{2,1,0:T(2,128)S(1)} async-done(((f32[16,2,128]{2,1,0:T(2,128)}), f32[16,2,128]{2,1,0:T(2,128)S(1)}, u32[]{:S(2)}, u32[]{:S(2)}) %all-to-all-start.1) | async-done | bytes 16416 | tf_op jit(solution)/shard_map/all_to_all | solution.py:145
  40.2 0.6 shard_map.107
  40.9 0.2 collective-permute-start.12
  41.0 1.5 %collective-permute-done.12 = bf16[1152,128]{1,0:T(8,128)(2,1)S(1)} collective-permute-done((bf16[1152,128]{1,0:T(8,128)(2,1)S(1)}, bf16[1152,128]{1,0:T(8,128)(2,1)S(1)}, u32[]{:S(2)}, u32[]{:S(2)}) %collective-permute-start.12) | collective-permute-done | bytes 294944 | tf_op jit(solution)/shard_map/ppermute | solution.py:189
  42.5 0.8 %add_convert_fusion = bf16[1152,128]{1,0:T(8,128)(2,1)} fusion(bf16[1152,128]{1,0:T(8,128)(2,1)S(1)} %collective-permute-done.12, bf16[1152,128]{1,0:T(8,128)(2,1)S(1)} %shard_map.106, bf16[1152,128]{1,0:T(8,128)(2,1)S(1)} %get-tuple-element.31, pred[]{:T(512)S(6)} %eq.19), kind=kLoop, calls=%fused_computation.1 | loop fusion | flops 737280 | bytes 1179649 | tf_op jit(solution)/shard_map/convert_element_type | solution.py:190
  43.3 3.5 %all-to-all-start.2 = ((bf16[16,72,128]{2,1,0:T(8,128)(2,1)}), bf16[16,72,128]{2,1,0:T(8,128)(2,1)S(1)}, u32[]{:S(2)}, u32[]{:S(2)}) async-start(bf16[16,72,128]{2,1,0:T(8,128)(2,1)} %bitcast.20), calls=%async_computation.2 | async-start | bytes 589824 | tf_op jit(solution)/shard_map/all_to_all | solution.py:192
  46.9 1.9 %collective-permute-start.8 = (bf16[24,12,128]{2,1,0:T(8,128)(2,1)S(1)}, bf16[24,12,128]{2,1,0:T(8,128)(2,1)S(1)}, u32[]{:S(2)}, u32[]{:S(2)}) collective-permute-start(bf16[24,12,128]{2,1,0:T(8,128)(2,1)S(1)} %get-tuple-element.54), channel_id=1, source_target_pairs={{0,2},{2,0},{4,6},{6,4},{1,3},{3,1},{5,7},{7,5},{8,10},{10,8},{12,... | collective-permute-start | bytes 221192 | tf_op jit(solution)/shard_map/ppermute | solution.py:24
  48.8 0.7 collective-permute-start.9
  49.5 1.5 %collective-permute-start.14 = (f32[2,128]{1,0:T(2,128)S(1)}, f32[2,128]{1,0:T(2,128)S(1)}, u32[]{:S(2)}, u32[]{:S(2)}) collective-permute-start(f32[2,128]{1,0:T(2,128)S(1)} %get-tuple-element.34), channel_id=1, source_target_pairs={{0,1},{1,0},{2,3},{3,2},{4,5},{5,4},{6,7},{7,6},{8,9},{9,8},{10,11... | collective-permute-start | bytes 3080 | tf_op jit(solution)/shard_map/ppermute | solution.py:176
  51.0 2.1 %collective-permute-done.14 = f32[2,128]{1,0:T(2,128)S(1)} collective-permute-done((f32[2,128]{1,0:T(2,128)S(1)}, f32[2,128]{1,0:T(2,128)S(1)}, u32[]{:S(2)}, u32[]{:S(2)}) %collective-permute-start.14) | collective-permute-done | bytes 1056 | tf_op jit(solution)/shard_map/ppermute | solution.py:176
  53.1 2.8 %collective-permute-done.8 = bf16[24,12,128]{2,1,0:T(8,128)(2,1)S(1)} collective-permute-done((bf16[24,12,128]{2,1,0:T(8,128)(2,1)S(1)}, bf16[24,12,128]{2,1,0:T(8,128)(2,1)S(1)}, u32[]{:S(2)}, u32[]{:S(2)}) %collective-permute-start.8) | collective-permute-done | bytes 73760 | tf_op jit(solution)/shard_map/ppermute | solution.py:24
  56.0 0.0 collective-permute-done.9
  56.0 0.1 pad_maximum_fusion.8
  56.1 2.1 %all-to-all-done.2 = bf16[16,72,128]{2,1,0:T(8,128)(2,1)S(1)} async-done(((bf16[16,72,128]{2,1,0:T(8,128)(2,1)}), bf16[16,72,128]{2,1,0:T(8,128)(2,1)S(1)}, u32[]{:S(2)}, u32[]{:S(2)}) %all-to-all-start.2) | async-done | bytes 294944 | tf_op jit(solution)/shard_map/all_to_all | solution.py:192
  58.2 0.8 broadcast_in_dim.14
  59.0 4.7 %all-to-all-start.3 = ((bf16[16,72,128]{2,1,0:T(8,128)(2,1)}), bf16[16,72,128]{2,1,0:T(8,128)(2,1)S(1)}, u32[]{:S(2)}, u32[]{:S(2)}) async-start(bf16[16,72,128]{2,1,0:T(8,128)(2,1)} %broadcast_in_dim.14), calls=%async_computation.3 | async-start | bytes 589824 | tf_op jit(solution)/shard_map/all_to_all | solution.py:194
  63.7 0.1 collective-permute-start.10
  63.8 2.0 %collective-permute-start.11 = (bf16[12,48,128]{2,1,0:T(8,128)(2,1)S(1)}, bf16[12,48,128]{2,1,0:T(8,128)(2,1)S(1)}, u32[]{:S(2)}, u32[]{:S(2)}) collective-permute-start(bf16[12,48,128]{2,1,0:T(8,128)(2,1)S(1)} %get-tuple-element.43), channel_id=1, source_target_pairs={{0,24},{8,16},{16,8},{24,0},{1,25},{9,17},{17,9},{25,1},{2,26},{10... | collective-permute-start | bytes 442376 | tf_op jit(solution)/shard_map/ppermute | solution.py:25
  65.8 0.5 slice_bitcast_fusion
  66.4 0.0 collective-permute-done.10
  66.4 5.1 %collective-permute-done.11 = bf16[12,48,128]{2,1,0:T(8,128)(2,1)S(1)} collective-permute-done((bf16[12,48,128]{2,1,0:T(8,128)(2,1)S(1)}, bf16[12,48,128]{2,1,0:T(8,128)(2,1)S(1)}, u32[]{:S(2)}, u32[]{:S(2)}) %collective-permute-start.11) | collective-permute-done | bytes 147488 | tf_op jit(solution)/shard_map/ppermute | solution.py:25
  71.5 3.0 %all-to-all-done.3 = bf16[16,72,128]{2,1,0:T(8,128)(2,1)S(1)} async-done(((bf16[16,72,128]{2,1,0:T(8,128)(2,1)}), bf16[16,72,128]{2,1,0:T(8,128)(2,1)S(1)}, u32[]{:S(2)}, u32[]{:S(2)}) %all-to-all-start.3) | async-done | bytes 294944 | tf_op jit(solution)/shard_map/all_to_all | solution.py:194
  74.4 0.0 collective-permute-start.13
  74.4 0.1 pad_maximum_fusion
  74.6 0.2 fusion
  74.7 1.2 %shard_map.105 = bf16[576,128]{1,0:T(8,128)(2,1)} custom-call(bf16[1152,128]{1,0:T(8,128)(2,1)S(1)} %bitcast.49, bf16[1152,128]{1,0:T(8,128)(2,1)S(1)} %bitcast.48, bf16[1152,128]{1,0:T(8,128)(2,1)S(1)} %bitcast.47, bf16[3,3,128,128]{3,2,1,0:T(8,128)(2,1)S(1)} %get-tuple-element.23.weight), custom_call_target="tpu_custom_call" | custom-call | flops 169869312 | bytes 1327104 | tf_op jit(solution)/shard_map/pallas_call | solution.py:51
  75.9 0.1 collective-permute-done.13.other
  76.0 1.2 %shard_map.108 = (f32[1152,128]{1,0:T(8,128)}, f32[1152,128]{1,0:T(8,128)}) custom-call(s32[1,1]{1,0:T(1,128)} %bitcast.19.odd, bf16[1152,128]{1,0:T(8,128)(2,1)S(1)} %bitcast.51, bf16[1152,128]{1,0:T(8,128)(2,1)S(1)} %collective-permute-done.13.other), custom_call_target="tpu_custom_call" | custom-call | bytes 1769476 | tf_op jit(solution)/shard_map/pallas_call | solution.py:51
  (19 shorter events, 0.4 us)
Async XLA Ops:
  0.6 5.1 %copy-start = (bf16[3,3,128,128]{3,2,1,0:T(8,128)(2,1)S(1)}, bf16[3,3,128,128]{3,2,1,0:T(8,128)(2,1)}, u32[]{:S(2)}) copy-start(bf16[3,3,128,128]{3,2,1,0:T(8,128)(2,1)} %w1.1) | copy-start | bytes 884740
  0.7 7.5 %copy-start.5 = (bf16[1,24,24,128]{3,2,1,0:T(8,128)(2,1)S(1)}, bf16[1,24,24,128]{3,2,1,0:T(8,128)(2,1)}, u32[]{:S(2)}) copy-start(bf16[1,24,24,128]{3,2,1,0:T(8,128)(2,1)} %param.6) | copy-start | bytes 442372
  1.5 6.6 %collective-permute-start = (bf16[6,24,128]{2,1,0:T(8,128)(2,1)S(1)}, bf16[6,24,128]{2,1,0:T(8,128)(2,1)S(1)}, u32[]{:S(2)}, u32[]{:S(2)}) collective-permute-start(bf16[6,24,128]{2,1,0:T(8,128)(2,1)S(1)} %get-tuple-element.62), channel_id=1, source_target_pairs={{0,8},{8,0},{16,24},{24,16},{1,9},{9,1},{17,25},{25,17},{2,10},{10... | collective-permute-start | bytes 110600 | tf_op jit(solution)/shard_map/ppermute | solution.py:24
  2.1 6.1 %collective-permute-start.1 = (bf16[6,24,128]{2,1,0:T(8,128)(2,1)S(1)}, bf16[6,24,128]{2,1,0:T(8,128)(2,1)S(1)}, u32[]{:S(2)}, u32[]{:S(2)}) collective-permute-start(bf16[6,24,128]{2,1,0:T(8,128)(2,1)S(1)} %get-tuple-element.63), channel_id=1, source_target_pairs={{0,24},{8,16},{16,8},{24,0},{1,25},{9,17},{17,9},{25,1},{2,26},{10... | collective-permute-start | bytes 110600 | tf_op jit(solution)/shard_map/ppermute | solution.py:25
  5.6 5.5 %collective-permute-start.4 = (bf16[12,24,128]{2,1,0:T(8,128)(2,1)S(1)}, bf16[12,24,128]{2,1,0:T(8,128)(2,1)S(1)}, u32[]{:S(2)}, u32[]{:S(2)}) collective-permute-start(bf16[12,24,128]{2,1,0:T(8,128)(2,1)S(1)} %get-tuple-element.58), channel_id=1, source_target_pairs={{0,8},{8,0},{16,24},{24,16},{1,9},{9,1},{17,25},{25,17},{2,10},{10... | collective-permute-start | bytes 221192 | tf_op jit(solution)/shard_map/ppermute | solution.py:24
  5.7 5.3 %collective-permute-start.5 = (bf16[12,24,128]{2,1,0:T(8,128)(2,1)S(1)}, bf16[12,24,128]{2,1,0:T(8,128)(2,1)S(1)}, u32[]{:S(2)}, u32[]{:S(2)}) collective-permute-start(bf16[12,24,128]{2,1,0:T(8,128)(2,1)S(1)} %get-tuple-element.59), channel_id=1, source_target_pairs={{0,24},{8,16},{16,8},{24,0},{1,25},{9,17},{17,9},{25,1},{2,26},{10... | collective-permute-start | bytes 221192 | tf_op jit(solution)/shard_map/ppermute | solution.py:25
  5.8 1.0 %copy-start.1 = (bf16[3,3,128,128]{3,2,1,0:T(8,128)(2,1)S(1)}, bf16[3,3,128,128]{3,2,1,0:T(8,128)(2,1)}, u32[]{:S(2)}) copy-start(bf16[3,3,128,128]{3,2,1,0:T(8,128)(2,1)} %w2.1) | copy-start | bytes 884740
  6.7 0.7 copy-start.2
  7.4 0.7 copy-start.3
  8.1 3.0 %copy-start.4 = (bf16[1,24,24,128]{3,2,1,0:T(8,128)(2,1)S(1)}, bf16[1,24,24,128]{3,2,1,0:T(8,128)(2,1)}, u32[]{:S(2)}) copy-start(bf16[1,24,24,128]{3,2,1,0:T(8,128)(2,1)} %param.11) | copy-start | bytes 442372
  8.2 8.1 %collective-permute-start.2 = (bf16[36,6,128]{2,1,0:T(8,128)(2,1)S(1)}, bf16[36,6,128]{2,1,0:T(8,128)(2,1)S(1)}, u32[]{:S(2)}, u32[]{:S(2)}) collective-permute-start(bf16[36,6,128]{2,1,0:T(8,128)(2,1)S(1)} %get-tuple-element.51), channel_id=1, source_target_pairs={{0,2},{2,0},{4,6},{6,4},{1,3},{3,1},{5,7},{7,5},{8,10},{10,8},{12,... | collective-permute-start | bytes 165896 | tf_op jit(solution)/shard_map/ppermute | solution.py:24
  10.4 6.0 %collective-permute-start.3 = (bf16[36,6,128]{2,1,0:T(8,128)(2,1)S(1)}, bf16[36,6,128]{2,1,0:T(8,128)(2,1)S(1)}, u32[]{:S(2)}, u32[]{:S(2)}) collective-permute-start(bf16[36,6,128]{2,1,0:T(8,128)(2,1)S(1)} %get-tuple-element.50), channel_id=1, source_target_pairs={{2,4},{4,2},{3,5},{5,3},{10,12},{12,10},{11,13},{13,11},{18,20},{2... | collective-permute-start | bytes 165896 | tf_op jit(solution)/shard_map/ppermute | solution.py:25
  11.2 11.7 %collective-permute-start.6 = (bf16[48,12,128]{2,1,0:T(8,128)(2,1)S(1)}, bf16[48,12,128]{2,1,0:T(8,128)(2,1)S(1)}, u32[]{:S(2)}, u32[]{:S(2)}) collective-permute-start(bf16[48,12,128]{2,1,0:T(8,128)(2,1)S(1)} %get-tuple-element.47), channel_id=1, source_target_pairs={{0,2},{2,0},{4,6},{6,4},{1,3},{3,1},{5,7},{7,5},{8,10},{10,8},{12,... | collective-permute-start | bytes 442376 | tf_op jit(solution)/shard_map/ppermute | solution.py:24
  15.7 7.3 %collective-permute-start.7 = (bf16[48,12,128]{2,1,0:T(8,128)(2,1)S(1)}, bf16[48,12,128]{2,1,0:T(8,128)(2,1)S(1)}, u32[]{:S(2)}, u32[]{:S(2)}) collective-permute-start(bf16[48,12,128]{2,1,0:T(8,128)(2,1)S(1)} %get-tuple-element.46), channel_id=1, source_target_pairs={{2,4},{4,2},{3,5},{5,3},{10,12},{12,10},{11,13},{13,11},{18,20},{2... | collective-permute-start | bytes 442376 | tf_op jit(solution)/shard_map/ppermute | solution.py:25
  17.8 11.6 %all-to-all-start = ((f32[16,2,128]{2,1,0:T(2,128)}), f32[16,2,128]{2,1,0:T(2,128)S(1)}, u32[]{:S(2)}, u32[]{:S(2)}) async-start(f32[16,2,128]{2,1,0:T(2,128)} %get-tuple-element.21), calls=%async_computation | async-start | bytes 32768 | tf_op jit(solution)/shard_map/all_to_all | solution.py:106
  30.3 9.9 %all-to-all-start.1 = ((f32[16,2,128]{2,1,0:T(2,128)}), f32[16,2,128]{2,1,0:T(2,128)S(1)}, u32[]{:S(2)}, u32[]{:S(2)}) async-start(f32[16,2,128]{2,1,0:T(2,128)} %get-tuple-element.27), calls=%async_computation.1 | async-start | bytes 32768 | tf_op jit(solution)/shard_map/all_to_all | solution.py:145
  40.9 1.6 %collective-permute-start.12 = (bf16[1152,128]{1,0:T(8,128)(2,1)S(1)}, bf16[1152,128]{1,0:T(8,128)(2,1)S(1)}, u32[]{:S(2)}, u32[]{:S(2)}) collective-permute-start(bf16[1152,128]{1,0:T(8,128)(2,1)S(1)} %broadcast_select_fusion), channel_id=1, source_target_pairs={{0,8},{8,0},{16,24},{24,16},{1,9},{9,1},{17,25},{25,17},{2,10},{10... | collective-permute-start | bytes 884744 | tf_op jit(solution)/shard_map/ppermute | solution.py:189
  43.3 14.8 %all-to-all-start.2 = ((bf16[16,72,128]{2,1,0:T(8,128)(2,1)}), bf16[16,72,128]{2,1,0:T(8,128)(2,1)S(1)}, u32[]{:S(2)}, u32[]{:S(2)}) async-start(bf16[16,72,128]{2,1,0:T(8,128)(2,1)} %bitcast.20), calls=%async_computation.2 | async-start | bytes 589824 | tf_op jit(solution)/shard_map/all_to_all | solution.py:192
  46.9 9.0 %collective-permute-start.8 = (bf16[24,12,128]{2,1,0:T(8,128)(2,1)S(1)}, bf16[24,12,128]{2,1,0:T(8,128)(2,1)S(1)}, u32[]{:S(2)}, u32[]{:S(2)}) collective-permute-start(bf16[24,12,128]{2,1,0:T(8,128)(2,1)S(1)} %get-tuple-element.54), channel_id=1, source_target_pairs={{0,2},{2,0},{4,6},{6,4},{1,3},{3,1},{5,7},{7,5},{8,10},{10,8},{12,... | collective-permute-start | bytes 221192 | tf_op jit(solution)/shard_map/ppermute | solution.py:24
  48.8 7.2 %collective-permute-start.9 = (bf16[24,12,128]{2,1,0:T(8,128)(2,1)S(1)}, bf16[24,12,128]{2,1,0:T(8,128)(2,1)S(1)}, u32[]{:S(2)}, u32[]{:S(2)}) collective-permute-start(bf16[24,12,128]{2,1,0:T(8,128)(2,1)S(1)} %get-tuple-element.55), channel_id=1, source_target_pairs={{2,4},{4,2},{3,5},{5,3},{10,12},{12,10},{11,13},{13,11},{18,20},{2... | collective-permute-start | bytes 221192 | tf_op jit(solution)/shard_map/ppermute | solution.py:25
  49.5 3.6 %collective-permute-start.14 = (f32[2,128]{1,0:T(2,128)S(1)}, f32[2,128]{1,0:T(2,128)S(1)}, u32[]{:S(2)}, u32[]{:S(2)}) collective-permute-start(f32[2,128]{1,0:T(2,128)S(1)} %get-tuple-element.34), channel_id=1, source_target_pairs={{0,1},{1,0},{2,3},{3,2},{4,5},{5,4},{6,7},{7,6},{8,9},{9,8},{10,11... | collective-permute-start | bytes 3080 | tf_op jit(solution)/shard_map/ppermute | solution.py:176
  59.0 15.5 %all-to-all-start.3 = ((bf16[16,72,128]{2,1,0:T(8,128)(2,1)}), bf16[16,72,128]{2,1,0:T(8,128)(2,1)S(1)}, u32[]{:S(2)}, u32[]{:S(2)}) async-start(bf16[16,72,128]{2,1,0:T(8,128)(2,1)} %broadcast_in_dim.14), calls=%async_computation.3 | async-start | bytes 589824 | tf_op jit(solution)/shard_map/all_to_all | solution.py:194
  63.7 2.6 %collective-permute-start.10 = (bf16[12,48,128]{2,1,0:T(8,128)(2,1)S(1)}, bf16[12,48,128]{2,1,0:T(8,128)(2,1)S(1)}, u32[]{:S(2)}, u32[]{:S(2)}) collective-permute-start(bf16[12,48,128]{2,1,0:T(8,128)(2,1)S(1)} %get-tuple-element.42), channel_id=1, source_target_pairs={{0,8},{8,0},{16,24},{24,16},{1,9},{9,1},{17,25},{25,17},{2,10},{10... | collective-permute-start | bytes 442376 | tf_op jit(solution)/shard_map/ppermute | solution.py:24
  63.8 7.6 %collective-permute-start.11 = (bf16[12,48,128]{2,1,0:T(8,128)(2,1)S(1)}, bf16[12,48,128]{2,1,0:T(8,128)(2,1)S(1)}, u32[]{:S(2)}, u32[]{:S(2)}) collective-permute-start(bf16[12,48,128]{2,1,0:T(8,128)(2,1)S(1)} %get-tuple-element.43), channel_id=1, source_target_pairs={{0,24},{8,16},{16,8},{24,0},{1,25},{9,17},{17,9},{25,1},{2,26},{10... | collective-permute-start | bytes 442376 | tf_op jit(solution)/shard_map/ppermute | solution.py:25
  74.4 1.6 %collective-permute-start.13 = (bf16[1152,128]{1,0:T(8,128)(2,1)S(1)}, bf16[1152,128]{1,0:T(8,128)(2,1)S(1)}, u32[]{:S(2)}, u32[]{:S(2)}) collective-permute-start(bf16[1152,128]{1,0:T(8,128)(2,1)S(1)} %bitcast.50), channel_id=1, source_target_pairs={{0,8},{8,0},{16,24},{24,16},{1,9},{9,1},{17,25},{25,17},{2,10},{10... | collective-permute-start | bytes 884744 | tf_op jit(solution)/shard_map/ppermute | solution.py:199

commit v4 on v3

--- a/solution.py
+++ b/solution.py
@@ -46,6 +46,17 @@
     return shifts(tile, width)
 
 
+def members_of(keep):
+    lon, lat, batch = (lax.axis_size(a) for a in EVERY)
+    middle = sorted(range(lat), key=lambda z: abs(2 * z + 1 - lat))
+    found = {}
+    for x in reversed(range(lon)):
+        for z in middle:
+            for y in range(batch):
+                found.setdefault(keep(x, y), []).append((x * lat + z) * batch + y)
+    return list(found.values())
+
+
 def call(body, outs, flops, *args):
     moved = sum(a.size * a.dtype.itemsize for a in args) + sum(o.size * o.dtype.itemsize for o in outs)
     return pl.pallas_call(
@@ -101,9 +112,10 @@
         stat_ref[...] = jnp.broadcast_to(jnp.concatenate([near, around])[None], stat_ref.shape)
 
     members = lax.axis_size(TILE)
+    tile = members_of(lambda x, y: y)
     copies = jax.ShapeDtypeStruct((members, 2, channels), jnp.float32)
     pre_one, stat = call(first_conv, [shaped(cells, channels), copies], work, *feats, weight_one)
-    stats = lax.all_to_all(stat, TILE, 0, 0)
+    stats = lax.all_to_all(stat, EVERY, 0, 0, axis_index_groups=tile)
 
     cotan = shifted_copies(out_cotangent[0], RATE_TWO, ("lon", "lat"))
 
@@ -142,7 +154,7 @@
         cells * channels * 20,
         stats, pre_one, grad_hidden, gain, bias,
     )
-    every = lax.all_to_all(sums, TILE, 0, 0)
+    every = lax.all_to_all(sums, EVERY, 0, 0, axis_index_groups=tile)
 
     hiddens = shifted_copies(hidden.reshape(rows, cols, channels), RATE_TWO, ("lat", "lon"))
 
@@ -177,10 +189,7 @@
     grad_bias, grad_gain = both
     pairs = [(i, i ^ 1) for i in range(lon)]
     core = lax.axis_index("lon") % 2 == 1
-    groups = [
-        [((x * 2 + c) * lat + z) * batch + y for x in range(lon // 2) for z in range(lat) for y in range(batch)]
-        for c in range(2)
-    ]
+    groups = members_of(lambda x, y: x % 2)
     size = lon * lat * batch // 2
     total = 9 * channels
     chunk = -(-total // (size * 8)) * 8

time: 77.8 us -> 72 us (0.925)
  waiting for transfers between devices: 28.1 us -> 21.9 us
    all_to_all x2, waiting for transfers between devices: 11.4 us -> 7.06 us  [the longest x1 3.63 us: local(): every = lax.all_to_all(sums, EVERY, 0, 0, axis_index_groups=tile)]
    all_to_all x1, waiting for transfers between devices: 2.96 us -> 1.19 us  [local(): lax.all_to_all(jnp.broadcast_to(piece[None], (size, chunk, channels)), EV...]
    all_to_all x1, starting transfers between devices: 3.54 us -> 5.17 us  [local(): lax.all_to_all(half.reshape(size, chunk, channels), EVERY, 0, 0, axis_ind...]
    ppermute x6, starting transfers between devices: 6.6 us -> 5.23 us  [swapped(): two = lax.ppermute(jnp.where(odd, last, first), axis, far)]
    ppermute x6, starting transfers between devices: 9.28 us -> 8.04 us  [swapped(): one = lax.ppermute(jnp.where(odd, first, last), axis, near)]
    all_to_all x2, starting transfers between devices: 8.64 us -> 9.52 us  [the longest x1 5.34 us: local(): stats = lax.all_to_all(stat, EVERY, 0, 0, axis_index_groups=tile)]
  transfers between devices with their start and end apart: 19 -> 19, of which waited for: 9 -> 10; matrix products, arithmetic and copies ran while one was open for 3% -> 4% of each run, Pallas kernels for 5% -> 5%
where the time goes in v4:
time: 72 us; the launch traced here: 71.4 us
  starting transfers between devices  35 us (49%)
  waiting for transfers between devices  21.9 us (30%)
  Pallas kernels  6.25 us (9%)
  local copies, waits for them, and re-layouts  3.72 us (5%)
  other arithmetic  3.65 us (5%)
  between operations  0.96 us (1%)
    ppermute x6, starting transfers between devices, swapped(): one = lax.ppermute(jnp.where(odd, first, last), axis, near)  8.04 us
    pallas_call x8, Pallas kernels, call(): pl.pallas_call(body, out_shape=outs, compiler_params=pltpu.CompilerParams...  6.25 us
    all_to_all x1, starting transfers between devices, local(): lax.all_to_all(jnp.broadcast_to(piece[None], (size, chunk, channels)), EV...  5.4 us
    all_to_all x1, starting transfers between devices, local(): stats = lax.all_to_all(stat, EVERY, 0, 0, axis_index_groups=tile)  5.34 us
    ppermute x6, waiting for transfers between devices, swapped(): two = lax.ppermute(jnp.where(odd, last, first), axis, far)  5.24 us
    ppermute x6, starting transfers between devices, swapped(): two = lax.ppermute(jnp.where(odd, last, first), axis, far)  5.23 us
    all_to_all x1, starting transfers between devices, local(): lax.all_to_all(half.reshape(size, chunk, channels), EVERY, 0, 0, axis_ind...  5.17 us
    all_to_all x1, starting transfers between devices, local(): every = lax.all_to_all(sums, EVERY, 0, 0, axis_index_groups=tile)  4.18 us
  transfers between devices with their start and end apart: 19, of which 10 were waited for; matrix products, arithmetic and copies ran while one was open for 4% of the time, Pallas kernels for 5%

profile of v4, /device:TPU:0, one launch (start us, length us, event | category | flops | bytes accessed | tf_op | source)
XLA Modules:
  0.0 71.4 jit_solution(135728296675755529)
XLA Ops:
  0.6 0.0 copy-start
  0.7 0.8 %select_bitcast_fusion.3 = (bf16[6,24,128]{2,1,0:T(8,128)(2,1)S(1)}, bf16[6,24,128]{2,1,0:T(8,128)(2,1)S(1)}) fusion(pred[]{:T(512)S(6)} %eq.19, bf16[1,24,24,128]{3,2,1,0:T(8,128)(2,1)} %param.6), kind=kLoop, calls=%fused_computation.39 | loop fusion | flops 36864 | bytes 147457 | tf_op jit(solution)/shard_map/jit(_where)/select_n | solution.py:24
  1.5 0.6 collective-permute-start
  2.1 2.6 %collective-permute-start.1 = (bf16[6,24,128]{2,1,0:T(8,128)(2,1)S(1)}, bf16[6,24,128]{2,1,0:T(8,128)(2,1)S(1)}, u32[]{:S(2)}, u32[]{:S(2)}) collective-permute-start(bf16[6,24,128]{2,1,0:T(8,128)(2,1)S(1)} %get-tuple-element.63), channel_id=1, source_target_pairs={{0,24},{8,16},{16,8},{24,0},{1,25},{9,17},{17,9},{25,1},{2,26},{10... | collective-permute-start | bytes 110600 | tf_op jit(solution)/shard_map/ppermute | solution.py:25
  4.7 0.9 %select_bitcast_fusion.1 = (bf16[12,24,128]{2,1,0:T(8,128)(2,1)S(1)}, bf16[12,24,128]{2,1,0:T(8,128)(2,1)S(1)}) fusion(pred[]{:T(512)S(6)} %eq.19, bf16[1,24,24,128]{3,2,1,0:T(8,128)(2,1)} %param.11), kind=kLoop, calls=%fused_computation.31 | loop fusion | flops 73728 | bytes 294913 | tf_op jit(solution)/shard_map/jit(_where)/select_n | solution.py:24
  5.6 0.1 collective-permute-start.4
  5.7 0.0 collective-permute-start.5
  5.8 0.0 copy-done
  5.8 0.0 copy-start.1
  5.8 1.0 %copy-done.1 = bf16[3,3,128,128]{3,2,1,0:T(8,128)(2,1)S(1)} copy-done((bf16[3,3,128,128]{3,2,1,0:T(8,128)(2,1)S(1)}, bf16[3,3,128,128]{3,2,1,0:T(8,128)(2,1)}, u32[]{:S(2)}) %copy-start.1) | copy-done | bytes 294936
  6.7 0.7 copy-done.2
  7.4 0.7 copy-done.3
  8.1 0.0 copy-start.4
  8.1 0.0 collective-permute-done
  8.1 0.0 collective-permute-done.1
  8.2 2.2 %collective-permute-start.2 = (bf16[36,6,128]{2,1,0:T(8,128)(2,1)S(1)}, bf16[36,6,128]{2,1,0:T(8,128)(2,1)S(1)}, u32[]{:S(2)}, u32[]{:S(2)}) collective-permute-start(bf16[36,6,128]{2,1,0:T(8,128)(2,1)S(1)} %get-tuple-element.51), channel_id=1, source_target_pairs={{0,2},{2,0},{4,6},{6,4},{1,3},{3,1},{5,7},{7,5},{8,10},{10,8},{12,... | collective-permute-start | bytes 165896 | tf_op jit(solution)/shard_map/ppermute | solution.py:24
  10.4 0.7 collective-permute-start.3
  11.1 0.0 collective-permute-done.4
  11.1 0.0 collective-permute-done.5
  11.1 0.0 copy-done.4
  11.2 0.1 broadcast_select_fusion.3
  11.2 4.5 %collective-permute-start.6 = (bf16[48,12,128]{2,1,0:T(8,128)(2,1)S(1)}, bf16[48,12,128]{2,1,0:T(8,128)(2,1)S(1)}, u32[]{:S(2)}, u32[]{:S(2)}) collective-permute-start(bf16[48,12,128]{2,1,0:T(8,128)(2,1)S(1)} %get-tuple-element.47), channel_id=1, source_target_pairs={{0,2},{2,0},{4,6},{6,4},{1,3},{3,1},{5,7},{7,5},{8,10},{10,8},{12,... | collective-permute-start | bytes 442376 | tf_op jit(solution)/shard_map/ppermute | solution.py:24
  15.7 0.7 collective-permute-start.7
  16.4 0.0 collective-permute-done.2
  16.4 0.0 collective-permute-done.3
  16.4 0.2 pad_maximum_fusion.9
  16.6 1.2 %shard_map.102 = (f32[576,128]{1,0:T(8,128)S(1)}, f32[16,2,128]{2,1,0:T(2,128)}) custom-call(bf16[864,128]{1,0:T(8,128)(2,1)S(1)} %bitcast.45, bf16[864,128]{1,0:T(8,128)(2,1)S(1)} %bitcast.34, bf16[864,128]{1,0:T(8,128)(2,1)S(1)} %bitcast.43, bf16[3,3,128,128]{3,2,1,0:T(8,128)(2,1)S(1)} %get-tuple-element.20.weight), custom_call_target="tpu_custom_call" | custom-call | flops 169869312 | bytes 1269760 | tf_op jit(solution)/shard_map/pallas_call | solution.py:62
  17.8 5.3 %all-to-all-start = ((f32[16,2,128]{2,1,0:T(2,128)}), f32[16,2,128]{2,1,0:T(2,128)S(1)}, u32[]{:S(2)}, u32[]{:S(2)}) async-start(f32[16,2,128]{2,1,0:T(2,128)} %get-tuple-element.21), calls=%async_computation | async-start | bytes 32768 | tf_op jit(solution)/shard_map/all_to_all | solution.py:118
  23.2 0.0 collective-permute-done.6
  23.2 0.0 collective-permute-done.7
  23.2 0.2 pad_maximum_fusion.1
  23.4 0.5 shard_map.103.grad
  24.0 3.4 %all-to-all-done.stats = f32[16,2,128]{2,1,0:T(2,128)S(1)} async-done(((f32[16,2,128]{2,1,0:T(2,128)}), f32[16,2,128]{2,1,0:T(2,128)S(1)}, u32[]{:S(2)}, u32[]{:S(2)}) %all-to-all-start) | async-done | bytes 16416 | tf_op jit(solution)/shard_map/all_to_all | solution.py:118
  27.4 0.9 %shard_map.104 = (bf16[576,128]{1,0:T(8,128)(2,1)S(1)}, f32[576,128]{1,0:T(8,128)S(1)}, f32[576,128]{1,0:T(8,128)S(1)}, f32[1,128]{1,0:T(1,128)S(1)}, f32[16,2,128]{2,1,0:T(2,128)}) custom-call(f32[16,2,128]{2,1,0:T(2,128)S(1)} %all-to-all-done.stats, f32[576,128]{1,0:T(8,128)S(1)} %get-tuple-element.22.pre, f32[576,128]{1,0:T(8,128)S(1)} %shard_map.103.grad, ...), custom_call_target="tpu_custom_call" | custom-call | flops 1474560 | bytes 1361408 | tf_op jit(solution)/shard_map/pallas_call | solution.py:62
  28.3 4.2 %all-to-all-start.1 = ((f32[16,2,128]{2,1,0:T(2,128)}), f32[16,2,128]{2,1,0:T(2,128)S(1)}, u32[]{:S(2)}, u32[]{:S(2)}) async-start(f32[16,2,128]{2,1,0:T(2,128)} %get-tuple-element.27), calls=%async_computation.1 | async-start | bytes 32768 | tf_op jit(solution)/shard_map/all_to_all | solution.py:157
  32.5 0.6 shard_map.106
  33.1 3.6 %all-to-all-done.1.every = f32[16,2,128]{2,1,0:T(2,128)S(1)} async-done(((f32[16,2,128]{2,1,0:T(2,128)}), f32[16,2,128]{2,1,0:T(2,128)S(1)}, u32[]{:S(2)}, u32[]{:S(2)}) %all-to-all-start.1) | async-done | bytes 16416 | tf_op jit(solution)/shard_map/all_to_all | solution.py:157
  36.7 0.6 shard_map.107
  37.4 0.1 collective-permute-start.12
  37.5 1.6 %collective-permute-done.12 = bf16[1152,128]{1,0:T(8,128)(2,1)S(1)} collective-permute-done((bf16[1152,128]{1,0:T(8,128)(2,1)S(1)}, bf16[1152,128]{1,0:T(8,128)(2,1)S(1)}, u32[]{:S(2)}, u32[]{:S(2)}) %collective-permute-start.12) | collective-permute-done | bytes 294944 | tf_op jit(solution)/shard_map/ppermute | solution.py:198
  39.0 0.8 %add_convert_fusion = bf16[1152,128]{1,0:T(8,128)(2,1)} fusion(bf16[1152,128]{1,0:T(8,128)(2,1)S(1)} %collective-permute-done.12, bf16[1152,128]{1,0:T(8,128)(2,1)S(1)} %shard_map.106, bf16[1152,128]{1,0:T(8,128)(2,1)S(1)} %get-tuple-element.31, pred[]{:T(512)S(6)} %eq.19), kind=kLoop, calls=%fused_computation.1 | loop fusion | flops 737280 | bytes 1179649 | tf_op jit(solution)/shard_map/convert_element_type | solution.py:199
  39.9 5.2 %all-to-all-start.2 = ((bf16[16,72,128]{2,1,0:T(8,128)(2,1)}), bf16[16,72,128]{2,1,0:T(8,128)(2,1)S(1)}, u32[]{:S(2)}, u32[]{:S(2)}) async-start(bf16[16,72,128]{2,1,0:T(8,128)(2,1)} %bitcast.20), calls=%async_computation.2 | async-start | bytes 589824 | tf_op jit(solution)/shard_map/all_to_all | solution.py:201
  45.1 0.6 collective-permute-start.8
  45.7 0.7 collective-permute-start.9
  46.4 1.5 %collective-permute-start.14 = (f32[2,128]{1,0:T(2,128)S(1)}, f32[2,128]{1,0:T(2,128)S(1)}, u32[]{:S(2)}, u32[]{:S(2)}) collective-permute-start(f32[2,128]{1,0:T(2,128)S(1)} %get-tuple-element.34), channel_id=1, source_target_pairs={{0,1},{1,0},{2,3},{3,2},{4,5},{5,4},{6,7},{7,6},{8,9},{9,8},{10,11... | collective-permute-start | bytes 3080 | tf_op jit(solution)/shard_map/ppermute | solution.py:188
  47.9 2.1 %collective-permute-done.14 = f32[2,128]{1,0:T(2,128)S(1)} collective-permute-done((f32[2,128]{1,0:T(2,128)S(1)}, f32[2,128]{1,0:T(2,128)S(1)}, u32[]{:S(2)}, u32[]{:S(2)}) %collective-permute-start.14) | collective-permute-done | bytes 1056 | tf_op jit(solution)/shard_map/ppermute | solution.py:188
  50.0 2.8 %collective-permute-done.8 = bf16[24,12,128]{2,1,0:T(8,128)(2,1)S(1)} collective-permute-done((bf16[24,12,128]{2,1,0:T(8,128)(2,1)S(1)}, bf16[24,12,128]{2,1,0:T(8,128)(2,1)S(1)}, u32[]{:S(2)}, u32[]{:S(2)}) %collective-permute-start.8) | collective-permute-done | bytes 73760 | tf_op jit(solution)/shard_map/ppermute | solution.py:24
  52.8 0.0 collective-permute-done.9
  52.8 0.1 pad_maximum_fusion.8
  52.9 1.6 %all-to-all-done.2 = bf16[16,72,128]{2,1,0:T(8,128)(2,1)S(1)} async-done(((bf16[16,72,128]{2,1,0:T(8,128)(2,1)}), bf16[16,72,128]{2,1,0:T(8,128)(2,1)S(1)}, u32[]{:S(2)}, u32[]{:S(2)}) %all-to-all-start.2) | async-done | bytes 294944 | tf_op jit(solution)/shard_map/all_to_all | solution.py:201
  54.6 0.8 %broadcast_in_dim.14 = bf16[16,72,128]{2,1,0:T(8,128)(2,1)} broadcast(bf16[72,128]{1,0:T(8,128)(2,1)S(1)} %reduce_sum.12), dimensions={1,2} | broadcast | bytes 313344 | tf_op jit(solution)/shard_map/broadcast_in_dim | solution.py:204
  55.3 5.4 %all-to-all-start.3 = ((bf16[16,72,128]{2,1,0:T(8,128)(2,1)}), bf16[16,72,128]{2,1,0:T(8,128)(2,1)S(1)}, u32[]{:S(2)}, u32[]{:S(2)}) async-start(bf16[16,72,128]{2,1,0:T(8,128)(2,1)} %broadcast_in_dim.14), calls=%async_computation.3 | async-start | bytes 589824 | tf_op jit(solution)/shard_map/all_to_all | solution.py:203
  60.7 0.1 collective-permute-start.10
  60.8 0.7 collective-permute-start.11
  61.5 0.5 slice_bitcast_fusion
  62.0 0.2 collective-permute-done.10
  62.2 5.2 %collective-permute-done.11 = bf16[12,48,128]{2,1,0:T(8,128)(2,1)S(1)} collective-permute-done((bf16[12,48,128]{2,1,0:T(8,128)(2,1)S(1)}, bf16[12,48,128]{2,1,0:T(8,128)(2,1)S(1)}, u32[]{:S(2)}, u32[]{:S(2)}) %collective-permute-start.11) | collective-permute-done | bytes 147488 | tf_op jit(solution)/shard_map/ppermute | solution.py:25
  67.4 1.2 %all-to-all-done.3 = bf16[16,72,128]{2,1,0:T(8,128)(2,1)S(1)} async-done(((bf16[16,72,128]{2,1,0:T(8,128)(2,1)}), bf16[16,72,128]{2,1,0:T(8,128)(2,1)S(1)}, u32[]{:S(2)}, u32[]{:S(2)}) %all-to-all-start.3) | async-done | bytes 294944 | tf_op jit(solution)/shard_map/all_to_all | solution.py:203
  68.6 0.0 collective-permute-start.13
  68.6 0.1 pad_maximum_fusion
  68.7 0.2 fusion
  68.9 1.2 %shard_map.105 = bf16[576,128]{1,0:T(8,128)(2,1)} custom-call(bf16[1152,128]{1,0:T(8,128)(2,1)S(1)} %bitcast.49, bf16[1152,128]{1,0:T(8,128)(2,1)S(1)} %bitcast.48, bf16[1152,128]{1,0:T(8,128)(2,1)S(1)} %bitcast.47, bf16[3,3,128,128]{3,2,1,0:T(8,128)(2,1)S(1)} %get-tuple-element.23.weight), custom_call_target="tpu_custom_call" | custom-call | flops 169869312 | bytes 1327104 | tf_op jit(solution)/shard_map/pallas_call | solution.py:62
  70.1 0.1 collective-permute-done.13.other
  70.2 1.2 %shard_map.108 = (f32[1152,128]{1,0:T(8,128)}, f32[1152,128]{1,0:T(8,128)}) custom-call(s32[1,1]{1,0:T(1,128)} %bitcast.19.odd, bf16[1152,128]{1,0:T(8,128)(2,1)S(1)} %bitcast.51, bf16[1152,128]{1,0:T(8,128)(2,1)S(1)} %collective-permute-done.13.other), custom_call_target="tpu_custom_call" | custom-call | bytes 1769476 | tf_op jit(solution)/shard_map/pallas_call | solution.py:62
  (19 shorter events, 0.4 us)
Async XLA Ops:
  0.6 5.1 %copy-start = (bf16[3,3,128,128]{3,2,1,0:T(8,128)(2,1)S(1)}, bf16[3,3,128,128]{3,2,1,0:T(8,128)(2,1)}, u32[]{:S(2)}) copy-start(bf16[3,3,128,128]{3,2,1,0:T(8,128)(2,1)} %w1.1) | copy-start | bytes 884740
  0.7 7.5 %copy-start.5 = (bf16[1,24,24,128]{3,2,1,0:T(8,128)(2,1)S(1)}, bf16[1,24,24,128]{3,2,1,0:T(8,128)(2,1)}, u32[]{:S(2)}) copy-start(bf16[1,24,24,128]{3,2,1,0:T(8,128)(2,1)} %param.6) | copy-start | bytes 442372
  1.5 6.6 %collective-permute-start = (bf16[6,24,128]{2,1,0:T(8,128)(2,1)S(1)}, bf16[6,24,128]{2,1,0:T(8,128)(2,1)S(1)}, u32[]{:S(2)}, u32[]{:S(2)}) collective-permute-start(bf16[6,24,128]{2,1,0:T(8,128)(2,1)S(1)} %get-tuple-element.62), channel_id=1, source_target_pairs={{0,8},{8,0},{16,24},{24,16},{1,9},{9,1},{17,25},{25,17},{2,10},{10... | collective-permute-start | bytes 110600 | tf_op jit(solution)/shard_map/ppermute | solution.py:24
  2.1 6.1 %collective-permute-start.1 = (bf16[6,24,128]{2,1,0:T(8,128)(2,1)S(1)}, bf16[6,24,128]{2,1,0:T(8,128)(2,1)S(1)}, u32[]{:S(2)}, u32[]{:S(2)}) collective-permute-start(bf16[6,24,128]{2,1,0:T(8,128)(2,1)S(1)} %get-tuple-element.63), channel_id=1, source_target_pairs={{0,24},{8,16},{16,8},{24,0},{1,25},{9,17},{17,9},{25,1},{2,26},{10... | collective-permute-start | bytes 110600 | tf_op jit(solution)/shard_map/ppermute | solution.py:25
  5.6 5.5 %collective-permute-start.4 = (bf16[12,24,128]{2,1,0:T(8,128)(2,1)S(1)}, bf16[12,24,128]{2,1,0:T(8,128)(2,1)S(1)}, u32[]{:S(2)}, u32[]{:S(2)}) collective-permute-start(bf16[12,24,128]{2,1,0:T(8,128)(2,1)S(1)} %get-tuple-element.58), channel_id=1, source_target_pairs={{0,8},{8,0},{16,24},{24,16},{1,9},{9,1},{17,25},{25,17},{2,10},{10... | collective-permute-start | bytes 221192 | tf_op jit(solution)/shard_map/ppermute | solution.py:24
  5.7 5.3 %collective-permute-start.5 = (bf16[12,24,128]{2,1,0:T(8,128)(2,1)S(1)}, bf16[12,24,128]{2,1,0:T(8,128)(2,1)S(1)}, u32[]{:S(2)}, u32[]{:S(2)}) collective-permute-start(bf16[12,24,128]{2,1,0:T(8,128)(2,1)S(1)} %get-tuple-element.59), channel_id=1, source_target_pairs={{0,24},{8,16},{16,8},{24,0},{1,25},{9,17},{17,9},{25,1},{2,26},{10... | collective-permute-start | bytes 221192 | tf_op jit(solution)/shard_map/ppermute | solution.py:25
  5.8 1.0 %copy-start.1 = (bf16[3,3,128,128]{3,2,1,0:T(8,128)(2,1)S(1)}, bf16[3,3,128,128]{3,2,1,0:T(8,128)(2,1)}, u32[]{:S(2)}) copy-start(bf16[3,3,128,128]{3,2,1,0:T(8,128)(2,1)} %w2.1) | copy-start | bytes 884740
  6.7 0.7 copy-start.2
  7.4 0.7 copy-start.3
  8.1 3.0 %copy-start.4 = (bf16[1,24,24,128]{3,2,1,0:T(8,128)(2,1)S(1)}, bf16[1,24,24,128]{3,2,1,0:T(8,128)(2,1)}, u32[]{:S(2)}) copy-start(bf16[1,24,24,128]{3,2,1,0:T(8,128)(2,1)} %param.11) | copy-start | bytes 442372
  8.2 8.1 %collective-permute-start.2 = (bf16[36,6,128]{2,1,0:T(8,128)(2,1)S(1)}, bf16[36,6,128]{2,1,0:T(8,128)(2,1)S(1)}, u32[]{:S(2)}, u32[]{:S(2)}) collective-permute-start(bf16[36,6,128]{2,1,0:T(8,128)(2,1)S(1)} %get-tuple-element.51), channel_id=1, source_target_pairs={{0,2},{2,0},{4,6},{6,4},{1,3},{3,1},{5,7},{7,5},{8,10},{10,8},{12,... | collective-permute-start | bytes 165896 | tf_op jit(solution)/shard_map/ppermute | solution.py:24
  10.4 6.0 %collective-permute-start.3 = (bf16[36,6,128]{2,1,0:T(8,128)(2,1)S(1)}, bf16[36,6,128]{2,1,0:T(8,128)(2,1)S(1)}, u32[]{:S(2)}, u32[]{:S(2)}) collective-permute-start(bf16[36,6,128]{2,1,0:T(8,128)(2,1)S(1)} %get-tuple-element.50), channel_id=1, source_target_pairs={{2,4},{4,2},{3,5},{5,3},{10,12},{12,10},{11,13},{13,11},{18,20},{2... | collective-permute-start | bytes 165896 | tf_op jit(solution)/shard_map/ppermute | solution.py:25
  11.2 11.9 %collective-permute-start.6 = (bf16[48,12,128]{2,1,0:T(8,128)(2,1)S(1)}, bf16[48,12,128]{2,1,0:T(8,128)(2,1)S(1)}, u32[]{:S(2)}, u32[]{:S(2)}) collective-permute-start(bf16[48,12,128]{2,1,0:T(8,128)(2,1)S(1)} %get-tuple-element.47), channel_id=1, source_target_pairs={{0,2},{2,0},{4,6},{6,4},{1,3},{3,1},{5,7},{7,5},{8,10},{10,8},{12,... | collective-permute-start | bytes 442376 | tf_op jit(solution)/shard_map/ppermute | solution.py:24
  15.7 7.5 %collective-permute-start.7 = (bf16[48,12,128]{2,1,0:T(8,128)(2,1)S(1)}, bf16[48,12,128]{2,1,0:T(8,128)(2,1)S(1)}, u32[]{:S(2)}, u32[]{:S(2)}) collective-permute-start(bf16[48,12,128]{2,1,0:T(8,128)(2,1)S(1)} %get-tuple-element.46), channel_id=1, source_target_pairs={{2,4},{4,2},{3,5},{5,3},{10,12},{12,10},{11,13},{13,11},{18,20},{2... | collective-permute-start | bytes 442376 | tf_op jit(solution)/shard_map/ppermute | solution.py:25
  17.8 9.6 %all-to-all-start = ((f32[16,2,128]{2,1,0:T(2,128)}), f32[16,2,128]{2,1,0:T(2,128)S(1)}, u32[]{:S(2)}, u32[]{:S(2)}) async-start(f32[16,2,128]{2,1,0:T(2,128)} %get-tuple-element.21), calls=%async_computation | async-start | bytes 32768 | tf_op jit(solution)/shard_map/all_to_all | solution.py:118
  28.3 8.4 %all-to-all-start.1 = ((f32[16,2,128]{2,1,0:T(2,128)}), f32[16,2,128]{2,1,0:T(2,128)S(1)}, u32[]{:S(2)}, u32[]{:S(2)}) async-start(f32[16,2,128]{2,1,0:T(2,128)} %get-tuple-element.27), calls=%async_computation.1 | async-start | bytes 32768 | tf_op jit(solution)/shard_map/all_to_all | solution.py:157
  37.4 1.6 %collective-permute-start.12 = (bf16[1152,128]{1,0:T(8,128)(2,1)S(1)}, bf16[1152,128]{1,0:T(8,128)(2,1)S(1)}, u32[]{:S(2)}, u32[]{:S(2)}) collective-permute-start(bf16[1152,128]{1,0:T(8,128)(2,1)S(1)} %broadcast_select_fusion), channel_id=1, source_target_pairs={{0,8},{8,0},{16,24},{24,16},{1,9},{9,1},{17,25},{25,17},{2,10},{10... | collective-permute-start | bytes 884744 | tf_op jit(solution)/shard_map/ppermute | solution.py:198
  39.9 14.7 %all-to-all-start.2 = ((bf16[16,72,128]{2,1,0:T(8,128)(2,1)}), bf16[16,72,128]{2,1,0:T(8,128)(2,1)S(1)}, u32[]{:S(2)}, u32[]{:S(2)}) async-start(bf16[16,72,128]{2,1,0:T(8,128)(2,1)} %bitcast.20), calls=%async_computation.2 | async-start | bytes 589824 | tf_op jit(solution)/shard_map/all_to_all | solution.py:201
  45.1 7.7 %collective-permute-start.8 = (bf16[24,12,128]{2,1,0:T(8,128)(2,1)S(1)}, bf16[24,12,128]{2,1,0:T(8,128)(2,1)S(1)}, u32[]{:S(2)}, u32[]{:S(2)}) collective-permute-start(bf16[24,12,128]{2,1,0:T(8,128)(2,1)S(1)} %get-tuple-element.54), channel_id=1, source_target_pairs={{0,2},{2,0},{4,6},{6,4},{1,3},{3,1},{5,7},{7,5},{8,10},{10,8},{12,... | collective-permute-start | bytes 221192 | tf_op jit(solution)/shard_map/ppermute | solution.py:24
  45.7 7.1 %collective-permute-start.9 = (bf16[24,12,128]{2,1,0:T(8,128)(2,1)S(1)}, bf16[24,12,128]{2,1,0:T(8,128)(2,1)S(1)}, u32[]{:S(2)}, u32[]{:S(2)}) collective-permute-start(bf16[24,12,128]{2,1,0:T(8,128)(2,1)S(1)} %get-tuple-element.55), channel_id=1, source_target_pairs={{2,4},{4,2},{3,5},{5,3},{10,12},{12,10},{11,13},{13,11},{18,20},{2... | collective-permute-start | bytes 221192 | tf_op jit(solution)/shard_map/ppermute | solution.py:25
  46.4 3.6 %collective-permute-start.14 = (f32[2,128]{1,0:T(2,128)S(1)}, f32[2,128]{1,0:T(2,128)S(1)}, u32[]{:S(2)}, u32[]{:S(2)}) collective-permute-start(f32[2,128]{1,0:T(2,128)S(1)} %get-tuple-element.34), channel_id=1, source_target_pairs={{0,1},{1,0},{2,3},{3,2},{4,5},{5,4},{6,7},{7,6},{8,9},{9,8},{10,11... | collective-permute-start | bytes 3080 | tf_op jit(solution)/shard_map/ppermute | solution.py:188
  55.3 13.3 %all-to-all-start.3 = ((bf16[16,72,128]{2,1,0:T(8,128)(2,1)}), bf16[16,72,128]{2,1,0:T(8,128)(2,1)S(1)}, u32[]{:S(2)}, u32[]{:S(2)}) async-start(bf16[16,72,128]{2,1,0:T(8,128)(2,1)} %broadcast_in_dim.14), calls=%async_computation.3 | async-start | bytes 589824 | tf_op jit(solution)/shard_map/all_to_all | solution.py:203
  60.7 1.4 %collective-permute-start.10 = (bf16[12,48,128]{2,1,0:T(8,128)(2,1)S(1)}, bf16[12,48,128]{2,1,0:T(8,128)(2,1)S(1)}, u32[]{:S(2)}, u32[]{:S(2)}) collective-permute-start(bf16[12,48,128]{2,1,0:T(8,128)(2,1)S(1)} %get-tuple-element.42), channel_id=1, source_target_pairs={{0,8},{8,0},{16,24},{24,16},{1,9},{9,1},{17,25},{25,17},{2,10},{10... | collective-permute-start | bytes 442376 | tf_op jit(solution)/shard_map/ppermute | solution.py:24
  60.8 6.6 %collective-permute-start.11 = (bf16[12,48,128]{2,1,0:T(8,128)(2,1)S(1)}, bf16[12,48,128]{2,1,0:T(8,128)(2,1)S(1)}, u32[]{:S(2)}, u32[]{:S(2)}) collective-permute-start(bf16[12,48,128]{2,1,0:T(8,128)(2,1)S(1)} %get-tuple-element.43), channel_id=1, source_target_pairs={{0,24},{8,16},{16,8},{24,0},{1,25},{9,17},{17,9},{25,1},{2,26},{10... | collective-permute-start | bytes 442376 | tf_op jit(solution)/shard_map/ppermute | solution.py:25
  68.6 1.6 %collective-permute-start.13 = (bf16[1152,128]{1,0:T(8,128)(2,1)S(1)}, bf16[1152,128]{1,0:T(8,128)(2,1)S(1)}, u32[]{:S(2)}, u32[]{:S(2)}) collective-permute-start(bf16[1152,128]{1,0:T(8,128)(2,1)S(1)} %bitcast.50), channel_id=1, source_target_pairs={{0,8},{8,0},{16,24},{24,16},{1,9},{9,1},{17,25},{25,17},{2,10},{10... | collective-permute-start | bytes 884744 | tf_op jit(solution)/shard_map/ppermute | solution.py:208

commit v5 on v4

--- a/solution.py
+++ b/solution.py
@@ -50,9 +50,9 @@
     lon, lat, batch = (lax.axis_size(a) for a in EVERY)
     middle = sorted(range(lat), key=lambda z: abs(2 * z + 1 - lat))
     found = {}
-    for x in reversed(range(lon)):
-        for z in middle:
-            for y in range(batch):
+    for y in range(batch):
+        for x in reversed(range(lon)):
+            for z in middle:
                 found.setdefault(keep(x, y), []).append((x * lat + z) * batch + y)
     return list(found.values())
 
@@ -91,17 +91,8 @@
     step_one, step_two = RATE_ONE * cols, RATE_TWO * cols
     work = 2 * 9 * cells * channels * channels
 
-    def stage(w1, w2, gain, bias, w1_ref, w2_ref, gain_ref, bias_ref):
-        w1_ref[...] = w1[...]
-        w2_ref[...] = w2[...]
-        gain_ref[...] = gain[...]
-        bias_ref[...] = bias[...]
-
     row = shaped(1, channels)
-    held = jax.ShapeDtypeStruct(weight_one.shape, weight_one.dtype)
-    weight_one, weight_two, gain, bias = call(
-        stage, [held, held, row, row], 0, weight_one, weight_two, norm_gain[None], norm_bias[None]
-    )
+    gain, bias = norm_gain[None], norm_bias[None]
     feats = shifted_copies(features[0], RATE_ONE, ("lon", "lat"))
 
     def first_conv(s0, s1, s2, weight, pre_ref, stat_ref):
@@ -208,20 +199,31 @@
     other = lax.ppermute(mine, "lon", pairs)
     odd = core.astype(jnp.int32).reshape(1, 1)
 
-    def emit(odd, mine, other, one_ref, two_ref):
-        swap = jnp.broadcast_to(odd[...], (8, channels)) == 1
-
-        def body(i, _):
-            at = pl.ds(pl.multiple_of(i * channels, channels), channels)
-            a, b = mine[at, :].astype(jnp.float32), other[at, :].astype(jnp.float32)
-            pick = jnp.broadcast_to(swap[:1], (channels, channels))
-            one_ref[at, :] = jnp.where(pick, b, a)
-            two_ref[at, :] = jnp.where(pick, a, b)
-            return 0
-
-        lax.fori_loop(0, 9, body, 0)
-
-    grad_one, grad_two = call(emit, [shaped(total, channels)] * 2, 0, odd, mine, other)
+    def emit(odd, mine, other, one_ref, two_ref, one_buf, two_buf, sems):
+        swap = jnp.broadcast_to(odd[...], (channels, channels)) == 1
+        sent = []
+        for part in range(3):
+            for n in range(3 * part, 3 * part + 3):
+                at = slice(n * channels, (n + 1) * channels)
+                a, b = mine[at, :].astype(jnp.float32), other[at, :].astype(jnp.float32)
+                one_buf[at, :] = jnp.where(swap, b, a)
+                two_buf[at, :] = jnp.where(swap, a, b)
+            span = pl.ds(3 * part * channels, 3 * channels)
+            for k, (buf, ref) in enumerate(((one_buf, one_ref), (two_buf, two_ref))):
+                sent.append(pltpu.make_async_copy(buf.at[span], ref.at[span], sems.at[k, part]))
+                sent[-1].start()
+        for copy in sent:
+            copy.wait()
+
+    grad_one, grad_two = pl.pallas_call(
+        emit,
+        out_shape=[shaped(total, channels)] * 2,
+        in_specs=[pl.BlockSpec(memory_space=pltpu.VMEM)] * 3,
+        out_specs=[pl.BlockSpec(memory_space=pl.ANY)] * 2,
+        scratch_shapes=[pltpu.VMEM((total, channels), jnp.float32)] * 2 + [pltpu.SemaphoreType.DMA((2, 3))],
+        compiler_params=pltpu.CompilerParams(vmem_limit_bytes=LIMIT),
+        name="emit",
+    )(odd, mine, other)
     shape = weight_one.shape
     grad_one, grad_two = grad_one.reshape(shape), grad_two.reshape(shape)
     return (maps.reshape(features.shape), grad_one, grad_two, grad_gain, grad_bias)

time: 72 us -> 70 us (0.972)
  starting transfers between devices: 35 us -> 33.3 us
  local copies, waits for them, and re-layouts: 3.72 us -> 2.2 us
  waiting for transfers between devices: 21.9 us -> 23.2 us
    unnamed x12, local copies, waits for them, and re-layouts: 2.28 us -> 0.77 us
    ppermute x6, waiting for transfers between devices: 5.24 us -> 6.57 us  [swapped(): two = lax.ppermute(jnp.where(odd, last, first), axis, far)]
    pallas_call x8 -> x6, Pallas kernels: 6.25 us -> 5 us  [call(): pl.pallas_call(body, out_shape=outs, compiler_params=pltpu.CompilerParams...]
    ppermute x6, starting transfers between devices: 8.04 us -> 6.83 us  [swapped(): one = lax.ppermute(jnp.where(odd, first, last), axis, near)]
    pallas_call x0 -> x1, Pallas kernels: none -> 1.16 us  [local(): pl.pallas_call(emit, out_shape=[shaped(total, channels)] * 2, in_specs=[p...]
    all_to_all x1, waiting for transfers between devices: 3.44 us -> 2.69 us  [local(): stats = lax.all_to_all(stat, EVERY, 0, 0, axis_index_groups=tile)]
    all_to_all x1, waiting for transfers between devices: 1.62 us -> 2.34 us  [local(): lax.all_to_all(half.reshape(size, chunk, channels), EVERY, 0, 0, axis_ind...]
  transfers between devices with their start and end apart: 19 -> 19, of which waited for: 10 -> 12; matrix products, arithmetic and copies ran while one was open for 4% -> 4% of each run, Pallas kernels for 5% -> 5%
where the time goes in v5:
time: 70 us; the launch traced here: 69.4 us
  starting transfers between devices  33.3 us (48%)
  waiting for transfers between devices  23.2 us (33%)
  Pallas kernels  6.16 us (9%)
  other arithmetic  3.64 us (5%)
  local copies, waits for them, and re-layouts  2.2 us (3%)
  between operations  0.93 us (1%)
    ppermute x6, starting transfers between devices, swapped(): one = lax.ppermute(jnp.where(odd, first, last), axis, near)  6.83 us
    ppermute x6, waiting for transfers between devices, swapped(): two = lax.ppermute(jnp.where(odd, last, first), axis, far)  6.57 us
    all_to_all x1, starting transfers between devices, local(): stats = lax.all_to_all(stat, EVERY, 0, 0, axis_index_groups=tile)  5.33 us
    ppermute x6, starting transfers between devices, swapped(): two = lax.ppermute(jnp.where(odd, last, first), axis, far)  5.24 us
    all_to_all x1, starting transfers between devices, local(): lax.all_to_all(half.reshape(size, chunk, channels), EVERY, 0, 0, axis_ind...  5.17 us
    pallas_call x6, Pallas kernels, call(): pl.pallas_call(body, out_shape=outs, compiler_params=pltpu.CompilerParams...  5 us
    all_to_all x1, starting transfers between devices, local(): lax.all_to_all(jnp.broadcast_to(piece[None], (size, chunk, channels)), EV...  4.89 us
    all_to_all x1, starting transfers between devices, local(): every = lax.all_to_all(sums, EVERY, 0, 0, axis_index_groups=tile)  4.18 us
  transfers between devices with their start and end apart: 19, of which 12 were waited for; matrix products, arithmetic and copies ran while one was open for 4% of the time, Pallas kernels for 5%

profile of v5, /device:TPU:0, one launch (start us, length us, event | category | flops | bytes accessed | tf_op | source)
XLA Modules:
  0.0 69.4 jit_solution(11701618478429051301)
XLA Ops:
  0.6 0.0 copy-start.5
  0.7 0.8 %select_bitcast_fusion.3 = (bf16[6,24,128]{2,1,0:T(8,128)(2,1)S(1)}, bf16[6,24,128]{2,1,0:T(8,128)(2,1)S(1)}) fusion(pred[]{:T(512)S(6)} %eq.19, bf16[1,24,24,128]{3,2,1,0:T(8,128)(2,1)} %param.6), kind=kLoop, calls=%fused_computation.39 | loop fusion | flops 36864 | bytes 147457 | tf_op jit(solution)/shard_map/jit(_where)/select_n | solution.py:24
  1.5 0.6 collective-permute-start
  2.0 2.6 %collective-permute-start.1 = (bf16[6,24,128]{2,1,0:T(8,128)(2,1)S(1)}, bf16[6,24,128]{2,1,0:T(8,128)(2,1)S(1)}, u32[]{:S(2)}, u32[]{:S(2)}) collective-permute-start(bf16[6,24,128]{2,1,0:T(8,128)(2,1)S(1)} %get-tuple-element.55), channel_id=1, source_target_pairs={{0,24},{8,16},{16,8},{24,0},{1,25},{9,17},{17,9},{25,1},{2,26},{10... | collective-permute-start | bytes 110600 | tf_op jit(solution)/shard_map/ppermute | solution.py:25
  4.6 0.9 %select_bitcast_fusion.1 = (bf16[12,24,128]{2,1,0:T(8,128)(2,1)S(1)}, bf16[12,24,128]{2,1,0:T(8,128)(2,1)S(1)}) fusion(pred[]{:T(512)S(6)} %eq.19, bf16[1,24,24,128]{3,2,1,0:T(8,128)(2,1)} %param.11), kind=kLoop, calls=%fused_computation.31 | loop fusion | flops 73728 | bytes 294913 | tf_op jit(solution)/shard_map/jit(_where)/select_n | solution.py:24
  5.6 0.1 collective-permute-start.4
  5.7 0.0 collective-permute-start.5
  5.7 0.0 copy-start.4
  5.8 0.0 collective-permute-done
  5.8 0.6 collective-permute-done.1
  6.4 0.0 copy-done.5
  6.5 1.7 %collective-permute-start.2 = (bf16[36,6,128]{2,1,0:T(8,128)(2,1)S(1)}, bf16[36,6,128]{2,1,0:T(8,128)(2,1)S(1)}, u32[]{:S(2)}, u32[]{:S(2)}) collective-permute-start(bf16[36,6,128]{2,1,0:T(8,128)(2,1)S(1)} %get-tuple-element.43), channel_id=1, source_target_pairs={{0,2},{2,0},{4,6},{6,4},{1,3},{3,1},{5,7},{7,5},{8,10},{10,8},{12,... | collective-permute-start | bytes 165896 | tf_op jit(solution)/shard_map/ppermute | solution.py:24
  8.2 0.7 collective-permute-start.3
  8.9 0.0 collective-permute-done.4
  8.9 0.8 %collective-permute-done.5 = bf16[12,24,128]{2,1,0:T(8,128)(2,1)S(1)} collective-permute-done((bf16[12,24,128]{2,1,0:T(8,128)(2,1)S(1)}, bf16[12,24,128]{2,1,0:T(8,128)(2,1)S(1)}, u32[]{:S(2)}, u32[]{:S(2)}) %collective-permute-start.5) | collective-permute-done | bytes 73760 | tf_op jit(solution)/shard_map/ppermute | solution.py:25
  9.7 0.1 broadcast_select_fusion.3
  9.8 0.0 copy-start.1
  9.8 3.7 %collective-permute-start.6 = (bf16[48,12,128]{2,1,0:T(8,128)(2,1)S(1)}, bf16[48,12,128]{2,1,0:T(8,128)(2,1)S(1)}, u32[]{:S(2)}, u32[]{:S(2)}) collective-permute-start(bf16[48,12,128]{2,1,0:T(8,128)(2,1)S(1)} %get-tuple-element.39), channel_id=1, source_target_pairs={{0,2},{2,0},{4,6},{6,4},{1,3},{3,1},{5,7},{7,5},{8,10},{10,8},{12,... | collective-permute-start | bytes 442376 | tf_op jit(solution)/shard_map/ppermute | solution.py:24
  13.5 0.7 collective-permute-start.7
  14.2 0.0 collective-permute-done.2
  14.2 0.0 collective-permute-done.3
  14.3 0.2 pad_maximum_fusion.9
  14.4 0.0 copy-done.1
  14.5 1.2 %shard_map.101 = (f32[576,128]{1,0:T(8,128)S(1)}, f32[16,2,128]{2,1,0:T(2,128)}) custom-call(bf16[864,128]{1,0:T(8,128)(2,1)S(1)} %bitcast.45, bf16[864,128]{1,0:T(8,128)(2,1)S(1)} %bitcast.34, bf16[864,128]{1,0:T(8,128)(2,1)S(1)} %bitcast.43, bf16[3,3,128,128]{3,2,1,0:T(8,128)(2,1)S(1)} %copy-done.1), custom_call_target="tpu_custom_call" | custom-call | flops 169869312 | bytes 1269760 | tf_op jit(solution)/shard_map/pallas_call | solution.py:62
  15.7 5.3 %all-to-all-start = ((f32[16,2,128]{2,1,0:T(2,128)}), f32[16,2,128]{2,1,0:T(2,128)S(1)}, u32[]{:S(2)}, u32[]{:S(2)}) async-start(f32[16,2,128]{2,1,0:T(2,128)} %get-tuple-element.16), calls=%async_computation | async-start | bytes 32768 | tf_op jit(solution)/shard_map/all_to_all | solution.py:109
  21.0 0.0 collective-permute-done.6
  21.0 0.0 collective-permute-done.7
  21.1 0.0 copy-start
  21.1 0.2 pad_maximum_fusion.1
  21.3 0.7 %copy-done = bf16[3,3,128,128]{3,2,1,0:T(8,128)(2,1)S(1)} copy-done((bf16[3,3,128,128]{3,2,1,0:T(8,128)(2,1)S(1)}, bf16[3,3,128,128]{3,2,1,0:T(8,128)(2,1)}, u32[]{:S(2)}) %copy-start) | copy-done | bytes 294936
  22.0 0.5 shard_map.102.grad
  22.5 2.7 %all-to-all-done.stats = f32[16,2,128]{2,1,0:T(2,128)S(1)} async-done(((f32[16,2,128]{2,1,0:T(2,128)}), f32[16,2,128]{2,1,0:T(2,128)S(1)}, u32[]{:S(2)}, u32[]{:S(2)}) %all-to-all-start) | async-done | bytes 16416 | tf_op jit(solution)/shard_map/all_to_all | solution.py:109
  25.2 0.0 copy-done.2
  25.2 0.9 %shard_map.103 = (bf16[576,128]{1,0:T(8,128)(2,1)S(1)}, f32[576,128]{1,0:T(8,128)S(1)}, f32[576,128]{1,0:T(8,128)S(1)}, f32[1,128]{1,0:T(1,128)S(1)}, f32[16,2,128]{2,1,0:T(2,128)}) custom-call(f32[16,2,128]{2,1,0:T(2,128)S(1)} %all-to-all-done.stats, f32[576,128]{1,0:T(8,128)S(1)} %get-tuple-element.17.pre, f32[576,128]{1,0:T(8,128)S(1)} %shard_map.102.grad, ...), custom_call_target="tpu_custom_call" | custom-call | flops 1474560 | bytes 1361408 | tf_op jit(solution)/shard_map/pallas_call | solution.py:62
  26.1 4.2 %all-to-all-start.1 = ((f32[16,2,128]{2,1,0:T(2,128)}), f32[16,2,128]{2,1,0:T(2,128)S(1)}, u32[]{:S(2)}, u32[]{:S(2)}) async-start(f32[16,2,128]{2,1,0:T(2,128)} %get-tuple-element.19), calls=%async_computation.1 | async-start | bytes 32768 | tf_op jit(solution)/shard_map/all_to_all | solution.py:148
  30.3 0.6 shard_map.105
  30.9 3.6 %all-to-all-done.1.every = f32[16,2,128]{2,1,0:T(2,128)S(1)} async-done(((f32[16,2,128]{2,1,0:T(2,128)}), f32[16,2,128]{2,1,0:T(2,128)S(1)}, u32[]{:S(2)}, u32[]{:S(2)}) %all-to-all-start.1) | async-done | bytes 16416 | tf_op jit(solution)/shard_map/all_to_all | solution.py:148
  34.6 0.6 shard_map.106
  35.2 0.1 collective-permute-start.12
  35.3 1.6 %collective-permute-done.12 = bf16[1152,128]{1,0:T(8,128)(2,1)S(1)} collective-permute-done((bf16[1152,128]{1,0:T(8,128)(2,1)S(1)}, bf16[1152,128]{1,0:T(8,128)(2,1)S(1)}, u32[]{:S(2)}, u32[]{:S(2)}) %collective-permute-start.12) | collective-permute-done | bytes 294944 | tf_op jit(solution)/shard_map/ppermute | solution.py:189
  36.9 0.8 %add_convert_fusion = bf16[1152,128]{1,0:T(8,128)(2,1)} fusion(bf16[1152,128]{1,0:T(8,128)(2,1)S(1)} %collective-permute-done.12, bf16[1152,128]{1,0:T(8,128)(2,1)S(1)} %shard_map.105, bf16[1152,128]{1,0:T(8,128)(2,1)S(1)} %get-tuple-element.23, pred[]{:T(512)S(6)} %eq.19), kind=kLoop, calls=%fused_computation.1 | loop fusion | flops 737280 | bytes 1179649 | tf_op jit(solution)/shard_map/convert_element_type | solution.py:190
  37.7 5.2 %all-to-all-start.2 = ((bf16[16,72,128]{2,1,0:T(8,128)(2,1)}), bf16[16,72,128]{2,1,0:T(8,128)(2,1)S(1)}, u32[]{:S(2)}, u32[]{:S(2)}) async-start(bf16[16,72,128]{2,1,0:T(8,128)(2,1)} %bitcast.20), calls=%async_computation.2 | async-start | bytes 589824 | tf_op jit(solution)/shard_map/all_to_all | solution.py:192
  42.9 0.6 collective-permute-start.8
  43.5 0.7 collective-permute-start.9
  44.2 1.5 %collective-permute-start.14 = (f32[2,128]{1,0:T(2,128)S(1)}, f32[2,128]{1,0:T(2,128)S(1)}, u32[]{:S(2)}, u32[]{:S(2)}) collective-permute-start(f32[2,128]{1,0:T(2,128)S(1)} %get-tuple-element.26), channel_id=1, source_target_pairs={{0,1},{1,0},{2,3},{3,2},{4,5},{5,4},{6,7},{7,6},{8,9},{9,8},{10,11... | collective-permute-start | bytes 3080 | tf_op jit(solution)/shard_map/ppermute | solution.py:179
  45.7 2.1 %collective-permute-done.14 = f32[2,128]{1,0:T(2,128)S(1)} collective-permute-done((f32[2,128]{1,0:T(2,128)S(1)}, f32[2,128]{1,0:T(2,128)S(1)}, u32[]{:S(2)}, u32[]{:S(2)}) %collective-permute-start.14) | collective-permute-done | bytes 1056 | tf_op jit(solution)/shard_map/ppermute | solution.py:179
  47.8 2.6 %collective-permute-done.8 = bf16[24,12,128]{2,1,0:T(8,128)(2,1)S(1)} collective-permute-done((bf16[24,12,128]{2,1,0:T(8,128)(2,1)S(1)}, bf16[24,12,128]{2,1,0:T(8,128)(2,1)S(1)}, u32[]{:S(2)}, u32[]{:S(2)}) %collective-permute-start.8) | collective-permute-done | bytes 73760 | tf_op jit(solution)/shard_map/ppermute | solution.py:24
  50.4 0.0 collective-permute-done.9
  50.4 0.1 pad_maximum_fusion.8
  50.5 2.3 %all-to-all-done.2 = bf16[16,72,128]{2,1,0:T(8,128)(2,1)S(1)} async-done(((bf16[16,72,128]{2,1,0:T(8,128)(2,1)}), bf16[16,72,128]{2,1,0:T(8,128)(2,1)S(1)}, u32[]{:S(2)}, u32[]{:S(2)}) %all-to-all-start.2) | async-done | bytes 294944 | tf_op jit(solution)/shard_map/all_to_all | solution.py:192
  52.9 0.8 %broadcast_in_dim.14 = bf16[16,72,128]{2,1,0:T(8,128)(2,1)} broadcast(bf16[72,128]{1,0:T(8,128)(2,1)S(1)} %reduce_sum.12), dimensions={1,2} | broadcast | bytes 313344 | tf_op jit(solution)/shard_map/broadcast_in_dim | solution.py:195
  53.7 4.9 %all-to-all-start.3 = ((bf16[16,72,128]{2,1,0:T(8,128)(2,1)}), bf16[16,72,128]{2,1,0:T(8,128)(2,1)S(1)}, u32[]{:S(2)}, u32[]{:S(2)}) async-start(bf16[16,72,128]{2,1,0:T(8,128)(2,1)} %broadcast_in_dim.14), calls=%async_computation.3 | async-start | bytes 589824 | tf_op jit(solution)/shard_map/all_to_all | solution.py:194
  58.6 0.1 collective-permute-start.10
  58.7 0.7 collective-permute-start.11
  59.3 0.5 slice_bitcast_fusion
  59.8 0.2 collective-permute-done.10
  60.0 5.2 %collective-permute-done.11 = bf16[12,48,128]{2,1,0:T(8,128)(2,1)S(1)} collective-permute-done((bf16[12,48,128]{2,1,0:T(8,128)(2,1)S(1)}, bf16[12,48,128]{2,1,0:T(8,128)(2,1)S(1)}, u32[]{:S(2)}, u32[]{:S(2)}) %collective-permute-start.11) | collective-permute-done | bytes 147488 | tf_op jit(solution)/shard_map/ppermute | solution.py:25
  65.2 1.5 %all-to-all-done.3 = bf16[16,72,128]{2,1,0:T(8,128)(2,1)S(1)} async-done(((bf16[16,72,128]{2,1,0:T(8,128)(2,1)}), bf16[16,72,128]{2,1,0:T(8,128)(2,1)S(1)}, u32[]{:S(2)}, u32[]{:S(2)}) %all-to-all-start.3) | async-done | bytes 294944 | tf_op jit(solution)/shard_map/all_to_all | solution.py:194
  66.7 0.0 collective-permute-start.13
  66.7 0.1 pad_maximum_fusion
  66.8 0.2 fusion
  67.0 1.2 %shard_map.104 = bf16[576,128]{1,0:T(8,128)(2,1)} custom-call(bf16[1152,128]{1,0:T(8,128)(2,1)S(1)} %bitcast.49, bf16[1152,128]{1,0:T(8,128)(2,1)S(1)} %bitcast.48, bf16[1152,128]{1,0:T(8,128)(2,1)S(1)} %bitcast.47, bf16[3,3,128,128]{3,2,1,0:T(8,128)(2,1)S(1)} %copy-done), custom_call_target="tpu_custom_call" | custom-call | flops 169869312 | bytes 1327104 | tf_op jit(solution)/shard_map/pallas_call | solution.py:62
  68.1 0.1 collective-permute-done.13.other
  68.3 1.2 %emit.1 = (f32[1152,128]{1,0:T(8,128)}, f32[1152,128]{1,0:T(8,128)}) custom-call(s32[1,1]{1,0:T(1,128)} %bitcast.19.odd, bf16[1152,128]{1,0:T(8,128)(2,1)S(1)} %bitcast.51, bf16[1152,128]{1,0:T(8,128)(2,1)S(1)} %collective-permute-done.13.other), custom_call_target="tpu_custom_call" | custom-call | tf_op jit(solution)/shard_map/emit/pallas_call | solution.py:218
  (18 shorter events, 0.4 us)
Async XLA Ops:
  0.6 5.8 %copy-start.5 = (bf16[1,24,24,128]{3,2,1,0:T(8,128)(2,1)S(1)}, bf16[1,24,24,128]{3,2,1,0:T(8,128)(2,1)}, u32[]{:S(2)}) copy-start(bf16[1,24,24,128]{3,2,1,0:T(8,128)(2,1)} %param.6) | copy-start | bytes 442372
  1.5 4.3 %collective-permute-start = (bf16[6,24,128]{2,1,0:T(8,128)(2,1)S(1)}, bf16[6,24,128]{2,1,0:T(8,128)(2,1)S(1)}, u32[]{:S(2)}, u32[]{:S(2)}) collective-permute-start(bf16[6,24,128]{2,1,0:T(8,128)(2,1)S(1)} %get-tuple-element.54), channel_id=1, source_target_pairs={{0,8},{8,0},{16,24},{24,16},{1,9},{9,1},{17,25},{25,17},{2,10},{10... | collective-permute-start | bytes 110600 | tf_op jit(solution)/shard_map/ppermute | solution.py:24
  2.0 4.4 %collective-permute-start.1 = (bf16[6,24,128]{2,1,0:T(8,128)(2,1)S(1)}, bf16[6,24,128]{2,1,0:T(8,128)(2,1)S(1)}, u32[]{:S(2)}, u32[]{:S(2)}) collective-permute-start(bf16[6,24,128]{2,1,0:T(8,128)(2,1)S(1)} %get-tuple-element.55), channel_id=1, source_target_pairs={{0,24},{8,16},{16,8},{24,0},{1,25},{9,17},{17,9},{25,1},{2,26},{10... | collective-permute-start | bytes 110600 | tf_op jit(solution)/shard_map/ppermute | solution.py:25
  5.6 3.3 %collective-permute-start.4 = (bf16[12,24,128]{2,1,0:T(8,128)(2,1)S(1)}, bf16[12,24,128]{2,1,0:T(8,128)(2,1)S(1)}, u32[]{:S(2)}, u32[]{:S(2)}) collective-permute-start(bf16[12,24,128]{2,1,0:T(8,128)(2,1)S(1)} %get-tuple-element.50), channel_id=1, source_target_pairs={{0,8},{8,0},{16,24},{24,16},{1,9},{9,1},{17,25},{25,17},{2,10},{10... | collective-permute-start | bytes 221192 | tf_op jit(solution)/shard_map/ppermute | solution.py:24
  5.7 4.0 %collective-permute-start.5 = (bf16[12,24,128]{2,1,0:T(8,128)(2,1)S(1)}, bf16[12,24,128]{2,1,0:T(8,128)(2,1)S(1)}, u32[]{:S(2)}, u32[]{:S(2)}) collective-permute-start(bf16[12,24,128]{2,1,0:T(8,128)(2,1)S(1)} %get-tuple-element.51), channel_id=1, source_target_pairs={{0,24},{8,16},{16,8},{24,0},{1,25},{9,17},{17,9},{25,1},{2,26},{10... | collective-permute-start | bytes 221192 | tf_op jit(solution)/shard_map/ppermute | solution.py:25
  5.7 3.9 %copy-start.4 = (bf16[1,24,24,128]{3,2,1,0:T(8,128)(2,1)S(1)}, bf16[1,24,24,128]{3,2,1,0:T(8,128)(2,1)}, u32[]{:S(2)}) copy-start(bf16[1,24,24,128]{3,2,1,0:T(8,128)(2,1)} %param.11) | copy-start | bytes 442372
  6.5 7.7 %collective-permute-start.2 = (bf16[36,6,128]{2,1,0:T(8,128)(2,1)S(1)}, bf16[36,6,128]{2,1,0:T(8,128)(2,1)S(1)}, u32[]{:S(2)}, u32[]{:S(2)}) collective-permute-start(bf16[36,6,128]{2,1,0:T(8,128)(2,1)S(1)} %get-tuple-element.43), channel_id=1, source_target_pairs={{0,2},{2,0},{4,6},{6,4},{1,3},{3,1},{5,7},{7,5},{8,10},{10,8},{12,... | collective-permute-start | bytes 165896 | tf_op jit(solution)/shard_map/ppermute | solution.py:24
  8.2 6.0 %collective-permute-start.3 = (bf16[36,6,128]{2,1,0:T(8,128)(2,1)S(1)}, bf16[36,6,128]{2,1,0:T(8,128)(2,1)S(1)}, u32[]{:S(2)}, u32[]{:S(2)}) collective-permute-start(bf16[36,6,128]{2,1,0:T(8,128)(2,1)S(1)} %get-tuple-element.42), channel_id=1, source_target_pairs={{2,4},{4,2},{3,5},{5,3},{10,12},{12,10},{11,13},{13,11},{18,20},{2... | collective-permute-start | bytes 165896 | tf_op jit(solution)/shard_map/ppermute | solution.py:25
  9.8 4.6 %copy-start.1 = (bf16[3,3,128,128]{3,2,1,0:T(8,128)(2,1)S(1)}, bf16[3,3,128,128]{3,2,1,0:T(8,128)(2,1)}, u32[]{:S(2)}) copy-start(bf16[3,3,128,128]{3,2,1,0:T(8,128)(2,1)} %weight.3) | copy-start | bytes 884740
  9.8 11.2 %collective-permute-start.6 = (bf16[48,12,128]{2,1,0:T(8,128)(2,1)S(1)}, bf16[48,12,128]{2,1,0:T(8,128)(2,1)S(1)}, u32[]{:S(2)}, u32[]{:S(2)}) collective-permute-start(bf16[48,12,128]{2,1,0:T(8,128)(2,1)S(1)} %get-tuple-element.39), channel_id=1, source_target_pairs={{0,2},{2,0},{4,6},{6,4},{1,3},{3,1},{5,7},{7,5},{8,10},{10,8},{12,... | collective-permute-start | bytes 442376 | tf_op jit(solution)/shard_map/ppermute | solution.py:24
  13.5 7.5 %collective-permute-start.7 = (bf16[48,12,128]{2,1,0:T(8,128)(2,1)S(1)}, bf16[48,12,128]{2,1,0:T(8,128)(2,1)S(1)}, u32[]{:S(2)}, u32[]{:S(2)}) collective-permute-start(bf16[48,12,128]{2,1,0:T(8,128)(2,1)S(1)} %get-tuple-element.38), channel_id=1, source_target_pairs={{2,4},{4,2},{3,5},{5,3},{10,12},{12,10},{11,13},{13,11},{18,20},{2... | collective-permute-start | bytes 442376 | tf_op jit(solution)/shard_map/ppermute | solution.py:25
  15.7 9.6 %all-to-all-start = ((f32[16,2,128]{2,1,0:T(2,128)}), f32[16,2,128]{2,1,0:T(2,128)S(1)}, u32[]{:S(2)}, u32[]{:S(2)}) async-start(f32[16,2,128]{2,1,0:T(2,128)} %get-tuple-element.16), calls=%async_computation | async-start | bytes 32768 | tf_op jit(solution)/shard_map/all_to_all | solution.py:109
  21.1 1.0 %copy-start = (bf16[3,3,128,128]{3,2,1,0:T(8,128)(2,1)S(1)}, bf16[3,3,128,128]{3,2,1,0:T(8,128)(2,1)}, u32[]{:S(2)}) copy-start(bf16[3,3,128,128]{3,2,1,0:T(8,128)(2,1)} %weight.5) | copy-start | bytes 884740
  22.0 3.2 %copy-start.2 = (f32[128]{0:T(128)S(1)}, f32[128]{0:T(128)}, u32[]{:S(2)}) copy-start(f32[128]{0:T(128)} %param.8) | copy-start | bytes 1540
  22.0 3.2 %copy-start.3 = (f32[128]{0:T(128)S(1)}, f32[128]{0:T(128)}, u32[]{:S(2)}) copy-start(f32[128]{0:T(128)} %param.9) | copy-start | bytes 1540
  26.1 8.4 %all-to-all-start.1 = ((f32[16,2,128]{2,1,0:T(2,128)}), f32[16,2,128]{2,1,0:T(2,128)S(1)}, u32[]{:S(2)}, u32[]{:S(2)}) async-start(f32[16,2,128]{2,1,0:T(2,128)} %get-tuple-element.19), calls=%async_computation.1 | async-start | bytes 32768 | tf_op jit(solution)/shard_map/all_to_all | solution.py:148
  35.2 1.6 %collective-permute-start.12 = (bf16[1152,128]{1,0:T(8,128)(2,1)S(1)}, bf16[1152,128]{1,0:T(8,128)(2,1)S(1)}, u32[]{:S(2)}, u32[]{:S(2)}) collective-permute-start(bf16[1152,128]{1,0:T(8,128)(2,1)S(1)} %broadcast_select_fusion), channel_id=1, source_target_pairs={{0,8},{8,0},{16,24},{24,16},{1,9},{9,1},{17,25},{25,17},{2,10},{10... | collective-permute-start | bytes 884744 | tf_op jit(solution)/shard_map/ppermute | solution.py:189
  37.7 15.2 %all-to-all-start.2 = ((bf16[16,72,128]{2,1,0:T(8,128)(2,1)}), bf16[16,72,128]{2,1,0:T(8,128)(2,1)S(1)}, u32[]{:S(2)}, u32[]{:S(2)}) async-start(bf16[16,72,128]{2,1,0:T(8,128)(2,1)} %bitcast.20), calls=%async_computation.2 | async-start | bytes 589824 | tf_op jit(solution)/shard_map/all_to_all | solution.py:192
  42.9 7.5 %collective-permute-start.8 = (bf16[24,12,128]{2,1,0:T(8,128)(2,1)S(1)}, bf16[24,12,128]{2,1,0:T(8,128)(2,1)S(1)}, u32[]{:S(2)}, u32[]{:S(2)}) collective-permute-start(bf16[24,12,128]{2,1,0:T(8,128)(2,1)S(1)} %get-tuple-element.46), channel_id=1, source_target_pairs={{0,2},{2,0},{4,6},{6,4},{1,3},{3,1},{5,7},{7,5},{8,10},{10,8},{12,... | collective-permute-start | bytes 221192 | tf_op jit(solution)/shard_map/ppermute | solution.py:24
  43.5 6.9 %collective-permute-start.9 = (bf16[24,12,128]{2,1,0:T(8,128)(2,1)S(1)}, bf16[24,12,128]{2,1,0:T(8,128)(2,1)S(1)}, u32[]{:S(2)}, u32[]{:S(2)}) collective-permute-start(bf16[24,12,128]{2,1,0:T(8,128)(2,1)S(1)} %get-tuple-element.47), channel_id=1, source_target_pairs={{2,4},{4,2},{3,5},{5,3},{10,12},{12,10},{11,13},{13,11},{18,20},{2... | collective-permute-start | bytes 221192 | tf_op jit(solution)/shard_map/ppermute | solution.py:25
  44.2 3.6 %collective-permute-start.14 = (f32[2,128]{1,0:T(2,128)S(1)}, f32[2,128]{1,0:T(2,128)S(1)}, u32[]{:S(2)}, u32[]{:S(2)}) collective-permute-start(f32[2,128]{1,0:T(2,128)S(1)} %get-tuple-element.26), channel_id=1, source_target_pairs={{0,1},{1,0},{2,3},{3,2},{4,5},{5,4},{6,7},{7,6},{8,9},{9,8},{10,11... | collective-permute-start | bytes 3080 | tf_op jit(solution)/shard_map/ppermute | solution.py:179
  53.7 13.0 %all-to-all-start.3 = ((bf16[16,72,128]{2,1,0:T(8,128)(2,1)}), bf16[16,72,128]{2,1,0:T(8,128)(2,1)S(1)}, u32[]{:S(2)}, u32[]{:S(2)}) async-start(bf16[16,72,128]{2,1,0:T(8,128)(2,1)} %broadcast_in_dim.14), calls=%async_computation.3 | async-start | bytes 589824 | tf_op jit(solution)/shard_map/all_to_all | solution.py:194
  58.6 1.4 %collective-permute-start.10 = (bf16[12,48,128]{2,1,0:T(8,128)(2,1)S(1)}, bf16[12,48,128]{2,1,0:T(8,128)(2,1)S(1)}, u32[]{:S(2)}, u32[]{:S(2)}) collective-permute-start(bf16[12,48,128]{2,1,0:T(8,128)(2,1)S(1)} %get-tuple-element.34), channel_id=1, source_target_pairs={{0,8},{8,0},{16,24},{24,16},{1,9},{9,1},{17,25},{25,17},{2,10},{10... | collective-permute-start | bytes 442376 | tf_op jit(solution)/shard_map/ppermute | solution.py:24
  58.7 6.5 %collective-permute-start.11 = (bf16[12,48,128]{2,1,0:T(8,128)(2,1)S(1)}, bf16[12,48,128]{2,1,0:T(8,128)(2,1)S(1)}, u32[]{:S(2)}, u32[]{:S(2)}) collective-permute-start(bf16[12,48,128]{2,1,0:T(8,128)(2,1)S(1)} %get-tuple-element.35), channel_id=1, source_target_pairs={{0,24},{8,16},{16,8},{24,0},{1,25},{9,17},{17,9},{25,1},{2,26},{10... | collective-permute-start | bytes 442376 | tf_op jit(solution)/shard_map/ppermute | solution.py:25
  66.7 1.6 %collective-permute-start.13 = (bf16[1152,128]{1,0:T(8,128)(2,1)S(1)}, bf16[1152,128]{1,0:T(8,128)(2,1)S(1)}, u32[]{:S(2)}, u32[]{:S(2)}) collective-permute-start(bf16[1152,128]{1,0:T(8,128)(2,1)S(1)} %bitcast.50), channel_id=1, source_target_pairs={{0,8},{8,0},{16,24},{24,16},{1,9},{9,1},{17,25},{25,17},{2,10},{10... | collective-permute-start | bytes 884744 | tf_op jit(solution)/shard_map/ppermute | solution.py:199
